TPU v7x, 512 devices: a whole 4x8x8 slice. The times are simulated.
512 devices in a mesh: wide: 64 (over x, y, core), row: 8 (over z).
Axes of the slice: x: 4, y: 8, z: 8, core: 2. Of those that a mesh axis runs over, the one named last changes fastest.
Arguments:
- points: float32 [128, 65536], P(None, ('wide', 'row')), may hold values from -6 to 6
- targets: float32 [32, 65536], P(None, ('wide', 'row')), may hold values from -6 to 6
- lengthscales: float32 [128], replicated, may hold values from 3.5 to 7
- outputscale: float32 [1], replicated, may hold values from 0.5 to 2
- noise: float32 [1], replicated, may hold values from 0.5 to 2
Outputs:
- solution: float32 [32, 65536], P(None, ('wide', 'row'))
- residual: float32 [32, 65536], P(None, ('wide', 'row'))
All inputs are finite; a program needn't handle non-finite values.
Results may differ from a plain program's by a relative error of at most 0.0003.
Values sent between devices are 32-bit elements; how exact they have to be, the bound alone decides.
No kernel may reach another device: no remote copies, remote signals or barrier semaphores. Data moves between devices by JAX's collectives and lax.ppermute only.
A program may use at most 64 MiB of HBM per device.

v0:
```python
import functools
import math

import jax
import jax.numpy as jnp
from jax import lax
from jax.experimental import pallas as pl
from jax.experimental.pallas import tpu as pltpu
from jax.sharding import Mesh
from jax.sharding import PartitionSpec as P

AXES = ("x", "y", "c", "z")
F32 = jnp.float32
BF16 = jnp.bfloat16
ROOT = math.sqrt(math.log2(math.e))
BLK = 128
RHS = 32
EXTRA = 8
TILE = 512
SUB = 512
WIDE = 1024
VMEM = pl.BlockSpec(memory_space=pltpu.VMEM)
SMEM = pl.BlockSpec(memory_space=pltpu.SMEM)
PARAMS = pltpu.CompilerParams(vmem_limit_bytes=12 << 20)


def shift(value, axis, steps):
    count = lax.axis_size(axis)
    return lax.ppermute(value, axis, [(s, (s + steps) % count) for s in range(count)])


def exchange(x, axes):
    return lax.all_to_all(x, axes, 0, 0, tiled=True)


def halves(x):
    high = x.astype(BF16)
    return high, (x - high.astype(F32)).astype(BF16)


def kept(x):
    return pltpu.with_memory_space_constraint(x, pltpu.VMEM)


def cost(flops=0, moved=0, powers=0):
    return pl.CostEstimate(flops=flops, bytes_accessed=moved, transcendentals=powers)


def spread_kernel(points, lengths, targets, scale, noise, out, own, aux):
    scaled = points[...] / lengths[...]
    vectors = targets[...]
    own[...] = scaled
    for peer in range(8):
        out[peer, pl.ds(0, BLK), :] = scaled
        out[peer, pl.ds(BLK, RHS), :] = vectors
    aux[...] = jnp.where(lax.broadcasted_iota(jnp.int32, (8, BLK), 0) == 0, scale[0], noise[0])


def spread(points, lengths, targets, scale, noise):
    return pl.pallas_call(
        spread_kernel,
        in_specs=[VMEM, VMEM, VMEM, SMEM, SMEM],
        out_specs=[VMEM] * 3,
        out_shape=[
            jax.ShapeDtypeStruct((8, BLK + RHS, BLK), F32),
            jax.ShapeDtypeStruct((BLK, BLK), F32),
            jax.ShapeDtypeStruct((8, BLK), F32),
        ],
        compiler_params=PARAMS,
        name="spread",
    )(points, lengths, targets, scale, noise)


ORDER = (0, -1, 1, 4, -3, -2, 2, 3)


def prepare_rows(place, row_refs, left, left_sq):
    for block in range(16):
        value = row_refs[block // 8][block % 8] * ROOT
        high, low = halves(value)
        z = lax.rem(place[0] + (ORDER[block % 8] + 8), 8)
        at = block // 8 * 2 + lax.div(z, 4)
        lanes = pl.ds(pl.multiple_of(lax.rem(z, 4) * BLK, BLK), BLK)
        left[at, pl.ds(0, 128), lanes] = high
        left[at, pl.ds(128, 128), lanes] = low
        left[at, pl.ds(256, 128), lanes] = high
        left[at, pl.ds(384, 128), lanes] = low
        left_sq[at, :, lanes] = -0.5 * jnp.sum(value * value, axis=0, keepdims=True)


def prepare_cols(col_refs, right, right_sq, vecs):
    each = 8 // len(col_refs)
    for block in range(8):
        ref, at = col_refs[block // each], block % each
        value = ref[at, pl.ds(0, BLK), :].T * ROOT
        high, low = halves(value)
        rows = pl.ds(block * BLK, BLK)
        right[rows, pl.ds(0, 128)] = high
        right[rows, pl.ds(128, 128)] = high
        right[rows, pl.ds(256, 128)] = low
        right[rows, pl.ds(384, 128)] = low
        right_sq[rows, :] = -0.5 * jnp.sum(value * value, axis=1, keepdims=True)
        high, low = halves(ref[at, pl.ds(BLK, RHS), :])
        vecs[pl.ds(0, RHS), rows] = high
        vecs[pl.ds(RHS, RHS), rows] = low


def make_values(left, left_sq, right, right_sq, vecs, high_ref, low_ref, out, before):
    def one(tile, carry):
        total = jnp.zeros((RHS, TILE), F32)
        for step in range(WIDE // SUB):
            rows = pl.ds(step * SUB, SUB)
            power = jnp.dot(right[rows, :], left[tile], preferred_element_type=F32)
            high, low = halves(jnp.exp2(power + right_sq[rows, :] + left_sq[tile]))
            high_ref[tile, rows, :] = high
            low_ref[tile, rows, :] = low
            both = jnp.dot(vecs[:, rows], high, preferred_element_type=F32)
            rest = jnp.dot(vecs[pl.ds(0, RHS), rows], low, preferred_element_type=F32)
            total = total + both[:RHS] + both[RHS:] + rest
        for local in range(TILE // BLK):
            at = tile * (TILE // BLK) + local
            piece = total[:, local * BLK : (local + 1) * BLK]
            out[at] = piece if before is None else piece + before[at]
        return carry

    lax.fori_loop(0, 4, one, 0)


def own_kernel(place, cols, same, other, out, high, low, left, left_sq, right, right_sq, vecs):
    prepare_rows(place, (same, other), left, left_sq)
    prepare_cols((cols,), right, right_sq, vecs)
    make_values(left, left_sq, right, right_sq, vecs, high, low, out, None)


def more_kernel(count, *refs):
    cols, (left, left_sq, before, out, high, low, right, right_sq, vecs) = refs[:count], refs[count:]
    prepare_cols(cols, right, right_sq, vecs)
    make_values(left, left_sq, right, right_sq, vecs, high, low, out, before)


PIECES = pltpu.VMEM((16, RHS, BLK), F32)
VALUES = pltpu.VMEM((4, WIDE, TILE), BF16)
LEFT = [pltpu.VMEM((4, 512, TILE), BF16), pltpu.VMEM((4, 1, TILE), F32)]
RIGHT = [pltpu.VMEM((WIDE, 512), BF16), pltpu.VMEM((WIDE, 1), F32), pltpu.VMEM((2 * RHS, WIDE), BF16)]
CHUNK_COST = cost(2 * 2048 * WIDE * 768, 4 * 2048 * WIDE, 2048 * WIDE)


def own_chunk(place, cols, same, other):
    return pl.pallas_call(
        own_kernel,
        in_specs=[SMEM] + [VMEM] * 3,
        out_specs=[VMEM] * 5,
        out_shape=[PIECES, VALUES, VALUES, *LEFT],
        scratch_shapes=RIGHT,
        compiler_params=PARAMS,
        cost_estimate=CHUNK_COST,
        name="own_chunk",
    )(place, cols, same, other)


def more_chunk(cols, left, left_sq, before):
    return pl.pallas_call(
        functools.partial(more_kernel, len(cols)),
        in_specs=[VMEM] * (len(cols) + 3),
        out_specs=[VMEM] * 3,
        out_shape=[PIECES, VALUES, VALUES],
        scratch_shapes=RIGHT,
        compiler_params=PARAMS,
        cost_estimate=CHUNK_COST,
        name="more_chunk",
    )(*cols, kept(left), kept(left_sq), kept(before))


def as_rows(columns):
    lane = lax.broadcasted_iota(jnp.int32, (RHS, BLK), 1)
    wide = jnp.zeros((RHS, BLK), F32)
    for at, column in enumerate(columns):
        wide = jnp.where(lane == at, column, wide)
    return jnp.concatenate([wide, jnp.zeros((BLK - RHS, BLK), F32)], axis=0).T[:EXTRA]


def as_columns(rows, count):
    tall = jnp.concatenate([rows, jnp.zeros((BLK - rows.shape[0], BLK), F32)], axis=0).T
    return [tall[:RHS, at : at + 1] for at in range(count)]


def total(x):
    return jnp.sum(x, axis=1, keepdims=True)


def between_kernel(aux, arrived, targets, first_ref, wide_ref):
    vectors = targets[...]
    first = aux[0:1, 0:1] * jnp.sum(arrived[...], axis=0) + aux[1:2, 0:1] * vectors
    extra = as_rows([total(vectors * vectors), total(vectors * first), total(first * first)])
    first_ref[...] = first
    for peer in range(8):
        wide_ref[peer, pl.ds(0, RHS), :] = first
        wide_ref[peer, pl.ds(RHS, EXTRA), :] = extra


def between(aux, arrived, targets):
    return pl.pallas_call(
        between_kernel,
        in_specs=[VMEM] * 3,
        out_specs=[VMEM] * 2,
        out_shape=[
            jax.ShapeDtypeStruct((RHS, BLK), F32),
            jax.ShapeDtypeStruct((8, RHS + EXTRA, BLK), F32),
        ],
        compiler_params=PARAMS,
        name="between",
    )(aux, arrived, targets)


def second_kernel(tiles, count, *refs):
    vectors, highs, lows = refs[:count], refs[count : 2 * count], refs[2 * count : 3 * count]
    before, out, vecs = refs[3 * count :] if len(refs) > 3 * count + 2 else (None, *refs[3 * count :])
    sums = jnp.zeros((EXTRA, BLK), F32)
    for chunk in range(count):
        for y in range(8):
            lanes = pl.ds(y * BLK, BLK)
            high, low = halves(vectors[chunk][y, pl.ds(0, RHS), :])
            vecs[chunk, pl.ds(0, RHS), lanes] = high
            vecs[chunk, pl.ds(RHS, RHS), lanes] = low
            sums = sums + vectors[chunk][y, pl.ds(RHS, EXTRA), :]
    for at, tile in enumerate(tiles):
        product = jnp.zeros((RHS, TILE), F32)
        for chunk in range(count):
            both = jnp.dot(vecs[chunk], highs[chunk][tile], preferred_element_type=F32)
            rest = jnp.dot(vecs[chunk, pl.ds(0, RHS), :], lows[chunk][tile], preferred_element_type=F32)
            product = product + both[:RHS] + both[RHS:] + rest
        for local in range(TILE // BLK):
            to = at * (TILE // BLK) + local
            from_ = tile * (TILE // BLK) + local
            piece = product[:, local * BLK : (local + 1) * BLK]
            if before is None:
                out[to, pl.ds(0, RHS), :] = piece
                out[to, pl.ds(RHS, EXTRA), :] = sums
            else:
                out[to, pl.ds(0, RHS), :] = piece + before[from_, pl.ds(0, RHS), :]
                out[to, pl.ds(RHS, EXTRA), :] = sums + before[from_, pl.ds(RHS, EXTRA), :]


def second(tiles, vectors, highs, lows, before=None):
    count = len(vectors)
    more = [] if before is None else [kept(before)]
    return pl.pallas_call(
        functools.partial(second_kernel, tiles, count),
        in_specs=[VMEM] * (3 * count + len(more)),
        out_specs=VMEM,
        out_shape=pltpu.VMEM((len(tiles) * 4, RHS + EXTRA, BLK), F32),
        scratch_shapes=[pltpu.VMEM((count, 2 * RHS, WIDE), BF16)],
        compiler_params=PARAMS,
        cost_estimate=cost(2 * 512 * len(tiles) * WIDE * count * 128, 4 * 512 * len(tiles) * WIDE * count, 0),
        name=f"second_{len(tiles)}x{count}",
    )(*vectors, *[kept(v) for v in highs], *[kept(v) for v in lows], *more)


def steps(extra):
    norm, curve, image_sq = as_columns(extra, 3)
    step = norm / curve
    norm_next = norm - 2.0 * step * curve + step * step * image_sq
    return step, norm_next, norm_next / norm


def settle_kernel(aux, arrived, targets, first, moves_ref, form_ref):
    whole = jnp.sum(arrived[...], axis=0)
    vectors, image = targets[...], first[...]
    second_image = aux[0:1, 0:1] * whole[:RHS] + aux[1:2, 0:1] * image
    step, norm_next, ratio = steps(whole[RHS:])
    residual = vectors - step * image
    direction = residual + ratio * vectors
    moved = image - step * second_image + ratio * image
    moves_ref[0] = step * vectors
    moves_ref[1] = residual
    moves_ref[2] = direction
    moves_ref[3] = moved
    moves_ref[4] = jnp.broadcast_to(norm_next, (RHS, BLK))
    form_ref[...] = as_rows([total(direction * moved)])


def settle(aux, arrived, targets, first):
    return pl.pallas_call(
        settle_kernel,
        in_specs=[VMEM] * 4,
        out_specs=[VMEM] * 2,
        out_shape=[jax.ShapeDtypeStruct((5, RHS, BLK), F32), jax.ShapeDtypeStruct((EXTRA, BLK), F32)],
        compiler_params=PARAMS,
        name="settle",
    )(aux, arrived, targets, first)


def finish_kernel(forms, moves, solution_ref, residual_ref):
    (curve,) = as_columns(jnp.sum(forms[...], axis=0), 1)
    step = moves[4][:, 0:1] / curve
    solution_ref[...] = moves[0] + step * moves[2]
    residual_ref[...] = moves[1] - step * moves[3]


def finish(forms, moves):
    shape = jax.ShapeDtypeStruct((RHS, BLK), F32)
    return pl.pallas_call(
        finish_kernel,
        in_specs=[VMEM] * 2,
        out_specs=[VMEM] * 2,
        out_shape=[shape, shape],
        compiler_params=PARAMS,
        name="finish",
    )(forms, moves)


def to_each(x, axes):
    peers = lax.axis_size(axes)
    return exchange(jnp.broadcast_to(x[None], (peers, *x.shape)), axes)


def on_device(points, targets, lengthscales, outputscale, noise):
    near, own, aux = spread(points, lengthscales[:, None], targets, outputscale, noise)
    near = exchange(near, "y")
    behind, ahead, across = shift(near, "x", 1), shift(near, "x", -1), shift(near, "x", 2)
    below, above, far = shift(own, "z", 1), shift(own, "z", -1), shift(own, "z", 4)
    pairs = [shift(jnp.stack([below, own]), "z", 2), shift(jnp.stack([own, above]), "z", -2)]
    same = jnp.concatenate([jnp.stack([own, below, above, far]), *pairs])
    other = shift(same, "c", 1)
    place = lax.axis_index("z").astype(jnp.int32)[None]
    pieces, high, low, left, left_sq = own_chunk(place, near, same, other)
    highs, lows = [high], [low]
    for cols in (behind, ahead, across):
        pieces, high, low = more_chunk([cols], left, left_sq, pieces)
        highs.append(high)
        lows.append(low)
    arrived = exchange(pieces[:8] + shift(pieces[8:], "c", 1), "z")
    first, wide = between(aux, arrived, targets)
    near = exchange(wide, "y")
    gathered = [shift(near, "x", 1), shift(near, "x", -1), shift(near, "x", 2)]
    before = second((0, 1, 2, 3), [near], highs[:1], lows[:1])
    theirs = shift(second((2, 3), gathered, highs[1:], lows[1:], before), "c", 1)
    mine = second((0, 1), gathered, highs[1:], lows[1:], before)
    arrived = exchange(mine + theirs, "z")
    moves, form = settle(aux, arrived, targets, first)
    form = jnp.sum(to_each(form[0:1], ("y", "c")), axis=0)
    return tuple(finish(to_each(form, ("x", "z")), moves))


def solution(mesh):
    finer = Mesh(mesh.devices.reshape(4, 8, 2, mesh.shape["row"]), AXES)
    spec = P(None, AXES)
    return jax.shard_map(
        on_device, mesh=finer, in_specs=(spec, spec, P(), P(), P()), out_specs=(spec, spec), check_vma=False
    )
```

profile of v0, /device:TPU:1, one launch (start us, length us, event | category | flops | bytes accessed | tf_op | source)
XLA Modules:
  0.0 186.8 jit_solution(14286331471343761057)
XLA Ops:
  1.9 0.8 copy.9.lengths
  2.7 0.0 copy-start
  2.7 0.7 copy-done
  3.4 0.0 copy-start.2
  3.4 0.8 copy-done.2
  4.2 1.0 spread.1
  5.2 11.4 %collective-permute-start.3 = (f32[128,128]{1,0:T(8,128)S(1)}, f32[128,128]{1,0:T(8,128)S(1)}, u32[]{:S(2)}, u32[]{:S(2)}) collective-permute-start(f32[128,128]{1,0:T(8,128)S(1)} %get-tuple-element.25), channel_id=1, source_target_pairs={{0,4},{1,5},{2,6},{3,7},{4,0},{5,1},{6,2},{7,3},{8,12},{9,13},{10,... | collective-permute-start | bytes 196616 | tf_op jit(solution)/shard_map/ppermute | solution.py:29
  16.7 2.0 %collective-permute-start.2 = (f32[128,128]{1,0:T(8,128)S(1)}, f32[128,128]{1,0:T(8,128)S(1)}, u32[]{:S(2)}, u32[]{:S(2)}) collective-permute-start(f32[128,128]{1,0:T(8,128)S(1)} %get-tuple-element.25), channel_id=1, source_target_pairs={{0,7},{1,0},{2,1},{3,2},{4,3},{5,4},{6,5},{7,6},{8,15},{9,8},{10,9... | collective-permute-start | bytes 196616 | tf_op jit(solution)/shard_map/ppermute | solution.py:29
  18.6 3.3 %collective-permute-start.1 = (f32[128,128]{1,0:T(8,128)S(1)}, f32[128,128]{1,0:T(8,128)S(1)}, u32[]{:S(2)}, u32[]{:S(2)}) collective-permute-start(f32[128,128]{1,0:T(8,128)S(1)} %get-tuple-element.25), channel_id=1, source_target_pairs={{0,1},{1,2},{2,3},{3,4},{4,5},{5,6},{6,7},{7,0},{8,9},{9,10},{10,1... | collective-permute-start | bytes 196616 | tf_op jit(solution)/shard_map/ppermute | solution.py:29
  22.0 6.8 %all-to-all-start = ((f32[8,160,128]{2,1,0:T(8,128)}), f32[8,160,128]{2,1,0:T(8,128)S(1)}, u32[]{:S(2)}, u32[]{:S(2)}) async-start(f32[8,160,128]{2,1,0:T(8,128)} %get-tuple-element.24), calls=%async_computation | async-start | bytes 1310720 | tf_op jit(solution)/shard_map/all_to_all | solution.py:33
  28.8 0.0 collective-permute-done.2
  28.8 0.0 collective-permute-done.1
  28.9 1.9 %collective-permute-start.5 = (f32[2,128,128]{2,1,0:T(8,128)S(1)}, f32[2,128,128]{2,1,0:T(8,128)S(1)}, u32[]{:S(2)}, u32[]{:S(2)}) collective-permute-start(f32[2,128,128]{2,1,0:T(8,128)S(1)} %get-tuple-element.44), channel_id=1, source_target_pairs={{0,6},{1,7},{2,0},{3,1},{4,2},{5,3},{6,4},{7,5},{8,14},{9,15},{10,... | collective-permute-start | bytes 393224 | tf_op jit(solution)/shard_map/ppermute | solution.py:29
  30.8 4.2 %collective-permute-start.4 = (f32[2,128,128]{2,1,0:T(8,128)S(1)}, f32[2,128,128]{2,1,0:T(8,128)S(1)}, u32[]{:S(2)}, u32[]{:S(2)}) collective-permute-start(f32[2,128,128]{2,1,0:T(8,128)S(1)} %get-tuple-element.45), channel_id=1, source_target_pairs={{0,2},{1,3},{2,4},{3,5},{4,6},{5,7},{6,0},{7,1},{8,10},{9,11},{10,... | collective-permute-start | bytes 393224 | tf_op jit(solution)/shard_map/ppermute | solution.py:29
  35.1 0.0 collective-permute-done.3
  35.1 4.5 %collective-permute-done.4 = f32[2,128,128]{2,1,0:T(8,128)S(1)} collective-permute-done((f32[2,128,128]{2,1,0:T(8,128)S(1)}, f32[2,128,128]{2,1,0:T(8,128)S(1)}, u32[]{:S(2)}, u32[]{:S(2)}) %collective-permute-start.4) | collective-permute-done | bytes 131104 | tf_op jit(solution)/shard_map/ppermute | solution.py:29
  39.6 0.0 collective-permute-done.5
  39.6 4.4 %collective-permute-start.6 = (f32[8,128,128]{2,1,0:T(8,128)S(1)}, f32[8,128,128]{2,1,0:T(8,128)S(1)}, u32[]{:S(2)}, u32[]{:S(2)}) collective-permute-start(f32[8,128,128]{2,1,0:T(8,128)S(1)} %constant_dynamic-update-slice_fusion.same), channel_id=1, source_target_pairs={{0,8},{8,0},{1,9},{9,1},{2,10},{10,2},{3,11},{11,3},{4,12},{12,4},... | collective-permute-start | bytes 1572872 | tf_op jit(solution)/shard_map/ppermute | solution.py:29
  44.0 4.1 %all-to-all-done.cols = f32[8,160,128]{2,1,0:T(8,128)S(1)} async-done(((f32[8,160,128]{2,1,0:T(8,128)}), f32[8,160,128]{2,1,0:T(8,128)S(1)}, u32[]{:S(2)}, u32[]{:S(2)}) %all-to-all-start) | async-done | bytes 655392 | tf_op jit(solution)/shard_map/all_to_all | solution.py:33
  48.1 3.1 %collective-permute-start.8 = (f32[8,160,128]{2,1,0:T(8,128)S(1)}, f32[8,160,128]{2,1,0:T(8,128)S(1)}, u32[]{:S(2)}, u32[]{:S(2)}) collective-permute-start(f32[8,160,128]{2,1,0:T(8,128)S(1)} %all-to-all-done.cols), channel_id=1, source_target_pairs={{0,128},{128,256},{256,384},{384,0},{1,129},{129,257},{257,385},{3... | collective-permute-start | bytes 1966088 | tf_op jit(solution)/shard_map/ppermute | solution.py:29
  51.2 3.4 %collective-permute-start.7 = (f32[8,160,128]{2,1,0:T(8,128)S(1)}, f32[8,160,128]{2,1,0:T(8,128)S(1)}, u32[]{:S(2)}, u32[]{:S(2)}) collective-permute-start(f32[8,160,128]{2,1,0:T(8,128)S(1)} %all-to-all-done.cols), channel_id=1, source_target_pairs={{0,384},{128,0},{256,128},{384,256},{1,385},{129,1},{257,129},{385... | collective-permute-start | bytes 1966088 | tf_op jit(solution)/shard_map/ppermute | solution.py:29
  54.6 3.4 %collective-permute-start = (f32[8,160,128]{2,1,0:T(8,128)S(1)}, f32[8,160,128]{2,1,0:T(8,128)S(1)}, u32[]{:S(2)}, u32[]{:S(2)}) collective-permute-start(f32[8,160,128]{2,1,0:T(8,128)S(1)} %all-to-all-done.cols), channel_id=1, source_target_pairs={{0,256},{128,384},{256,0},{384,128},{1,257},{129,385},{257,1},{385... | collective-permute-start | bytes 1966088 | tf_op jit(solution)/shard_map/ppermute | solution.py:29
  58.0 0.0 collective-permute-done.6.other
  58.0 6.0 %own_chunk.1 = (f32[16,32,128]{2,1,0:T(8,128)S(1)}, bf16[4,1024,512]{2,1,0:T(8,128)(2,1)S(1)}, bf16[4,1024,512]{2,1,0:T(8,128)(2,1)S(1)}, bf16[4,512,512]{2,1,0:T(8,128)(2,1)S(1)}, f32[4,1,512]{2,1,0:T(1,128)S(1)}) custom-call(s32[1]{0:T(128)} %bitcast.1.place, f32[8,160,128]{2,1,0:T(8,128)S(1)} %all-to-all-done.cols, ...), custom_call_target="tpu_custom_call" | custom-call | flops 3221225472 | bytes 8388608 | tf_op jit(solution)/shard_map/own_chunk/pallas_call | solution.py:149
  64.0 1.4 collective-permute-done.8.refs_0_
  65.5 5.6 %more_chunk.3 = (f32[16,32,128]{2,1,0:T(8,128)S(1)}, bf16[4,1024,512]{2,1,0:T(8,128)(2,1)S(1)}, bf16[4,1024,512]{2,1,0:T(8,128)(2,1)S(1)}) custom-call(f32[8,160,128]{2,1,0:T(8,128)S(1)} %collective-permute-done.8.refs_0_, bf16[4,512,512]{2,1,0:T(8,128)(2,1)S(1)} %get-tuple-element.26.refs_1_, f32[4,1,512]{2,1,0:T(1,128)S(1)} %get-tuple-element.27.refs_2_, ...), custom_call_target="tpu_custom_call" | custom-call | flops 3221225472 | bytes 8388608 | tf_op jit(solution)/shard_map/more_chunk/pallas_call | solution.py:162
  71.1 0.0 collective-permute-done.7.refs_0_
  71.1 5.7 %more_chunk.4 = (f32[16,32,128]{2,1,0:T(8,128)S(1)}, bf16[4,1024,512]{2,1,0:T(8,128)(2,1)S(1)}, bf16[4,1024,512]{2,1,0:T(8,128)(2,1)S(1)}) custom-call(f32[8,160,128]{2,1,0:T(8,128)S(1)} %collective-permute-done.7.refs_0_, bf16[4,512,512]{2,1,0:T(8,128)(2,1)S(1)} %get-tuple-element.26.refs_1_, f32[4,1,512]{2,1,0:T(1,128)S(1)} %get-tuple-element.27.refs_2_, ...), custom_call_target="tpu_custom_call" | custom-call | flops 3221225472 | bytes 8388608 | tf_op jit(solution)/shard_map/more_chunk/pallas_call | solution.py:162
  76.8 3.7 %collective-permute-done.refs_0_ = f32[8,160,128]{2,1,0:T(8,128)S(1)} collective-permute-done((f32[8,160,128]{2,1,0:T(8,128)S(1)}, f32[8,160,128]{2,1,0:T(8,128)S(1)}, u32[]{:S(2)}, u32[]{:S(2)}) %collective-permute-start) | collective-permute-done | bytes 655392 | tf_op jit(solution)/shard_map/ppermute | solution.py:29
  80.5 0.0 copy-start.1
  80.5 5.6 %more_chunk.5 = (f32[16,32,128]{2,1,0:T(8,128)S(1)}, bf16[4,1024,512]{2,1,0:T(8,128)(2,1)S(1)}, bf16[4,1024,512]{2,1,0:T(8,128)(2,1)S(1)}) custom-call(f32[8,160,128]{2,1,0:T(8,128)S(1)} %collective-permute-done.refs_0_, bf16[4,512,512]{2,1,0:T(8,128)(2,1)S(1)} %get-tuple-element.26.refs_1_, f32[4,1,512]{2,1,0:T(1,128)S(1)} %get-tuple-element.27.refs_2_, ...), custom_call_target="tpu_custom_call" | custom-call | flops 3221225472 | bytes 8388608 | tf_op jit(solution)/shard_map/more_chunk/pallas_call | solution.py:162
  86.2 10.7 %collective-permute-start.9 = (f32[8,32,128]{2,1,0:T(8,128)S(1)}, f32[8,32,128]{2,1,0:T(8,128)S(1)}, u32[]{:S(2)}, u32[]{:S(2)}) collective-permute-start(f32[8,32,128]{2,1,0:T(8,128)S(1)} %slice.10), channel_id=1, source_target_pairs={{0,8},{8,0},{1,9},{9,1},{2,10},{10,2},{3,11},{11,3},{4,12},{12,4},... | collective-permute-start | bytes 393224 | tf_op jit(solution)/shard_map/ppermute | solution.py:29
  96.8 1.0 collective-permute-done.9
  97.8 13.4 %all_to_all.30.arrived = f32[8,32,128]{2,1,0:T(8,128)S(1)} all-to-all(f32[8,32,128]{2,1,0:T(8,128)S(1)} %slice_add_fusion), channel_id=1, replica_groups=mesh['x'=4,'y'=8,'c'=2,'z'=8] {'z'}, dimensions={0} | all-to-all | bytes 262144 | tf_op jit(solution)/shard_map/all_to_all | solution.py:33
  111.2 0.0 copy-done.1
  111.2 0.2 between.1
  111.4 14.1 %all_to_all.31.refs_0_ = f32[8,40,128]{2,1,0:T(8,128)S(1)} all-to-all(f32[8,40,128]{2,1,0:T(8,128)S(1)} %get-tuple-element.32), channel_id=1, replica_groups=mesh['x'=4,'y'=8,'c'=2,'z'=8] {'y'}, dimensions={0} | all-to-all | bytes 327680 | tf_op jit(solution)/shard_map/all_to_all | solution.py:33
  125.6 1.9 %collective-permute-start.12 = (f32[8,40,128]{2,1,0:T(8,128)S(1)}, f32[8,40,128]{2,1,0:T(8,128)S(1)}, u32[]{:S(2)}, u32[]{:S(2)}) collective-permute-start(f32[8,40,128]{2,1,0:T(8,128)S(1)} %all_to_all.31.refs_0_), channel_id=1, source_target_pairs={{0,256},{128,384},{256,0},{384,128},{1,257},{129,385},{257,1},{385... | collective-permute-start | bytes 491528 | tf_op jit(solution)/shard_map/ppermute | solution.py:29
  127.5 5.3 %collective-permute-start.11 = (f32[8,40,128]{2,1,0:T(8,128)S(1)}, f32[8,40,128]{2,1,0:T(8,128)S(1)}, u32[]{:S(2)}, u32[]{:S(2)}) collective-permute-start(f32[8,40,128]{2,1,0:T(8,128)S(1)} %all_to_all.31.refs_0_), channel_id=1, source_target_pairs={{0,384},{128,0},{256,128},{384,256},{1,385},{129,1},{257,129},{385... | collective-permute-start | bytes 491528 | tf_op jit(solution)/shard_map/ppermute | solution.py:29
  132.8 2.5 %collective-permute-start.10 = (f32[8,40,128]{2,1,0:T(8,128)S(1)}, f32[8,40,128]{2,1,0:T(8,128)S(1)}, u32[]{:S(2)}, u32[]{:S(2)}) collective-permute-start(f32[8,40,128]{2,1,0:T(8,128)S(1)} %all_to_all.31.refs_0_), channel_id=1, source_target_pairs={{0,128},{128,256},{256,384},{384,0},{1,129},{129,257},{257,385},{3... | collective-permute-start | bytes 491528 | tf_op jit(solution)/shard_map/ppermute | solution.py:29
  135.3 1.5 second_4x1.1.refs_9_
  136.8 0.0 collective-permute-done.12.refs_2_
  136.8 0.0 collective-permute-done.11.refs_1_
  136.8 3.2 %collective-permute-done.10.refs_0_ = f32[8,40,128]{2,1,0:T(8,128)S(1)} collective-permute-done((f32[8,40,128]{2,1,0:T(8,128)S(1)}, f32[8,40,128]{2,1,0:T(8,128)S(1)}, u32[]{:S(2)}, u32[]{:S(2)}) %collective-permute-start.10) | collective-permute-done | bytes 163872 | tf_op jit(solution)/shard_map/ppermute | solution.py:29
  140.0 2.3 %second_2x3.3 = f32[8,40,128]{2,1,0:T(8,128)S(1)} custom-call(f32[8,40,128]{2,1,0:T(8,128)S(1)} %collective-permute-done.10.refs_0_, f32[8,40,128]{2,1,0:T(8,128)S(1)} %collective-permute-done.11.refs_1_, f32[8,40,128]{2,1,0:T(8,128)S(1)} %collective-permute-done.12.refs_2_, bf16[4,1024,512]{2,1,0:T(8,128)(2,1)S(1)} %get-tuple-element.33.refs_3_, ...), custom_call_target="tpu_custom_call" | custom-call | flops 805306368 | bytes 12582912 | tf_op jit(solution)/shard_map/second_2x3/pallas_call | solution.py:247
  142.3 6.8 %collective-permute-start.13 = (f32[8,40,128]{2,1,0:T(8,128)S(1)}, f32[8,40,128]{2,1,0:T(8,128)S(1)}, u32[]{:S(2)}, u32[]{:S(2)}) collective-permute-start(f32[8,40,128]{2,1,0:T(8,128)S(1)} %second_2x3.3), channel_id=1, source_target_pairs={{0,8},{8,0},{1,9},{9,1},{2,10},{10,2},{3,11},{11,3},{4,12},{12,4},... | collective-permute-start | bytes 491528 | tf_op jit(solution)/shard_map/ppermute | solution.py:29
  149.1 2.3 %second_2x3.2 = f32[8,40,128]{2,1,0:T(8,128)S(1)} custom-call(f32[8,40,128]{2,1,0:T(8,128)S(1)} %collective-permute-done.10.refs_0_, f32[8,40,128]{2,1,0:T(8,128)S(1)} %collective-permute-done.11.refs_1_, f32[8,40,128]{2,1,0:T(8,128)S(1)} %collective-permute-done.12.refs_2_, bf16[4,1024,512]{2,1,0:T(8,128)(2,1)S(1)} %get-tuple-element.33.refs_3_, ...), custom_call_target="tpu_custom_call" | custom-call | flops 805306368 | bytes 12582912 | tf_op jit(solution)/shard_map/second_2x3/pallas_call | solution.py:247
  151.4 0.0 collective-permute-done.13
  151.4 12.7 %all_to_all.32.arrived = f32[8,40,128]{2,1,0:T(8,128)S(1)} all-to-all(f32[8,40,128]{2,1,0:T(8,128)S(1)} %add.7), channel_id=1, replica_groups=mesh['x'=4,'y'=8,'c'=2,'z'=8] {'z'}, dimensions={0} | all-to-all | bytes 327680 | tf_op jit(solution)/shard_map/all_to_all | solution.py:33
  164.1 0.4 settle.1
  164.4 9.9 %all_to_all.33 = f32[16,1,128]{2,1,0:T(1,128)S(1)} all-to-all(f32[16,1,128]{2,1,0:T(1,128)S(1)} %broadcast_in_dim.23), channel_id=1, replica_groups=mesh['x'=4,'y'=8,'c'=2,'z'=8] {'y','c'}, dimensions={0} | all-to-all | bytes 16384 | tf_op jit(solution)/shard_map/all_to_all | solution.py:33
  174.4 11.6 %all_to_all.34.forms = f32[32,1,128]{2,1,0:T(1,128)S(1)} all-to-all(f32[32,1,128]{2,1,0:T(1,128)S(1)} %broadcast_in_dim.24), channel_id=1, replica_groups=mesh['x'=4,'y'=8,'c'=2,'z'=8] {'x','z'}, dimensions={0} | all-to-all | bytes 32768 | tf_op jit(solution)/shard_map/all_to_all | solution.py:33
  186.0 0.8 finish.1
  (14 shorter events, 0.2 us)
Async XLA Ops:
  2.7 0.7 copy-start
  3.4 0.8 copy-start.2
  5.2 29.9 %collective-permute-start.3 = (f32[128,128]{1,0:T(8,128)S(1)}, f32[128,128]{1,0:T(8,128)S(1)}, u32[]{:S(2)}, u32[]{:S(2)}) collective-permute-start(f32[128,128]{1,0:T(8,128)S(1)} %get-tuple-element.25), channel_id=1, source_target_pairs={{0,4},{1,5},{2,6},{3,7},{4,0},{5,1},{6,2},{7,3},{8,12},{9,13},{10,... | collective-permute-start | bytes 196616 | tf_op jit(solution)/shard_map/ppermute | solution.py:29
  16.7 12.1 %collective-permute-start.2 = (f32[128,128]{1,0:T(8,128)S(1)}, f32[128,128]{1,0:T(8,128)S(1)}, u32[]{:S(2)}, u32[]{:S(2)}) collective-permute-start(f32[128,128]{1,0:T(8,128)S(1)} %get-tuple-element.25), channel_id=1, source_target_pairs={{0,7},{1,0},{2,1},{3,2},{4,3},{5,4},{6,5},{7,6},{8,15},{9,8},{10,9... | collective-permute-start | bytes 196616 | tf_op jit(solution)/shard_map/ppermute | solution.py:29
  18.6 10.2 %collective-permute-start.1 = (f32[128,128]{1,0:T(8,128)S(1)}, f32[128,128]{1,0:T(8,128)S(1)}, u32[]{:S(2)}, u32[]{:S(2)}) collective-permute-start(f32[128,128]{1,0:T(8,128)S(1)} %get-tuple-element.25), channel_id=1, source_target_pairs={{0,1},{1,2},{2,3},{3,4},{4,5},{5,6},{6,7},{7,0},{8,9},{9,10},{10,1... | collective-permute-start | bytes 196616 | tf_op jit(solution)/shard_map/ppermute | solution.py:29
  22.0 26.1 %all-to-all-start = ((f32[8,160,128]{2,1,0:T(8,128)}), f32[8,160,128]{2,1,0:T(8,128)S(1)}, u32[]{:S(2)}, u32[]{:S(2)}) async-start(f32[8,160,128]{2,1,0:T(8,128)} %get-tuple-element.24), calls=%async_computation | async-start | bytes 1310720 | tf_op jit(solution)/shard_map/all_to_all | solution.py:33
  28.9 10.7 %collective-permute-start.5 = (f32[2,128,128]{2,1,0:T(8,128)S(1)}, f32[2,128,128]{2,1,0:T(8,128)S(1)}, u32[]{:S(2)}, u32[]{:S(2)}) collective-permute-start(f32[2,128,128]{2,1,0:T(8,128)S(1)} %get-tuple-element.44), channel_id=1, source_target_pairs={{0,6},{1,7},{2,0},{3,1},{4,2},{5,3},{6,4},{7,5},{8,14},{9,15},{10,... | collective-permute-start | bytes 393224 | tf_op jit(solution)/shard_map/ppermute | solution.py:29
  30.8 8.8 %collective-permute-start.4 = (f32[2,128,128]{2,1,0:T(8,128)S(1)}, f32[2,128,128]{2,1,0:T(8,128)S(1)}, u32[]{:S(2)}, u32[]{:S(2)}) collective-permute-start(f32[2,128,128]{2,1,0:T(8,128)S(1)} %get-tuple-element.45), channel_id=1, source_target_pairs={{0,2},{1,3},{2,4},{3,5},{4,6},{5,7},{6,0},{7,1},{8,10},{9,11},{10,... | collective-permute-start | bytes 393224 | tf_op jit(solution)/shard_map/ppermute | solution.py:29
  39.6 18.4 %collective-permute-start.6 = (f32[8,128,128]{2,1,0:T(8,128)S(1)}, f32[8,128,128]{2,1,0:T(8,128)S(1)}, u32[]{:S(2)}, u32[]{:S(2)}) collective-permute-start(f32[8,128,128]{2,1,0:T(8,128)S(1)} %constant_dynamic-update-slice_fusion.same), channel_id=1, source_target_pairs={{0,8},{8,0},{1,9},{9,1},{2,10},{10,2},{3,11},{11,3},{4,12},{12,4},... | collective-permute-start | bytes 1572872 | tf_op jit(solution)/shard_map/ppermute | solution.py:29
  48.1 17.4 %collective-permute-start.8 = (f32[8,160,128]{2,1,0:T(8,128)S(1)}, f32[8,160,128]{2,1,0:T(8,128)S(1)}, u32[]{:S(2)}, u32[]{:S(2)}) collective-permute-start(f32[8,160,128]{2,1,0:T(8,128)S(1)} %all-to-all-done.cols), channel_id=1, source_target_pairs={{0,128},{128,256},{256,384},{384,0},{1,129},{129,257},{257,385},{3... | collective-permute-start | bytes 1966088 | tf_op jit(solution)/shard_map/ppermute | solution.py:29
  51.2 19.9 %collective-permute-start.7 = (f32[8,160,128]{2,1,0:T(8,128)S(1)}, f32[8,160,128]{2,1,0:T(8,128)S(1)}, u32[]{:S(2)}, u32[]{:S(2)}) collective-permute-start(f32[8,160,128]{2,1,0:T(8,128)S(1)} %all-to-all-done.cols), channel_id=1, source_target_pairs={{0,384},{128,0},{256,128},{384,256},{1,385},{129,1},{257,129},{385... | collective-permute-start | bytes 1966088 | tf_op jit(solution)/shard_map/ppermute | solution.py:29
  54.6 25.9 %collective-permute-start = (f32[8,160,128]{2,1,0:T(8,128)S(1)}, f32[8,160,128]{2,1,0:T(8,128)S(1)}, u32[]{:S(2)}, u32[]{:S(2)}) collective-permute-start(f32[8,160,128]{2,1,0:T(8,128)S(1)} %all-to-all-done.cols), channel_id=1, source_target_pairs={{0,256},{128,384},{256,0},{384,128},{1,257},{129,385},{257,1},{385... | collective-permute-start | bytes 1966088 | tf_op jit(solution)/shard_map/ppermute | solution.py:29
  80.5 30.7 %copy-start.1 = (f32[32,128]{1,0:T(8,128)S(1)}, f32[32,128]{1,0:T(8,128)}, u32[]{:S(2)}) copy-start(f32[32,128]{1,0:T(8,128)} %targets.5) | copy-start | bytes 49156
  86.2 11.6 %collective-permute-start.9 = (f32[8,32,128]{2,1,0:T(8,128)S(1)}, f32[8,32,128]{2,1,0:T(8,128)S(1)}, u32[]{:S(2)}, u32[]{:S(2)}) collective-permute-start(f32[8,32,128]{2,1,0:T(8,128)S(1)} %slice.10), channel_id=1, source_target_pairs={{0,8},{8,0},{1,9},{9,1},{2,10},{10,2},{3,11},{11,3},{4,12},{12,4},... | collective-permute-start | bytes 393224 | tf_op jit(solution)/shard_map/ppermute | solution.py:29
  125.6 11.3 %collective-permute-start.12 = (f32[8,40,128]{2,1,0:T(8,128)S(1)}, f32[8,40,128]{2,1,0:T(8,128)S(1)}, u32[]{:S(2)}, u32[]{:S(2)}) collective-permute-start(f32[8,40,128]{2,1,0:T(8,128)S(1)} %all_to_all.31.refs_0_), channel_id=1, source_target_pairs={{0,256},{128,384},{256,0},{384,128},{1,257},{129,385},{257,1},{385... | collective-permute-start | bytes 491528 | tf_op jit(solution)/shard_map/ppermute | solution.py:29
  127.5 9.3 %collective-permute-start.11 = (f32[8,40,128]{2,1,0:T(8,128)S(1)}, f32[8,40,128]{2,1,0:T(8,128)S(1)}, u32[]{:S(2)}, u32[]{:S(2)}) collective-permute-start(f32[8,40,128]{2,1,0:T(8,128)S(1)} %all_to_all.31.refs_0_), channel_id=1, source_target_pairs={{0,384},{128,0},{256,128},{384,256},{1,385},{129,1},{257,129},{385... | collective-permute-start | bytes 491528 | tf_op jit(solution)/shard_map/ppermute | solution.py:29
  132.8 7.3 %collective-permute-start.10 = (f32[8,40,128]{2,1,0:T(8,128)S(1)}, f32[8,40,128]{2,1,0:T(8,128)S(1)}, u32[]{:S(2)}, u32[]{:S(2)}) collective-permute-start(f32[8,40,128]{2,1,0:T(8,128)S(1)} %all_to_all.31.refs_0_), channel_id=1, source_target_pairs={{0,128},{128,256},{256,384},{384,0},{1,129},{129,257},{257,385},{3... | collective-permute-start | bytes 491528 | tf_op jit(solution)/shard_map/ppermute | solution.py:29
  142.3 9.1 %collective-permute-start.13 = (f32[8,40,128]{2,1,0:T(8,128)S(1)}, f32[8,40,128]{2,1,0:T(8,128)S(1)}, u32[]{:S(2)}, u32[]{:S(2)}) collective-permute-start(f32[8,40,128]{2,1,0:T(8,128)S(1)} %second_2x3.3), channel_id=1, source_target_pairs={{0,8},{8,0},{1,9},{9,1},{2,10},{10,2},{3,11},{11,3},{4,12},{12,4},... | collective-permute-start | bytes 491528 | tf_op jit(solution)/shard_map/ppermute | solution.py:29
where the time goes:
time: 188 us; the launch traced here: 187 us
  starting transfers between devices  71.2 us (38%)
  blocking collectives  61.8 us (33%)
  Pallas kernels  31.4 us (17%)
  waiting for transfers between devices  17.9 us (10%)
  local copies, waits for them, and re-layouts  2.41 us (1%)
  between operations  2.18 us (1%)
    ppermute x14, starting transfers between devices, shift(): lax.ppermute(value, axis, [(s, (s + steps) % count) for s in range(count)])  64.3 us
    all_to_all x5, blocking collectives, exchange(): return lax.all_to_all(x, axes, 0, 0, tiled=True)  61.8 us
    pallas_call x3, Pallas kernels, more_chunk(): pl.pallas_call(functools.partial(more_kernel, len(cols)), in_specs=[VMEM]...  16.9 us
    ppermute x14, waiting for transfers between devices, shift(): lax.ppermute(value, axis, [(s, (s + steps) % count) for s in range(count)])  13.8 us
    all_to_all x1, starting transfers between devices, exchange(): return lax.all_to_all(x, axes, 0, 0, tiled=True)  6.83 us
    pallas_call x3, Pallas kernels, second(): pl.pallas_call(functools.partial(second_kernel, tiles, count), in_specs=[...  6.07 us
    pallas_call x1, Pallas kernels, own_chunk(): pl.pallas_call(own_kernel, in_specs=[SMEM] + [VMEM] * 3, out_specs=[VMEM]...  6.01 us
    all_to_all x1, waiting for transfers between devices, exchange(): return lax.all_to_all(x, axes, 0, 0, tiled=True)  4.06 us
  transfers between devices with their start and end apart: 15, of which 6 were waited for; matrix products, arithmetic and copies ran while one was open for 0% of the time, Pallas kernels for 11%

commit v1 on v0

v1 whole, which is shorter than its diff:
```python
import functools
import math

import jax
import jax.numpy as jnp
from jax import lax
from jax.experimental import pallas as pl
from jax.experimental.pallas import tpu as pltpu
from jax.sharding import Mesh
from jax.sharding import PartitionSpec as P


AXES = ("x", "y", "c", "z")
F32 = jnp.float32
BF16 = jnp.bfloat16
ROOT = math.sqrt(math.log2(math.e))
BLK = 128
RHS = 32
TILE = 512
SUB = 512
WIDE = 1024
VMEM = pl.BlockSpec(memory_space=pltpu.VMEM)
SMEM = pl.BlockSpec(memory_space=pltpu.SMEM)
PARAMS = pltpu.CompilerParams(vmem_limit_bytes=12 << 20)


def shift(value, axis, steps):
    count = lax.axis_size(axis)
    return lax.ppermute(value, axis, [(s, (s + steps) % count) for s in range(count)])


def exchange(x, axes):
    return lax.all_to_all(x, axes, 0, 0, tiled=True)


def halves(x):
    high = x.astype(BF16)
    return high, (x - high.astype(F32)).astype(BF16)


def kept(x):
    return pltpu.with_memory_space_constraint(x, pltpu.VMEM)


def cost(flops=0, moved=0, powers=0):
    return pl.CostEstimate(flops=flops, bytes_accessed=moved, transcendentals=powers)


def spread_kernel(points, lengths, targets, scale, noise, out, own, aux):
    scaled = points[...] / jnp.broadcast_to(lengths[...], (BLK, BLK)).T
    vectors = targets[...]
    own[...] = scaled
    for peer in range(8):
        out[peer, pl.ds(0, BLK), :] = scaled
        out[peer, pl.ds(BLK, RHS), :] = vectors
    aux[...] = jnp.where(lax.broadcasted_iota(jnp.int32, (8, BLK), 0) == 0, scale[0], noise[0])


def spread(points, lengths, targets, scale, noise):
    return pl.pallas_call(
        spread_kernel,
        in_specs=[VMEM, VMEM, VMEM, SMEM, SMEM],
        out_specs=[VMEM] * 3,
        out_shape=[
            jax.ShapeDtypeStruct((8, BLK + RHS, BLK), F32),
            jax.ShapeDtypeStruct((BLK, BLK), F32),
            jax.ShapeDtypeStruct((8, BLK), F32),
        ],
        compiler_params=PARAMS,
        name="spread",
    )(points, lengths, targets, scale, noise)


ORDER = (0, -1, 1, 4, -3, -2, 2, 3)


def prepare_rows(place, row_refs, left, left_sq):
    for block in range(16):
        value = row_refs[block // 8][block % 8] * ROOT
        high, low = halves(value)
        z = lax.rem(place[0] + (ORDER[block % 8] + 8), 8)
        at = block // 8 * 2 + lax.div(z, 4)
        lanes = pl.ds(pl.multiple_of(lax.rem(z, 4) * BLK, BLK), BLK)
        left[at, pl.ds(0, 128), lanes] = high
        left[at, pl.ds(128, 128), lanes] = low
        left[at, pl.ds(256, 128), lanes] = high
        left[at, pl.ds(384, 128), lanes] = low
        left_sq[at, :, lanes] = -0.5 * jnp.sum(value * value, axis=0, keepdims=True)


def prepare_cols(col_refs, right, right_sq, vecs):
    each = 8 // len(col_refs)
    for block in range(8):
        ref, at = col_refs[block // each], block % each
        value = ref[at, pl.ds(0, BLK), :].T * ROOT
        high, low = halves(value)
        rows = pl.ds(block * BLK, BLK)
        right[rows, pl.ds(0, 128)] = high
        right[rows, pl.ds(128, 128)] = high
        right[rows, pl.ds(256, 128)] = low
        right[rows, pl.ds(384, 128)] = low
        right_sq[rows, :] = -0.5 * jnp.sum(value * value, axis=1, keepdims=True)
        high, low = halves(ref[at, pl.ds(BLK, RHS), :])
        vecs[pl.ds(0, RHS), rows] = high
        vecs[pl.ds(RHS, RHS), rows] = low


def make_values(tiles, left, left_sq, right, right_sq, vecs, high_ref, low_ref, out, before):
    def one(to, carry):
        tile = tiles[0] + to
        total = jnp.zeros((RHS, TILE), F32)
        for step in range(WIDE // SUB):
            rows = pl.ds(step * SUB, SUB)
            power = jnp.dot(right[rows, :], left[tile], preferred_element_type=F32)
            high, low = halves(jnp.exp2(power + right_sq[rows, :] + left_sq[tile]))
            high_ref[to, rows, :] = high
            low_ref[to, rows, :] = low
            both = jnp.dot(vecs[:, rows], high, preferred_element_type=F32)
            rest = jnp.dot(vecs[pl.ds(0, RHS), rows], low, preferred_element_type=F32)
            total = total + both[:RHS] + both[RHS:] + rest
        for local in range(TILE // BLK):
            piece = total[:, local * BLK : (local + 1) * BLK]
            if before is not None:
                piece = piece + before[tile * (TILE // BLK) + local]
            out[to * (TILE // BLK) + local] = piece
        return carry

    lax.fori_loop(0, len(tiles), one, 0)


def own_kernel(place, cols, same, other, out, high, low, left, left_sq, right, right_sq, vecs):
    prepare_rows(place, (same, other), left, left_sq)
    prepare_cols((cols,), right, right_sq, vecs)
    make_values(ALL, left, left_sq, right, right_sq, vecs, high, low, out, None)


def more_kernel(tiles, cols, left, left_sq, before, out, high, low, right, right_sq, vecs):
    prepare_cols((cols,), right, right_sq, vecs)
    make_values(tiles, left, left_sq, right, right_sq, vecs, high, low, out, before)


ALL, MINE, THEIRS = (0, 1, 2, 3), (0, 1), (2, 3)


def made(tiles):
    values = pltpu.VMEM((len(tiles), WIDE, TILE), BF16)
    return [pltpu.VMEM((len(tiles) * TILE // BLK, RHS, BLK), F32), values, values]


def made_cost(tiles):
    width = len(tiles) * TILE
    return cost(2 * width * WIDE * 768, 4 * width * WIDE, width * WIDE)


LEFT = [pltpu.VMEM((4, 512, TILE), BF16), pltpu.VMEM((4, 1, TILE), F32)]
RIGHT = [pltpu.VMEM((WIDE, 512), BF16), pltpu.VMEM((WIDE, 1), F32), pltpu.VMEM((2 * RHS, WIDE), BF16)]


def own_chunk(place, cols, same, other):
    return pl.pallas_call(
        own_kernel,
        in_specs=[SMEM] + [VMEM] * 3,
        out_specs=[VMEM] * 5,
        out_shape=[*made(ALL), *LEFT],
        scratch_shapes=RIGHT,
        compiler_params=PARAMS,
        cost_estimate=made_cost(ALL),
        name="own_chunk",
    )(place, cols, same, other)


def more_chunk(tiles, cols, left, left_sq, before):
    return pl.pallas_call(
        functools.partial(more_kernel, tiles),
        in_specs=[VMEM] * 4,
        out_specs=[VMEM] * 3,
        out_shape=made(tiles),
        scratch_shapes=RIGHT,
        compiler_params=PARAMS,
        cost_estimate=made_cost(tiles),
    )(cols, kept(left), kept(left_sq), kept(before))


def total(x):
    return jnp.sum(x, axis=1, keepdims=True)


def between_kernel(aux, arrived, targets, first_ref, wide_ref):
    first = aux[0:1, 0:1] * jnp.sum(arrived[...], axis=0) + aux[1:2, 0:1] * targets[...]
    first_ref[...] = first
    for peer in range(32):
        wide_ref[peer] = first


def between(aux, arrived, targets):
    return pl.pallas_call(
        between_kernel,
        in_specs=[VMEM] * 3,
        out_specs=[VMEM] * 2,
        out_shape=[jax.ShapeDtypeStruct((RHS, BLK), F32), jax.ShapeDtypeStruct((32, RHS, BLK), F32)],
        compiler_params=PARAMS,
        name="between",
    )(aux, arrived, targets)


def second_kernel(tiles, gathered, *refs):
    highs, lows, out, vecs = refs[0:4], refs[4:8], refs[8], refs[9]
    place = lax.axis_index("x")
    for chunk in range(4):
        source = lax.rem(place + (0, 3, 1, 2)[chunk], 4) * 8
        for y in range(8):
            lanes = pl.ds(y * BLK, BLK)
            high, low = halves(gathered[source + y])
            vecs[chunk, pl.ds(0, RHS), lanes] = high
            vecs[chunk, pl.ds(RHS, RHS), lanes] = low
    for to, tile in enumerate(tiles):
        product = jnp.zeros((RHS, TILE), F32)
        for chunk in range(4):
            at = to if chunk == 3 else tile
            both = jnp.dot(vecs[chunk], highs[chunk][at], preferred_element_type=F32)
            rest = jnp.dot(vecs[chunk, pl.ds(0, RHS), :], lows[chunk][at], preferred_element_type=F32)
            product = product + both[:RHS] + both[RHS:] + rest
        for local in range(TILE // BLK):
            out[to * (TILE // BLK) + local] = product[:, local * BLK : (local + 1) * BLK]


def second(tiles, gathered, highs, lows):
    width = len(tiles) * TILE
    return pl.pallas_call(
        functools.partial(second_kernel, tiles),
        in_specs=[VMEM] * 9,
        out_specs=VMEM,
        out_shape=pltpu.VMEM((width // BLK, RHS, BLK), F32),
        scratch_shapes=[pltpu.VMEM((4, 2 * RHS, WIDE), BF16)],
        compiler_params=PARAMS,
        cost_estimate=cost(2 * width * 4 * WIDE * 128, 4 * width * 4 * WIDE, 0),
    )(gathered, *[kept(v) for v in highs], *[kept(v) for v in lows])


def total(x):
    return jnp.sum(x, axis=1, keepdims=True)


def settle_kernel(aux, arrived, targets, first_ref, second_ref, dots_ref):
    vectors, first = targets[...], first_ref[...]
    second_image = aux[0:1, 0:1] * jnp.sum(arrived[...], axis=0) + aux[1:2, 0:1] * first
    second_ref[...] = second_image
    dots = (vectors * vectors, vectors * first, first * first, first * second_image)
    lane = lax.broadcasted_iota(jnp.int32, (RHS, BLK), 1)
    wide = jnp.zeros((RHS, BLK), F32)
    for at, dot in enumerate(dots):
        wide = jnp.where(lane == at, total(dot), wide)
    tall = jnp.concatenate([wide, jnp.zeros((BLK - RHS, BLK), F32)], axis=0).T
    row = tall[0:1]
    for at in range(1, 4):
        row = row + pltpu.roll(tall[at : at + 1], at * RHS, 1)
    dots_ref[...] = jnp.broadcast_to(row, (8, BLK))


def settle(aux, arrived, targets, first):
    return pl.pallas_call(
        settle_kernel,
        in_specs=[VMEM] * 4,
        out_specs=[VMEM] * 2,
        out_shape=[jax.ShapeDtypeStruct((RHS, BLK), F32), jax.ShapeDtypeStruct((8, BLK), F32)],
        compiler_params=PARAMS,
        name="settle",
    )(aux, arrived, targets, first)


def finish_kernel(sums, targets, first_ref, second_ref, solution_ref, residual_ref):
    row = jnp.broadcast_to(jnp.sum(sums[...], axis=0), (8, BLK))
    sub = lax.broadcasted_iota(jnp.int32, (8, BLK), 0)
    rows = jnp.zeros((8, BLK), F32)
    for at in range(4):
        rows = jnp.where(sub == at, pltpu.roll(row, (BLK - at * RHS) % BLK, 1), rows)
    tall = jnp.concatenate([rows, jnp.zeros((BLK - 8, BLK), F32)], axis=0).T
    norm, curve, square, cubic = [tall[:RHS, at : at + 1] for at in range(4)]
    vectors, first = targets[...], first_ref[...]
    step = norm / curve
    norm_next = norm - 2.0 * step * curve + step * step * square
    more = 1.0 + norm_next / norm
    new_curve = more * more * curve - 2.0 * step * more * square + step * step * cubic
    new_step = norm_next / new_curve
    solution_ref[...] = step * vectors + new_step * (more * vectors - step * first)
    residual_ref[...] = vectors - step * first - new_step * (more * first - step * second_ref[...])


def finish(sums, targets, first, second_image):
    shape = jax.ShapeDtypeStruct((RHS, BLK), F32)
    return pl.pallas_call(
        finish_kernel,
        in_specs=[VMEM] * 4,
        out_specs=[VMEM] * 2,
        out_shape=[shape, shape],
        compiler_params=PARAMS,
        name="finish",
    )(sums, targets, first, second_image)


def to_each(x, axes):
    peers = lax.axis_size(axes)
    return exchange(jnp.broadcast_to(x[None], (peers, *x.shape)), axes)


def on_device(points, targets, lengthscales, outputscale, noise):
    near, own, aux = spread(points, lengthscales[None], targets, outputscale, noise)
    near = exchange(near, "y")
    behind, ahead, across = shift(near, "x", 1), shift(near, "x", -1), shift(near, "x", 2)
    below, above, far = shift(own, "z", 1), shift(own, "z", -1), shift(own, "z", 4)
    pairs = [shift(jnp.stack([below, own]), "z", 2), shift(jnp.stack([own, above]), "z", -2)]
    same = jnp.concatenate([jnp.stack([own, below, above, far]), *pairs])
    other = shift(same, "c", 1)
    place = lax.axis_index("z").astype(jnp.int32)[None]
    pieces, high, low, left, left_sq = own_chunk(place, near, same, other)
    highs, lows = [high], [low]
    for cols in (behind, ahead):
        pieces, high, low = more_chunk(ALL, cols, left, left_sq, pieces)
        highs.append(high)
        lows.append(low)
    theirs, high_theirs, low_theirs = more_chunk(THEIRS, across, left, left_sq, pieces)
    theirs = shift(theirs, "c", 1)
    mine, high_mine, low_mine = more_chunk(MINE, across, left, left_sq, pieces)
    arrived = exchange(mine + theirs, "z")
    first, wide = between(aux, arrived, targets)
    gathered = exchange(wide, ("x", "y"))
    theirs = shift(second(THEIRS, gathered, highs + [high_theirs], lows + [low_theirs]), "c", 1)
    mine = second(MINE, gathered, highs + [high_mine], lows + [low_mine])
    arrived = exchange(mine + theirs, "z")
    second_image, dots = settle(aux, arrived, targets, first)
    sums = jnp.sum(to_each(dots[0:1], ("y", "c")), axis=0)
    return tuple(finish(to_each(sums, ("x", "z")), targets, first, second_image))


def solution(mesh):
    finer = Mesh(mesh.devices.reshape(4, 8, 2, mesh.shape["row"]), AXES)
    spec = P(None, AXES)

    return jax.shard_map(
        on_device, mesh=finer, in_specs=(spec, spec, P(), P(), P()), out_specs=(spec, spec), check_vma=False
    )
```

time: 188 us -> 184 us (0.979)
  blocking collectives: 61.8 us -> 71 us
  starting transfers between devices: 71.2 us -> 62.2 us
  waiting for transfers between devices: 17.9 us -> 13.7 us
    all_to_all x5, blocking collectives: 61.8 us -> 71 us  [exchange(): return lax.all_to_all(x, axes, 0, 0, tiled=True)]
    ppermute x14 -> x11, starting transfers between devices: 64.3 us -> 55.3 us  [shift(): lax.ppermute(value, axis, [(s, (s + steps) % count) for s in range(count)])]
    ppermute x14 -> x11, waiting for transfers between devices: 13.8 us -> 9.61 us  [shift(): lax.ppermute(value, axis, [(s, (s + steps) % count) for s in range(count)])]
  transfers between devices with their start and end apart: 15 -> 12, of which waited for: 6 -> 4; matrix products, arithmetic and copies ran while one was open for 0% -> 0% of each run, Pallas kernels for 11% -> 13%
where the time goes in v1:
time: 184 us; the launch traced here: 183 us
  blocking collectives  71 us (39%)
  starting transfers between devices  62.2 us (34%)
  Pallas kernels  31.5 us (17%)
  waiting for transfers between devices  13.7 us (7%)
  local copies, waits for them, and re-layouts  2.29 us (1%)
  between operations  2.17 us (1%)
    all_to_all x5, blocking collectives, exchange(): return lax.all_to_all(x, axes, 0, 0, tiled=True)  71 us
    ppermute x11, starting transfers between devices, shift(): lax.ppermute(value, axis, [(s, (s + steps) % count) for s in range(count)])  55.3 us
    pallas_call x4, Pallas kernels, more_chunk(): pl.pallas_call(functools.partial(more_kernel, tiles), in_specs=[VMEM] * 4...  17.3 us
    ppermute x11, waiting for transfers between devices, shift(): lax.ppermute(value, axis, [(s, (s + steps) % count) for s in range(count)])  9.61 us
    all_to_all x1, starting transfers between devices, exchange(): return lax.all_to_all(x, axes, 0, 0, tiled=True)  6.83 us
    pallas_call x1, Pallas kernels, own_chunk(): pl.pallas_call(own_kernel, in_specs=[SMEM] + [VMEM] * 3, out_specs=[VMEM]...  5.99 us
    pallas_call x2, Pallas kernels, second(): pl.pallas_call(functools.partial(second_kernel, tiles), in_specs=[VMEM] *...  5.95 us
    all_to_all x1, waiting for transfers between devices, exchange(): return lax.all_to_all(x, axes, 0, 0, tiled=True)  4.06 us
  transfers between devices with their start and end apart: 12, of which 4 were waited for; matrix products, arithmetic and copies ran while one was open for 0% of the time, Pallas kernels for 13%

profile of v1, /device:TPU:1, one launch (start us, length us, event | category | flops | bytes accessed | tf_op | source)
XLA Modules:
  0.0 182.9 jit_solution(13790459581574878256)
XLA Ops:
  1.9 0.0 copy-start
  1.9 0.7 copy-done
  2.6 0.0 copy-start.2
  2.6 0.8 copy-done.2
  3.5 0.0 copy-start.3
  3.5 0.7 copy-done.3
  4.1 1.0 spread.1
  5.1 11.4 %collective-permute-start.3 = (f32[128,128]{1,0:T(8,128)S(1)}, f32[128,128]{1,0:T(8,128)S(1)}, u32[]{:S(2)}, u32[]{:S(2)}) collective-permute-start(f32[128,128]{1,0:T(8,128)S(1)} %get-tuple-element.28), channel_id=1, source_target_pairs={{0,4},{1,5},{2,6},{3,7},{4,0},{5,1},{6,2},{7,3},{8,12},{9,13},{10,... | collective-permute-start | bytes 196616 | tf_op jit(solution)/shard_map/ppermute | solution.py:29
  16.6 2.0 %collective-permute-start.2 = (f32[128,128]{1,0:T(8,128)S(1)}, f32[128,128]{1,0:T(8,128)S(1)}, u32[]{:S(2)}, u32[]{:S(2)}) collective-permute-start(f32[128,128]{1,0:T(8,128)S(1)} %get-tuple-element.28), channel_id=1, source_target_pairs={{0,7},{1,0},{2,1},{3,2},{4,3},{5,4},{6,5},{7,6},{8,15},{9,8},{10,9... | collective-permute-start | bytes 196616 | tf_op jit(solution)/shard_map/ppermute | solution.py:29
  18.5 3.3 %collective-permute-start.1 = (f32[128,128]{1,0:T(8,128)S(1)}, f32[128,128]{1,0:T(8,128)S(1)}, u32[]{:S(2)}, u32[]{:S(2)}) collective-permute-start(f32[128,128]{1,0:T(8,128)S(1)} %get-tuple-element.28), channel_id=1, source_target_pairs={{0,1},{1,2},{2,3},{3,4},{4,5},{5,6},{6,7},{7,0},{8,9},{9,10},{10,1... | collective-permute-start | bytes 196616 | tf_op jit(solution)/shard_map/ppermute | solution.py:29
  21.9 6.8 %all-to-all-start = ((f32[8,160,128]{2,1,0:T(8,128)}), f32[8,160,128]{2,1,0:T(8,128)S(1)}, u32[]{:S(2)}, u32[]{:S(2)}) async-start(f32[8,160,128]{2,1,0:T(8,128)} %get-tuple-element.27), calls=%async_computation | async-start | bytes 1310720 | tf_op jit(solution)/shard_map/all_to_all | solution.py:33
  28.7 0.0 collective-permute-done.2
  28.7 0.0 collective-permute-done.1
  28.8 1.9 %collective-permute-start.5 = (f32[2,128,128]{2,1,0:T(8,128)S(1)}, f32[2,128,128]{2,1,0:T(8,128)S(1)}, u32[]{:S(2)}, u32[]{:S(2)}) collective-permute-start(f32[2,128,128]{2,1,0:T(8,128)S(1)} %get-tuple-element.50), channel_id=1, source_target_pairs={{0,6},{1,7},{2,0},{3,1},{4,2},{5,3},{6,4},{7,5},{8,14},{9,15},{10,... | collective-permute-start | bytes 393224 | tf_op jit(solution)/shard_map/ppermute | solution.py:29
  30.7 4.2 %collective-permute-start.4 = (f32[2,128,128]{2,1,0:T(8,128)S(1)}, f32[2,128,128]{2,1,0:T(8,128)S(1)}, u32[]{:S(2)}, u32[]{:S(2)}) collective-permute-start(f32[2,128,128]{2,1,0:T(8,128)S(1)} %get-tuple-element.51), channel_id=1, source_target_pairs={{0,2},{1,3},{2,4},{3,5},{4,6},{5,7},{6,0},{7,1},{8,10},{9,11},{10,... | collective-permute-start | bytes 393224 | tf_op jit(solution)/shard_map/ppermute | solution.py:29
  35.0 0.0 collective-permute-done.3
  35.0 4.5 %collective-permute-done.4 = f32[2,128,128]{2,1,0:T(8,128)S(1)} collective-permute-done((f32[2,128,128]{2,1,0:T(8,128)S(1)}, f32[2,128,128]{2,1,0:T(8,128)S(1)}, u32[]{:S(2)}, u32[]{:S(2)}) %collective-permute-start.4) | collective-permute-done | bytes 131104 | tf_op jit(solution)/shard_map/ppermute | solution.py:29
  39.5 0.0 collective-permute-done.5
  39.5 4.4 %collective-permute-start.6 = (f32[8,128,128]{2,1,0:T(8,128)S(1)}, f32[8,128,128]{2,1,0:T(8,128)S(1)}, u32[]{:S(2)}, u32[]{:S(2)}) collective-permute-start(f32[8,128,128]{2,1,0:T(8,128)S(1)} %constant_dynamic-update-slice_fusion.same), channel_id=1, source_target_pairs={{0,8},{8,0},{1,9},{9,1},{2,10},{10,2},{3,11},{11,3},{4,12},{12,4},... | collective-permute-start | bytes 1572872 | tf_op jit(solution)/shard_map/ppermute | solution.py:29
  43.9 4.1 %all-to-all-done.cols = f32[8,160,128]{2,1,0:T(8,128)S(1)} async-done(((f32[8,160,128]{2,1,0:T(8,128)}), f32[8,160,128]{2,1,0:T(8,128)S(1)}, u32[]{:S(2)}, u32[]{:S(2)}) %all-to-all-start) | async-done | bytes 655392 | tf_op jit(solution)/shard_map/all_to_all | solution.py:33
  48.0 3.1 %collective-permute-start.8 = (f32[8,160,128]{2,1,0:T(8,128)S(1)}, f32[8,160,128]{2,1,0:T(8,128)S(1)}, u32[]{:S(2)}, u32[]{:S(2)}) collective-permute-start(f32[8,160,128]{2,1,0:T(8,128)S(1)} %all-to-all-done.cols), channel_id=1, source_target_pairs={{0,128},{128,256},{256,384},{384,0},{1,129},{129,257},{257,385},{3... | collective-permute-start | bytes 1966088 | tf_op jit(solution)/shard_map/ppermute | solution.py:29
  51.1 3.4 %collective-permute-start.7 = (f32[8,160,128]{2,1,0:T(8,128)S(1)}, f32[8,160,128]{2,1,0:T(8,128)S(1)}, u32[]{:S(2)}, u32[]{:S(2)}) collective-permute-start(f32[8,160,128]{2,1,0:T(8,128)S(1)} %all-to-all-done.cols), channel_id=1, source_target_pairs={{0,384},{128,0},{256,128},{384,256},{1,385},{129,1},{257,129},{385... | collective-permute-start | bytes 1966088 | tf_op jit(solution)/shard_map/ppermute | solution.py:29
  54.5 3.4 %collective-permute-start = (f32[8,160,128]{2,1,0:T(8,128)S(1)}, f32[8,160,128]{2,1,0:T(8,128)S(1)}, u32[]{:S(2)}, u32[]{:S(2)}) collective-permute-start(f32[8,160,128]{2,1,0:T(8,128)S(1)} %all-to-all-done.cols), channel_id=1, source_target_pairs={{0,256},{128,384},{256,0},{384,128},{1,257},{129,385},{257,1},{385... | collective-permute-start | bytes 1966088 | tf_op jit(solution)/shard_map/ppermute | solution.py:29
  57.9 0.0 collective-permute-done.6.other
  57.9 6.0 %own_chunk.1 = (f32[16,32,128]{2,1,0:T(8,128)S(1)}, bf16[4,1024,512]{2,1,0:T(8,128)(2,1)S(1)}, bf16[4,1024,512]{2,1,0:T(8,128)(2,1)S(1)}, bf16[4,512,512]{2,1,0:T(8,128)(2,1)S(1)}, f32[4,1,512]{2,1,0:T(1,128)S(1)}) custom-call(s32[1]{0:T(128)} %bitcast.1.place, f32[8,160,128]{2,1,0:T(8,128)S(1)} %all-to-all-done.cols, ...), custom_call_target="tpu_custom_call" | custom-call | flops 3221225472 | bytes 8388608 | tf_op jit(solution)/shard_map/own_chunk/pallas_call | solution.py:160
  63.9 1.4 collective-permute-done.8.cols
  65.3 5.7 %shard_map.68 = (f32[16,32,128]{2,1,0:T(8,128)S(1)}, bf16[4,1024,512]{2,1,0:T(8,128)(2,1)S(1)}, bf16[4,1024,512]{2,1,0:T(8,128)(2,1)S(1)}) custom-call(f32[8,160,128]{2,1,0:T(8,128)S(1)} %collective-permute-done.8.cols, bf16[4,512,512]{2,1,0:T(8,128)(2,1)S(1)} %get-tuple-element.29.left, f32[4,1,512]{2,1,0:T(1,128)S(1)} %get-tuple-element.30.left_sq, ...), custom_call_target="tpu_custom_call" | custom-call | flops 3221225472 | bytes 8388608 | tf_op jit(solution)/shard_map/pallas_call | solution.py:173
  71.0 0.0 collective-permute-done.7.cols
  71.0 5.6 %shard_map.69 = (f32[16,32,128]{2,1,0:T(8,128)S(1)}, bf16[4,1024,512]{2,1,0:T(8,128)(2,1)S(1)}, bf16[4,1024,512]{2,1,0:T(8,128)(2,1)S(1)}) custom-call(f32[8,160,128]{2,1,0:T(8,128)S(1)} %collective-permute-done.7.cols, bf16[4,512,512]{2,1,0:T(8,128)(2,1)S(1)} %get-tuple-element.29.left, f32[4,1,512]{2,1,0:T(1,128)S(1)} %get-tuple-element.30.left_sq, ...), custom_call_target="tpu_custom_call" | custom-call | flops 3221225472 | bytes 8388608 | tf_op jit(solution)/shard_map/pallas_call | solution.py:173
  76.7 3.7 %collective-permute-done.cols = f32[8,160,128]{2,1,0:T(8,128)S(1)} collective-permute-done((f32[8,160,128]{2,1,0:T(8,128)S(1)}, f32[8,160,128]{2,1,0:T(8,128)S(1)}, u32[]{:S(2)}, u32[]{:S(2)}) %collective-permute-start) | collective-permute-done | bytes 655392 | tf_op jit(solution)/shard_map/ppermute | solution.py:29
  80.4 3.0 %shard_map.71 = (f32[8,32,128]{2,1,0:T(8,128)S(1)}, bf16[2,1024,512]{2,1,0:T(8,128)(2,1)S(1)}, bf16[2,1024,512]{2,1,0:T(8,128)(2,1)S(1)}) custom-call(f32[8,160,128]{2,1,0:T(8,128)S(1)} %collective-permute-done.cols, bf16[4,512,512]{2,1,0:T(8,128)(2,1)S(1)} %get-tuple-element.29.left, f32[4,1,512]{2,1,0:T(1,128)S(1)} %get-tuple-element.30.left_sq, ...), custom_call_target="tpu_custom_call" | custom-call | flops 1610612736 | bytes 4194304 | tf_op jit(solution)/shard_map/pallas_call | solution.py:173
  83.4 0.0 copy-start.1
  83.4 10.7 %collective-permute-start.9 = (f32[8,32,128]{2,1,0:T(8,128)S(1)}, f32[8,32,128]{2,1,0:T(8,128)S(1)}, u32[]{:S(2)}, u32[]{:S(2)}) collective-permute-start(f32[8,32,128]{2,1,0:T(8,128)S(1)} %get-tuple-element.35), channel_id=1, source_target_pairs={{0,8},{8,0},{1,9},{9,1},{2,10},{10,2},{3,11},{11,3},{4,12},{12,4},... | collective-permute-start | bytes 393224 | tf_op jit(solution)/shard_map/ppermute | solution.py:29
  94.1 3.0 %shard_map.70 = (f32[8,32,128]{2,1,0:T(8,128)S(1)}, bf16[2,1024,512]{2,1,0:T(8,128)(2,1)S(1)}, bf16[2,1024,512]{2,1,0:T(8,128)(2,1)S(1)}) custom-call(f32[8,160,128]{2,1,0:T(8,128)S(1)} %collective-permute-done.cols, bf16[4,512,512]{2,1,0:T(8,128)(2,1)S(1)} %get-tuple-element.29.left, f32[4,1,512]{2,1,0:T(1,128)S(1)} %get-tuple-element.30.left_sq, ...), custom_call_target="tpu_custom_call" | custom-call | flops 1610612736 | bytes 4194304 | tf_op jit(solution)/shard_map/pallas_call | solution.py:173
  97.1 0.0 collective-permute-done.9
  97.1 13.9 %all_to_all.30.arrived = f32[8,32,128]{2,1,0:T(8,128)S(1)} all-to-all(f32[8,32,128]{2,1,0:T(8,128)S(1)} %add.6), channel_id=1, replica_groups=mesh['x'=4,'y'=8,'c'=2,'z'=8] {'z'}, dimensions={0} | all-to-all | bytes 262144 | tf_op jit(solution)/shard_map/all_to_all | solution.py:33
  111.1 0.0 copy-done.1
  111.1 0.1 between.1
  111.2 22.2 %all_to_all.31.gathered = f32[32,32,128]{2,1,0:T(8,128)S(1)} all-to-all(f32[32,32,128]{2,1,0:T(8,128)S(1)} %get-tuple-element.36), channel_id=1, replica_groups=mesh['x'=4,'y'=8,'c'=2,'z'=8] {'x','y'}, dimensions={0} | all-to-all | bytes 1048576 | tf_op jit(solution)/shard_map/all_to_all | solution.py:33
  133.4 3.0 %shard_map.73 = f32[8,32,128]{2,1,0:T(8,128)S(1)} custom-call(f32[32,32,128]{2,1,0:T(8,128)S(1)} %all_to_all.31.gathered, bf16[4,1024,512]{2,1,0:T(8,128)(2,1)S(1)} %get-tuple-element.37.refs_0_, bf16[4,1024,512]{2,1,0:T(8,128)(2,1)S(1)} %get-tuple-element.38.refs_1_, bf16[4,1024,512]{2,1,0:T(8,128)(2,1)S(1)} %get-tuple-element.39.refs_2_, ...), custom_call_target="tpu_custom_call" | custom-call | flops 1073741824 | bytes 16777216 | tf_op jit(solution)/shard_map/pallas_call | solution.py:229
  136.3 7.5 %collective-permute-start.10 = (f32[8,32,128]{2,1,0:T(8,128)S(1)}, f32[8,32,128]{2,1,0:T(8,128)S(1)}, u32[]{:S(2)}, u32[]{:S(2)}) collective-permute-start(f32[8,32,128]{2,1,0:T(8,128)S(1)} %shard_map.73), channel_id=1, source_target_pairs={{0,8},{8,0},{1,9},{9,1},{2,10},{10,2},{3,11},{11,3},{4,12},{12,4},... | collective-permute-start | bytes 393224 | tf_op jit(solution)/shard_map/ppermute | solution.py:29
  143.8 3.0 %shard_map.72 = f32[8,32,128]{2,1,0:T(8,128)S(1)} custom-call(f32[32,32,128]{2,1,0:T(8,128)S(1)} %all_to_all.31.gathered, bf16[4,1024,512]{2,1,0:T(8,128)(2,1)S(1)} %get-tuple-element.37.refs_0_, bf16[4,1024,512]{2,1,0:T(8,128)(2,1)S(1)} %get-tuple-element.38.refs_1_, bf16[4,1024,512]{2,1,0:T(8,128)(2,1)S(1)} %get-tuple-element.39.refs_2_, ...), custom_call_target="tpu_custom_call" | custom-call | flops 1073741824 | bytes 16777216 | tf_op jit(solution)/shard_map/pallas_call | solution.py:229
  146.8 0.0 collective-permute-done.10
  146.8 11.9 %all_to_all.32.arrived = f32[8,32,128]{2,1,0:T(8,128)S(1)} all-to-all(f32[8,32,128]{2,1,0:T(8,128)S(1)} %add.7), channel_id=1, replica_groups=mesh['x'=4,'y'=8,'c'=2,'z'=8] {'z'}, dimensions={0} | all-to-all | bytes 262144 | tf_op jit(solution)/shard_map/all_to_all | solution.py:33
  158.7 0.2 settle.1
  158.9 11.4 %all_to_all.33 = f32[16,1,128]{2,1,0:T(1,128)S(1)} all-to-all(f32[16,1,128]{2,1,0:T(1,128)S(1)} %broadcast_in_dim.23), channel_id=1, replica_groups=mesh['x'=4,'y'=8,'c'=2,'z'=8] {'y','c'}, dimensions={0} | all-to-all | bytes 16384 | tf_op jit(solution)/shard_map/all_to_all | solution.py:33
  170.3 11.6 %all_to_all.34.sums = f32[32,1,128]{2,1,0:T(1,128)S(1)} all-to-all(f32[32,1,128]{2,1,0:T(1,128)S(1)} %broadcast_in_dim.24), channel_id=1, replica_groups=mesh['x'=4,'y'=8,'c'=2,'z'=8] {'x','z'}, dimensions={0} | all-to-all | bytes 32768 | tf_op jit(solution)/shard_map/all_to_all | solution.py:33
  181.9 1.0 finish.1
  (13 shorter events, 0.2 us)
Async XLA Ops:
  1.9 0.7 copy-start
  2.6 0.8 copy-start.2
  3.5 0.7 copy-start.3
  5.1 29.9 %collective-permute-start.3 = (f32[128,128]{1,0:T(8,128)S(1)}, f32[128,128]{1,0:T(8,128)S(1)}, u32[]{:S(2)}, u32[]{:S(2)}) collective-permute-start(f32[128,128]{1,0:T(8,128)S(1)} %get-tuple-element.28), channel_id=1, source_target_pairs={{0,4},{1,5},{2,6},{3,7},{4,0},{5,1},{6,2},{7,3},{8,12},{9,13},{10,... | collective-permute-start | bytes 196616 | tf_op jit(solution)/shard_map/ppermute | solution.py:29
  16.6 12.1 %collective-permute-start.2 = (f32[128,128]{1,0:T(8,128)S(1)}, f32[128,128]{1,0:T(8,128)S(1)}, u32[]{:S(2)}, u32[]{:S(2)}) collective-permute-start(f32[128,128]{1,0:T(8,128)S(1)} %get-tuple-element.28), channel_id=1, source_target_pairs={{0,7},{1,0},{2,1},{3,2},{4,3},{5,4},{6,5},{7,6},{8,15},{9,8},{10,9... | collective-permute-start | bytes 196616 | tf_op jit(solution)/shard_map/ppermute | solution.py:29
  18.5 10.2 %collective-permute-start.1 = (f32[128,128]{1,0:T(8,128)S(1)}, f32[128,128]{1,0:T(8,128)S(1)}, u32[]{:S(2)}, u32[]{:S(2)}) collective-permute-start(f32[128,128]{1,0:T(8,128)S(1)} %get-tuple-element.28), channel_id=1, source_target_pairs={{0,1},{1,2},{2,3},{3,4},{4,5},{5,6},{6,7},{7,0},{8,9},{9,10},{10,1... | collective-permute-start | bytes 196616 | tf_op jit(solution)/shard_map/ppermute | solution.py:29
  21.9 26.1 %all-to-all-start = ((f32[8,160,128]{2,1,0:T(8,128)}), f32[8,160,128]{2,1,0:T(8,128)S(1)}, u32[]{:S(2)}, u32[]{:S(2)}) async-start(f32[8,160,128]{2,1,0:T(8,128)} %get-tuple-element.27), calls=%async_computation | async-start | bytes 1310720 | tf_op jit(solution)/shard_map/all_to_all | solution.py:33
  28.8 10.7 %collective-permute-start.5 = (f32[2,128,128]{2,1,0:T(8,128)S(1)}, f32[2,128,128]{2,1,0:T(8,128)S(1)}, u32[]{:S(2)}, u32[]{:S(2)}) collective-permute-start(f32[2,128,128]{2,1,0:T(8,128)S(1)} %get-tuple-element.50), channel_id=1, source_target_pairs={{0,6},{1,7},{2,0},{3,1},{4,2},{5,3},{6,4},{7,5},{8,14},{9,15},{10,... | collective-permute-start | bytes 393224 | tf_op jit(solution)/shard_map/ppermute | solution.py:29
  30.7 8.8 %collective-permute-start.4 = (f32[2,128,128]{2,1,0:T(8,128)S(1)}, f32[2,128,128]{2,1,0:T(8,128)S(1)}, u32[]{:S(2)}, u32[]{:S(2)}) collective-permute-start(f32[2,128,128]{2,1,0:T(8,128)S(1)} %get-tuple-element.51), channel_id=1, source_target_pairs={{0,2},{1,3},{2,4},{3,5},{4,6},{5,7},{6,0},{7,1},{8,10},{9,11},{10,... | collective-permute-start | bytes 393224 | tf_op jit(solution)/shard_map/ppermute | solution.py:29
  39.5 18.4 %collective-permute-start.6 = (f32[8,128,128]{2,1,0:T(8,128)S(1)}, f32[8,128,128]{2,1,0:T(8,128)S(1)}, u32[]{:S(2)}, u32[]{:S(2)}) collective-permute-start(f32[8,128,128]{2,1,0:T(8,128)S(1)} %constant_dynamic-update-slice_fusion.same), channel_id=1, source_target_pairs={{0,8},{8,0},{1,9},{9,1},{2,10},{10,2},{3,11},{11,3},{4,12},{12,4},... | collective-permute-start | bytes 1572872 | tf_op jit(solution)/shard_map/ppermute | solution.py:29
  48.0 17.4 %collective-permute-start.8 = (f32[8,160,128]{2,1,0:T(8,128)S(1)}, f32[8,160,128]{2,1,0:T(8,128)S(1)}, u32[]{:S(2)}, u32[]{:S(2)}) collective-permute-start(f32[8,160,128]{2,1,0:T(8,128)S(1)} %all-to-all-done.cols), channel_id=1, source_target_pairs={{0,128},{128,256},{256,384},{384,0},{1,129},{129,257},{257,385},{3... | collective-permute-start | bytes 1966088 | tf_op jit(solution)/shard_map/ppermute | solution.py:29
  51.1 19.9 %collective-permute-start.7 = (f32[8,160,128]{2,1,0:T(8,128)S(1)}, f32[8,160,128]{2,1,0:T(8,128)S(1)}, u32[]{:S(2)}, u32[]{:S(2)}) collective-permute-start(f32[8,160,128]{2,1,0:T(8,128)S(1)} %all-to-all-done.cols), channel_id=1, source_target_pairs={{0,384},{128,0},{256,128},{384,256},{1,385},{129,1},{257,129},{385... | collective-permute-start | bytes 1966088 | tf_op jit(solution)/shard_map/ppermute | solution.py:29
  54.5 25.9 %collective-permute-start = (f32[8,160,128]{2,1,0:T(8,128)S(1)}, f32[8,160,128]{2,1,0:T(8,128)S(1)}, u32[]{:S(2)}, u32[]{:S(2)}) collective-permute-start(f32[8,160,128]{2,1,0:T(8,128)S(1)} %all-to-all-done.cols), channel_id=1, source_target_pairs={{0,256},{128,384},{256,0},{384,128},{1,257},{129,385},{257,1},{385... | collective-permute-start | bytes 1966088 | tf_op jit(solution)/shard_map/ppermute | solution.py:29
  83.4 27.7 %copy-start.1 = (f32[32,128]{1,0:T(8,128)S(1)}, f32[32,128]{1,0:T(8,128)}, u32[]{:S(2)}) copy-start(f32[32,128]{1,0:T(8,128)} %targets.7) | copy-start | bytes 49156
  83.4 13.7 %collective-permute-start.9 = (f32[8,32,128]{2,1,0:T(8,128)S(1)}, f32[8,32,128]{2,1,0:T(8,128)S(1)}, u32[]{:S(2)}, u32[]{:S(2)}) collective-permute-start(f32[8,32,128]{2,1,0:T(8,128)S(1)} %get-tuple-element.35), channel_id=1, source_target_pairs={{0,8},{8,0},{1,9},{9,1},{2,10},{10,2},{3,11},{11,3},{4,12},{12,4},... | collective-permute-start | bytes 393224 | tf_op jit(solution)/shard_map/ppermute | solution.py:29
  136.3 10.4 %collective-permute-start.10 = (f32[8,32,128]{2,1,0:T(8,128)S(1)}, f32[8,32,128]{2,1,0:T(8,128)S(1)}, u32[]{:S(2)}, u32[]{:S(2)}) collective-permute-start(f32[8,32,128]{2,1,0:T(8,128)S(1)} %shard_map.73), channel_id=1, source_target_pairs={{0,8},{8,0},{1,9},{9,1},{2,10},{10,2},{3,11},{11,3},{4,12},{12,4},... | collective-permute-start | bytes 393224 | tf_op jit(solution)/shard_map/ppermute | solution.py:29

commit v2 on v1

--- a/solution.py
+++ b/solution.py
@@ -46,7 +46,15 @@
     return pl.CostEstimate(flops=flops, bytes_accessed=moved, transcendentals=powers)
 
 
-def spread_kernel(points, lengths, targets, scale, noise, out, own, aux):
+def spread_kernel(points_in, lengths_in, targets_in, scale, noise, out, own, aux, points, lengths, targets, sems):
+    copies = [
+        pltpu.make_async_copy(source, to, sems.at[at])
+        for at, (source, to) in enumerate(((points_in, points), (lengths_in, lengths), (targets_in, targets)))
+    ]
+    for copy in copies:
+        copy.start()
+    for copy in copies:
+        copy.wait()
     scaled = points[...] / jnp.broadcast_to(lengths[...], (BLK, BLK)).T
     vectors = targets[...]
     own[...] = scaled
@@ -59,8 +67,14 @@
 def spread(points, lengths, targets, scale, noise):
     return pl.pallas_call(
         spread_kernel,
-        in_specs=[VMEM, VMEM, VMEM, SMEM, SMEM],
+        in_specs=[pl.BlockSpec(memory_space=pltpu.HBM)] * 3 + [SMEM, SMEM],
         out_specs=[VMEM] * 3,
+        scratch_shapes=[
+            pltpu.VMEM((BLK, BLK), F32),
+            pltpu.VMEM((1, BLK), F32),
+            pltpu.VMEM((RHS, BLK), F32),
+            pltpu.SemaphoreType.DMA((3,)),
+        ],
         out_shape=[
             jax.ShapeDtypeStruct((8, BLK + RHS, BLK), F32),
             jax.ShapeDtypeStruct((BLK, BLK), F32),
@@ -68,7 +82,7 @@
         ],
         compiler_params=PARAMS,
         name="spread",
-    )(points, lengths, targets, scale, noise)
+    )(*[pltpu.with_memory_space_constraint(v, pltpu.HBM) for v in (points, lengths, targets)], scale, noise)
 
 
 ORDER = (0, -1, 1, 4, -3, -2, 2, 3)
@@ -306,7 +320,8 @@
 def on_device(points, targets, lengthscales, outputscale, noise):
     near, own, aux = spread(points, lengthscales[None], targets, outputscale, noise)
     near = exchange(near, "y")
-    behind, ahead, across = shift(near, "x", 1), shift(near, "x", -1), shift(near, "x", 2)
+    behind, ahead = shift(near, "x", 1), shift(near, "x", -1)
+    across = shift(near, "x", 2)
     below, above, far = shift(own, "z", 1), shift(own, "z", -1), shift(own, "z", 4)
     pairs = [shift(jnp.stack([below, own]), "z", 2), shift(jnp.stack([own, above]), "z", -2)]
     same = jnp.concatenate([jnp.stack([own, below, above, far]), *pairs])

time: 184 us -> 182 us (0.989)
  local copies, waits for them, and re-layouts: 2.29 us -> 0.08 us
    unnamed x13 -> x7, local copies, waits for them, and re-layouts: 2.25 us -> 0.04 us
where the time goes in v2:
time: 182 us
  blocking collectives  71 us (39%)
  starting transfers between devices  62.2 us (34%)
  Pallas kernels  32.4 us (18%)
  waiting for transfers between devices  13.7 us (8%)
  between operations  2.17 us (1%)
    all_to_all x5, blocking collectives, exchange(): return lax.all_to_all(x, axes, 0, 0, tiled=True)  71 us
    ppermute x11, starting transfers between devices, shift(): lax.ppermute(value, axis, [(s, (s + steps) % count) for s in range(count)])  55.3 us
    pallas_call x4, Pallas kernels, more_chunk(): pl.pallas_call(functools.partial(more_kernel, tiles), in_specs=[VMEM] * 4...  17.3 us
    ppermute x11, waiting for transfers between devices, shift(): lax.ppermute(value, axis, [(s, (s + steps) % count) for s in range(count)])  9.61 us
    all_to_all x1, starting transfers between devices, exchange(): return lax.all_to_all(x, axes, 0, 0, tiled=True)  6.83 us
    pallas_call x1, Pallas kernels, own_chunk(): pl.pallas_call(own_kernel, in_specs=[SMEM] + [VMEM] * 3, out_specs=[VMEM]...  5.99 us
    pallas_call x2, Pallas kernels, second(): pl.pallas_call(functools.partial(second_kernel, tiles), in_specs=[VMEM] *...  5.95 us
    all_to_all x1, waiting for transfers between devices, exchange(): return lax.all_to_all(x, axes, 0, 0, tiled=True)  4.06 us
  transfers between devices with their start and end apart: 12, of which 4 were waited for; matrix products, arithmetic and copies ran while one was open for 0% of the time, Pallas kernels for 13%

profile of v2, /device:TPU:1, one launch (start us, length us, event | category | flops | bytes accessed | tf_op | source)
XLA Modules:
  0.0 181.5 jit_solution(729582653559992178)
XLA Ops:
  1.9 1.8 %spread.1 = (f32[8,160,128]{2,1,0:T(8,128)}, f32[128,128]{1,0:T(8,128)S(1)}, f32[8,128]{1,0:T(8,128)S(1)}) custom-call(f32[128,128]{1,0:T(8,128)} %points_in.1, f32[1,128]{1,0:T(1,128)} %bitcast.17, f32[32,128]{1,0:T(8,128)} %targets.5, f32[1]{0:T(128)S(6)} %copy.13.scale, f32[1]{0:T(128)S(6)} %copy.14.noise), custom_call_target="tpu_custom_call" | custom-call | tf_op jit(solution)/shard_map/spread/pallas_call | solution.py:68
  3.8 11.5 %collective-permute-start.3 = (f32[128,128]{1,0:T(8,128)S(1)}, f32[128,128]{1,0:T(8,128)S(1)}, u32[]{:S(2)}, u32[]{:S(2)}) collective-permute-start(f32[128,128]{1,0:T(8,128)S(1)} %get-tuple-element.28), channel_id=1, source_target_pairs={{0,4},{1,5},{2,6},{3,7},{4,0},{5,1},{6,2},{7,3},{8,12},{9,13},{10,... | collective-permute-start | bytes 196616 | tf_op jit(solution)/shard_map/ppermute | solution.py:29
  15.2 2.0 %collective-permute-start.2 = (f32[128,128]{1,0:T(8,128)S(1)}, f32[128,128]{1,0:T(8,128)S(1)}, u32[]{:S(2)}, u32[]{:S(2)}) collective-permute-start(f32[128,128]{1,0:T(8,128)S(1)} %get-tuple-element.28), channel_id=1, source_target_pairs={{0,7},{1,0},{2,1},{3,2},{4,3},{5,4},{6,5},{7,6},{8,15},{9,8},{10,9... | collective-permute-start | bytes 196616 | tf_op jit(solution)/shard_map/ppermute | solution.py:29
  17.2 3.3 %collective-permute-start.1 = (f32[128,128]{1,0:T(8,128)S(1)}, f32[128,128]{1,0:T(8,128)S(1)}, u32[]{:S(2)}, u32[]{:S(2)}) collective-permute-start(f32[128,128]{1,0:T(8,128)S(1)} %get-tuple-element.28), channel_id=1, source_target_pairs={{0,1},{1,2},{2,3},{3,4},{4,5},{5,6},{6,7},{7,0},{8,9},{9,10},{10,1... | collective-permute-start | bytes 196616 | tf_op jit(solution)/shard_map/ppermute | solution.py:29
  20.5 6.8 %all-to-all-start = ((f32[8,160,128]{2,1,0:T(8,128)}), f32[8,160,128]{2,1,0:T(8,128)S(1)}, u32[]{:S(2)}, u32[]{:S(2)}) async-start(f32[8,160,128]{2,1,0:T(8,128)} %get-tuple-element.27), calls=%async_computation | async-start | bytes 1310720 | tf_op jit(solution)/shard_map/all_to_all | solution.py:33
  27.4 0.0 collective-permute-done.2
  27.4 0.0 collective-permute-done.1
  27.4 1.9 %collective-permute-start.5 = (f32[2,128,128]{2,1,0:T(8,128)S(1)}, f32[2,128,128]{2,1,0:T(8,128)S(1)}, u32[]{:S(2)}, u32[]{:S(2)}) collective-permute-start(f32[2,128,128]{2,1,0:T(8,128)S(1)} %get-tuple-element.50), channel_id=1, source_target_pairs={{0,6},{1,7},{2,0},{3,1},{4,2},{5,3},{6,4},{7,5},{8,14},{9,15},{10,... | collective-permute-start | bytes 393224 | tf_op jit(solution)/shard_map/ppermute | solution.py:29
  29.4 4.2 %collective-permute-start.4 = (f32[2,128,128]{2,1,0:T(8,128)S(1)}, f32[2,128,128]{2,1,0:T(8,128)S(1)}, u32[]{:S(2)}, u32[]{:S(2)}) collective-permute-start(f32[2,128,128]{2,1,0:T(8,128)S(1)} %get-tuple-element.51), channel_id=1, source_target_pairs={{0,2},{1,3},{2,4},{3,5},{4,6},{5,7},{6,0},{7,1},{8,10},{9,11},{10,... | collective-permute-start | bytes 393224 | tf_op jit(solution)/shard_map/ppermute | solution.py:29
  33.6 0.0 collective-permute-done.3
  33.7 4.5 %collective-permute-done.4 = f32[2,128,128]{2,1,0:T(8,128)S(1)} collective-permute-done((f32[2,128,128]{2,1,0:T(8,128)S(1)}, f32[2,128,128]{2,1,0:T(8,128)S(1)}, u32[]{:S(2)}, u32[]{:S(2)}) %collective-permute-start.4) | collective-permute-done | bytes 131104 | tf_op jit(solution)/shard_map/ppermute | solution.py:29
  38.1 0.0 collective-permute-done.5
  38.2 4.4 %collective-permute-start.6 = (f32[8,128,128]{2,1,0:T(8,128)S(1)}, f32[8,128,128]{2,1,0:T(8,128)S(1)}, u32[]{:S(2)}, u32[]{:S(2)}) collective-permute-start(f32[8,128,128]{2,1,0:T(8,128)S(1)} %constant_dynamic-update-slice_fusion.same), channel_id=1, source_target_pairs={{0,8},{8,0},{1,9},{9,1},{2,10},{10,2},{3,11},{11,3},{4,12},{12,4},... | collective-permute-start | bytes 1572872 | tf_op jit(solution)/shard_map/ppermute | solution.py:29
  42.6 4.1 %all-to-all-done.cols = f32[8,160,128]{2,1,0:T(8,128)S(1)} async-done(((f32[8,160,128]{2,1,0:T(8,128)}), f32[8,160,128]{2,1,0:T(8,128)S(1)}, u32[]{:S(2)}, u32[]{:S(2)}) %all-to-all-start) | async-done | bytes 655392 | tf_op jit(solution)/shard_map/all_to_all | solution.py:33
  46.6 3.1 %collective-permute-start.8 = (f32[8,160,128]{2,1,0:T(8,128)S(1)}, f32[8,160,128]{2,1,0:T(8,128)S(1)}, u32[]{:S(2)}, u32[]{:S(2)}) collective-permute-start(f32[8,160,128]{2,1,0:T(8,128)S(1)} %all-to-all-done.cols), channel_id=1, source_target_pairs={{0,128},{128,256},{256,384},{384,0},{1,129},{129,257},{257,385},{3... | collective-permute-start | bytes 1966088 | tf_op jit(solution)/shard_map/ppermute | solution.py:29
  49.7 3.4 %collective-permute-start.7 = (f32[8,160,128]{2,1,0:T(8,128)S(1)}, f32[8,160,128]{2,1,0:T(8,128)S(1)}, u32[]{:S(2)}, u32[]{:S(2)}) collective-permute-start(f32[8,160,128]{2,1,0:T(8,128)S(1)} %all-to-all-done.cols), channel_id=1, source_target_pairs={{0,384},{128,0},{256,128},{384,256},{1,385},{129,1},{257,129},{385... | collective-permute-start | bytes 1966088 | tf_op jit(solution)/shard_map/ppermute | solution.py:29
  53.1 3.4 %collective-permute-start = (f32[8,160,128]{2,1,0:T(8,128)S(1)}, f32[8,160,128]{2,1,0:T(8,128)S(1)}, u32[]{:S(2)}, u32[]{:S(2)}) collective-permute-start(f32[8,160,128]{2,1,0:T(8,128)S(1)} %all-to-all-done.cols), channel_id=1, source_target_pairs={{0,256},{128,384},{256,0},{384,128},{1,257},{129,385},{257,1},{385... | collective-permute-start | bytes 1966088 | tf_op jit(solution)/shard_map/ppermute | solution.py:29
  56.6 0.0 collective-permute-done.6.other
  56.6 6.0 %own_chunk.1 = (f32[16,32,128]{2,1,0:T(8,128)S(1)}, bf16[4,1024,512]{2,1,0:T(8,128)(2,1)S(1)}, bf16[4,1024,512]{2,1,0:T(8,128)(2,1)S(1)}, bf16[4,512,512]{2,1,0:T(8,128)(2,1)S(1)}, f32[4,1,512]{2,1,0:T(1,128)S(1)}) custom-call(s32[1]{0:T(128)} %bitcast.1.place, f32[8,160,128]{2,1,0:T(8,128)S(1)} %all-to-all-done.cols, ...), custom_call_target="tpu_custom_call" | custom-call | flops 3221225472 | bytes 8388608 | tf_op jit(solution)/shard_map/own_chunk/pallas_call | solution.py:174
  62.6 1.4 collective-permute-done.8.cols
  64.0 5.7 %shard_map.68 = (f32[16,32,128]{2,1,0:T(8,128)S(1)}, bf16[4,1024,512]{2,1,0:T(8,128)(2,1)S(1)}, bf16[4,1024,512]{2,1,0:T(8,128)(2,1)S(1)}) custom-call(f32[8,160,128]{2,1,0:T(8,128)S(1)} %collective-permute-done.8.cols, bf16[4,512,512]{2,1,0:T(8,128)(2,1)S(1)} %get-tuple-element.29.left, f32[4,1,512]{2,1,0:T(1,128)S(1)} %get-tuple-element.30.left_sq, ...), custom_call_target="tpu_custom_call" | custom-call | flops 3221225472 | bytes 8388608 | tf_op jit(solution)/shard_map/pallas_call | solution.py:187
  69.7 0.0 collective-permute-done.7.cols
  69.7 5.6 %shard_map.69 = (f32[16,32,128]{2,1,0:T(8,128)S(1)}, bf16[4,1024,512]{2,1,0:T(8,128)(2,1)S(1)}, bf16[4,1024,512]{2,1,0:T(8,128)(2,1)S(1)}) custom-call(f32[8,160,128]{2,1,0:T(8,128)S(1)} %collective-permute-done.7.cols, bf16[4,512,512]{2,1,0:T(8,128)(2,1)S(1)} %get-tuple-element.29.left, f32[4,1,512]{2,1,0:T(1,128)S(1)} %get-tuple-element.30.left_sq, ...), custom_call_target="tpu_custom_call" | custom-call | flops 3221225472 | bytes 8388608 | tf_op jit(solution)/shard_map/pallas_call | solution.py:187
  75.3 3.7 %collective-permute-done.cols = f32[8,160,128]{2,1,0:T(8,128)S(1)} collective-permute-done((f32[8,160,128]{2,1,0:T(8,128)S(1)}, f32[8,160,128]{2,1,0:T(8,128)S(1)}, u32[]{:S(2)}, u32[]{:S(2)}) %collective-permute-start) | collective-permute-done | bytes 655392 | tf_op jit(solution)/shard_map/ppermute | solution.py:29
  79.0 3.0 %shard_map.71 = (f32[8,32,128]{2,1,0:T(8,128)S(1)}, bf16[2,1024,512]{2,1,0:T(8,128)(2,1)S(1)}, bf16[2,1024,512]{2,1,0:T(8,128)(2,1)S(1)}) custom-call(f32[8,160,128]{2,1,0:T(8,128)S(1)} %collective-permute-done.cols, bf16[4,512,512]{2,1,0:T(8,128)(2,1)S(1)} %get-tuple-element.29.left, f32[4,1,512]{2,1,0:T(1,128)S(1)} %get-tuple-element.30.left_sq, ...), custom_call_target="tpu_custom_call" | custom-call | flops 1610612736 | bytes 4194304 | tf_op jit(solution)/shard_map/pallas_call | solution.py:187
  82.1 0.0 copy-start
  82.1 10.7 %collective-permute-start.9 = (f32[8,32,128]{2,1,0:T(8,128)S(1)}, f32[8,32,128]{2,1,0:T(8,128)S(1)}, u32[]{:S(2)}, u32[]{:S(2)}) collective-permute-start(f32[8,32,128]{2,1,0:T(8,128)S(1)} %get-tuple-element.35), channel_id=1, source_target_pairs={{0,8},{8,0},{1,9},{9,1},{2,10},{10,2},{3,11},{11,3},{4,12},{12,4},... | collective-permute-start | bytes 393224 | tf_op jit(solution)/shard_map/ppermute | solution.py:29
  92.7 3.0 %shard_map.70 = (f32[8,32,128]{2,1,0:T(8,128)S(1)}, bf16[2,1024,512]{2,1,0:T(8,128)(2,1)S(1)}, bf16[2,1024,512]{2,1,0:T(8,128)(2,1)S(1)}) custom-call(f32[8,160,128]{2,1,0:T(8,128)S(1)} %collective-permute-done.cols, bf16[4,512,512]{2,1,0:T(8,128)(2,1)S(1)} %get-tuple-element.29.left, f32[4,1,512]{2,1,0:T(1,128)S(1)} %get-tuple-element.30.left_sq, ...), custom_call_target="tpu_custom_call" | custom-call | flops 1610612736 | bytes 4194304 | tf_op jit(solution)/shard_map/pallas_call | solution.py:187
  95.8 0.0 collective-permute-done.9
  95.8 13.9 %all_to_all.30.arrived = f32[8,32,128]{2,1,0:T(8,128)S(1)} all-to-all(f32[8,32,128]{2,1,0:T(8,128)S(1)} %add.6), channel_id=1, replica_groups=mesh['x'=4,'y'=8,'c'=2,'z'=8] {'z'}, dimensions={0} | all-to-all | bytes 262144 | tf_op jit(solution)/shard_map/all_to_all | solution.py:33
  109.7 0.0 copy-done
  109.7 0.1 between.1
  109.8 22.2 %all_to_all.31.gathered = f32[32,32,128]{2,1,0:T(8,128)S(1)} all-to-all(f32[32,32,128]{2,1,0:T(8,128)S(1)} %get-tuple-element.36), channel_id=1, replica_groups=mesh['x'=4,'y'=8,'c'=2,'z'=8] {'x','y'}, dimensions={0} | all-to-all | bytes 1048576 | tf_op jit(solution)/shard_map/all_to_all | solution.py:33
  132.0 3.0 %shard_map.73 = f32[8,32,128]{2,1,0:T(8,128)S(1)} custom-call(f32[32,32,128]{2,1,0:T(8,128)S(1)} %all_to_all.31.gathered, bf16[4,1024,512]{2,1,0:T(8,128)(2,1)S(1)} %get-tuple-element.37.refs_0_, bf16[4,1024,512]{2,1,0:T(8,128)(2,1)S(1)} %get-tuple-element.38.refs_1_, bf16[4,1024,512]{2,1,0:T(8,128)(2,1)S(1)} %get-tuple-element.39.refs_2_, ...), custom_call_target="tpu_custom_call" | custom-call | flops 1073741824 | bytes 16777216 | tf_op jit(solution)/shard_map/pallas_call | solution.py:243
  135.0 7.5 %collective-permute-start.10 = (f32[8,32,128]{2,1,0:T(8,128)S(1)}, f32[8,32,128]{2,1,0:T(8,128)S(1)}, u32[]{:S(2)}, u32[]{:S(2)}) collective-permute-start(f32[8,32,128]{2,1,0:T(8,128)S(1)} %shard_map.73), channel_id=1, source_target_pairs={{0,8},{8,0},{1,9},{9,1},{2,10},{10,2},{3,11},{11,3},{4,12},{12,4},... | collective-permute-start | bytes 393224 | tf_op jit(solution)/shard_map/ppermute | solution.py:29
  142.4 3.0 %shard_map.72 = f32[8,32,128]{2,1,0:T(8,128)S(1)} custom-call(f32[32,32,128]{2,1,0:T(8,128)S(1)} %all_to_all.31.gathered, bf16[4,1024,512]{2,1,0:T(8,128)(2,1)S(1)} %get-tuple-element.37.refs_0_, bf16[4,1024,512]{2,1,0:T(8,128)(2,1)S(1)} %get-tuple-element.38.refs_1_, bf16[4,1024,512]{2,1,0:T(8,128)(2,1)S(1)} %get-tuple-element.39.refs_2_, ...), custom_call_target="tpu_custom_call" | custom-call | flops 1073741824 | bytes 16777216 | tf_op jit(solution)/shard_map/pallas_call | solution.py:243
  145.4 0.0 collective-permute-done.10
  145.4 11.9 %all_to_all.32.arrived = f32[8,32,128]{2,1,0:T(8,128)S(1)} all-to-all(f32[8,32,128]{2,1,0:T(8,128)S(1)} %add.7), channel_id=1, replica_groups=mesh['x'=4,'y'=8,'c'=2,'z'=8] {'z'}, dimensions={0} | all-to-all | bytes 262144 | tf_op jit(solution)/shard_map/all_to_all | solution.py:33
  157.3 0.2 settle.1
  157.6 11.4 %all_to_all.33 = f32[16,1,128]{2,1,0:T(1,128)S(1)} all-to-all(f32[16,1,128]{2,1,0:T(1,128)S(1)} %broadcast_in_dim.23), channel_id=1, replica_groups=mesh['x'=4,'y'=8,'c'=2,'z'=8] {'y','c'}, dimensions={0} | all-to-all | bytes 16384 | tf_op jit(solution)/shard_map/all_to_all | solution.py:33
  169.0 11.6 %all_to_all.34.sums = f32[32,1,128]{2,1,0:T(1,128)S(1)} all-to-all(f32[32,1,128]{2,1,0:T(1,128)S(1)} %broadcast_in_dim.24), channel_id=1, replica_groups=mesh['x'=4,'y'=8,'c'=2,'z'=8] {'x','z'}, dimensions={0} | all-to-all | bytes 32768 | tf_op jit(solution)/shard_map/all_to_all | solution.py:33
  180.6 1.0 finish.1
  (13 shorter events, 0.2 us)
Async XLA Ops:
  3.8 29.9 %collective-permute-start.3 = (f32[128,128]{1,0:T(8,128)S(1)}, f32[128,128]{1,0:T(8,128)S(1)}, u32[]{:S(2)}, u32[]{:S(2)}) collective-permute-start(f32[128,128]{1,0:T(8,128)S(1)} %get-tuple-element.28), channel_id=1, source_target_pairs={{0,4},{1,5},{2,6},{3,7},{4,0},{5,1},{6,2},{7,3},{8,12},{9,13},{10,... | collective-permute-start | bytes 196616 | tf_op jit(solution)/shard_map/ppermute | solution.py:29
  15.2 12.1 %collective-permute-start.2 = (f32[128,128]{1,0:T(8,128)S(1)}, f32[128,128]{1,0:T(8,128)S(1)}, u32[]{:S(2)}, u32[]{:S(2)}) collective-permute-start(f32[128,128]{1,0:T(8,128)S(1)} %get-tuple-element.28), channel_id=1, source_target_pairs={{0,7},{1,0},{2,1},{3,2},{4,3},{5,4},{6,5},{7,6},{8,15},{9,8},{10,9... | collective-permute-start | bytes 196616 | tf_op jit(solution)/shard_map/ppermute | solution.py:29
  17.2 10.2 %collective-permute-start.1 = (f32[128,128]{1,0:T(8,128)S(1)}, f32[128,128]{1,0:T(8,128)S(1)}, u32[]{:S(2)}, u32[]{:S(2)}) collective-permute-start(f32[128,128]{1,0:T(8,128)S(1)} %get-tuple-element.28), channel_id=1, source_target_pairs={{0,1},{1,2},{2,3},{3,4},{4,5},{5,6},{6,7},{7,0},{8,9},{9,10},{10,1... | collective-permute-start | bytes 196616 | tf_op jit(solution)/shard_map/ppermute | solution.py:29
  20.5 26.1 %all-to-all-start = ((f32[8,160,128]{2,1,0:T(8,128)}), f32[8,160,128]{2,1,0:T(8,128)S(1)}, u32[]{:S(2)}, u32[]{:S(2)}) async-start(f32[8,160,128]{2,1,0:T(8,128)} %get-tuple-element.27), calls=%async_computation | async-start | bytes 1310720 | tf_op jit(solution)/shard_map/all_to_all | solution.py:33
  27.4 10.7 %collective-permute-start.5 = (f32[2,128,128]{2,1,0:T(8,128)S(1)}, f32[2,128,128]{2,1,0:T(8,128)S(1)}, u32[]{:S(2)}, u32[]{:S(2)}) collective-permute-start(f32[2,128,128]{2,1,0:T(8,128)S(1)} %get-tuple-element.50), channel_id=1, source_target_pairs={{0,6},{1,7},{2,0},{3,1},{4,2},{5,3},{6,4},{7,5},{8,14},{9,15},{10,... | collective-permute-start | bytes 393224 | tf_op jit(solution)/shard_map/ppermute | solution.py:29
  29.4 8.8 %collective-permute-start.4 = (f32[2,128,128]{2,1,0:T(8,128)S(1)}, f32[2,128,128]{2,1,0:T(8,128)S(1)}, u32[]{:S(2)}, u32[]{:S(2)}) collective-permute-start(f32[2,128,128]{2,1,0:T(8,128)S(1)} %get-tuple-element.51), channel_id=1, source_target_pairs={{0,2},{1,3},{2,4},{3,5},{4,6},{5,7},{6,0},{7,1},{8,10},{9,11},{10,... | collective-permute-start | bytes 393224 | tf_op jit(solution)/shard_map/ppermute | solution.py:29
  38.2 18.4 %collective-permute-start.6 = (f32[8,128,128]{2,1,0:T(8,128)S(1)}, f32[8,128,128]{2,1,0:T(8,128)S(1)}, u32[]{:S(2)}, u32[]{:S(2)}) collective-permute-start(f32[8,128,128]{2,1,0:T(8,128)S(1)} %constant_dynamic-update-slice_fusion.same), channel_id=1, source_target_pairs={{0,8},{8,0},{1,9},{9,1},{2,10},{10,2},{3,11},{11,3},{4,12},{12,4},... | collective-permute-start | bytes 1572872 | tf_op jit(solution)/shard_map/ppermute | solution.py:29
  46.6 17.4 %collective-permute-start.8 = (f32[8,160,128]{2,1,0:T(8,128)S(1)}, f32[8,160,128]{2,1,0:T(8,128)S(1)}, u32[]{:S(2)}, u32[]{:S(2)}) collective-permute-start(f32[8,160,128]{2,1,0:T(8,128)S(1)} %all-to-all-done.cols), channel_id=1, source_target_pairs={{0,128},{128,256},{256,384},{384,0},{1,129},{129,257},{257,385},{3... | collective-permute-start | bytes 1966088 | tf_op jit(solution)/shard_map/ppermute | solution.py:29
  49.7 19.9 %collective-permute-start.7 = (f32[8,160,128]{2,1,0:T(8,128)S(1)}, f32[8,160,128]{2,1,0:T(8,128)S(1)}, u32[]{:S(2)}, u32[]{:S(2)}) collective-permute-start(f32[8,160,128]{2,1,0:T(8,128)S(1)} %all-to-all-done.cols), channel_id=1, source_target_pairs={{0,384},{128,0},{256,128},{384,256},{1,385},{129,1},{257,129},{385... | collective-permute-start | bytes 1966088 | tf_op jit(solution)/shard_map/ppermute | solution.py:29
  53.1 25.9 %collective-permute-start = (f32[8,160,128]{2,1,0:T(8,128)S(1)}, f32[8,160,128]{2,1,0:T(8,128)S(1)}, u32[]{:S(2)}, u32[]{:S(2)}) collective-permute-start(f32[8,160,128]{2,1,0:T(8,128)S(1)} %all-to-all-done.cols), channel_id=1, source_target_pairs={{0,256},{128,384},{256,0},{384,128},{1,257},{129,385},{257,1},{385... | collective-permute-start | bytes 1966088 | tf_op jit(solution)/shard_map/ppermute | solution.py:29
  82.1 27.7 %copy-start = (f32[32,128]{1,0:T(8,128)S(1)}, f32[32,128]{1,0:T(8,128)}, u32[]{:S(2)}) copy-start(f32[32,128]{1,0:T(8,128)} %targets.5) | copy-start | bytes 49156
  82.1 13.7 %collective-permute-start.9 = (f32[8,32,128]{2,1,0:T(8,128)S(1)}, f32[8,32,128]{2,1,0:T(8,128)S(1)}, u32[]{:S(2)}, u32[]{:S(2)}) collective-permute-start(f32[8,32,128]{2,1,0:T(8,128)S(1)} %get-tuple-element.35), channel_id=1, source_target_pairs={{0,8},{8,0},{1,9},{9,1},{2,10},{10,2},{3,11},{11,3},{4,12},{12,4},... | collective-permute-start | bytes 393224 | tf_op jit(solution)/shard_map/ppermute | solution.py:29
  135.0 10.4 %collective-permute-start.10 = (f32[8,32,128]{2,1,0:T(8,128)S(1)}, f32[8,32,128]{2,1,0:T(8,128)S(1)}, u32[]{:S(2)}, u32[]{:S(2)}) collective-permute-start(f32[8,32,128]{2,1,0:T(8,128)S(1)} %shard_map.73), channel_id=1, source_target_pairs={{0,8},{8,0},{1,9},{9,1},{2,10},{10,2},{3,11},{11,3},{4,12},{12,4},... | collective-permute-start | bytes 393224 | tf_op jit(solution)/shard_map/ppermute | solution.py:29

commit v3 on v2

--- a/solution.py
+++ b/solution.py
@@ -88,11 +88,12 @@
 ORDER = (0, -1, 1, 4, -3, -2, 2, 3)
 
 
-def prepare_rows(place, row_refs, left, left_sq):
+def prepare_rows(row_refs, left, left_sq):
+    place = lax.axis_index("z")
     for block in range(16):
         value = row_refs[block // 8][block % 8] * ROOT
         high, low = halves(value)
-        z = lax.rem(place[0] + (ORDER[block % 8] + 8), 8)
+        z = lax.rem(place + (ORDER[block % 8] + 8), 8)
         at = block // 8 * 2 + lax.div(z, 4)
         lanes = pl.ds(pl.multiple_of(lax.rem(z, 4) * BLK, BLK), BLK)
         left[at, pl.ds(0, 128), lanes] = high
@@ -142,9 +143,12 @@
     lax.fori_loop(0, len(tiles), one, 0)
 
 
-def own_kernel(place, cols, same, other, out, high, low, left, left_sq, right, right_sq, vecs):
-    prepare_rows(place, (same, other), left, left_sq)
+def cols_kernel(cols, right, right_sq, vecs):
     prepare_cols((cols,), right, right_sq, vecs)
+
+
+def own_kernel(same, other, right, right_sq, vecs, out, high, low, left, left_sq):
+    prepare_rows((same, other), left, left_sq)
     make_values(ALL, left, left_sq, right, right_sq, vecs, high, low, out, None)
 
 
@@ -170,17 +174,28 @@
 RIGHT = [pltpu.VMEM((WIDE, 512), BF16), pltpu.VMEM((WIDE, 1), F32), pltpu.VMEM((2 * RHS, WIDE), BF16)]
 
 
-def own_chunk(place, cols, same, other):
+def own_cols(cols):
+    return pl.pallas_call(
+        cols_kernel,
+        in_specs=[VMEM],
+        out_specs=[VMEM] * 3,
+        out_shape=RIGHT,
+        compiler_params=PARAMS,
+        cost_estimate=cost(0, 2 << 20, 0),
+        name="own_cols",
+    )(cols)
+
+
+def own_chunk(same, other, cols):
     return pl.pallas_call(
         own_kernel,
-        in_specs=[SMEM] + [VMEM] * 3,
+        in_specs=[VMEM] * 5,
         out_specs=[VMEM] * 5,
         out_shape=[*made(ALL), *LEFT],
-        scratch_shapes=RIGHT,
         compiler_params=PARAMS,
         cost_estimate=made_cost(ALL),
         name="own_chunk",
-    )(place, cols, same, other)
+    )(same, other, *[kept(v) for v in cols])
 
 
 def more_chunk(tiles, cols, left, left_sq, before):
@@ -322,12 +337,12 @@
     near = exchange(near, "y")
     behind, ahead = shift(near, "x", 1), shift(near, "x", -1)
     across = shift(near, "x", 2)
+    prepared = own_cols(near)
     below, above, far = shift(own, "z", 1), shift(own, "z", -1), shift(own, "z", 4)
     pairs = [shift(jnp.stack([below, own]), "z", 2), shift(jnp.stack([own, above]), "z", -2)]
     same = jnp.concatenate([jnp.stack([own, below, above, far]), *pairs])
     other = shift(same, "c", 1)
-    place = lax.axis_index("z").astype(jnp.int32)[None]
-    pieces, high, low, left, left_sq = own_chunk(place, near, same, other)
+    pieces, high, low, left, left_sq = own_chunk(same, other, prepared)
     highs, lows = [high], [low]
     for cols in (behind, ahead):
         pieces, high, low = more_chunk(ALL, cols, left, left_sq, pieces)

time: 182 us -> 182 us (level)
    pallas_call x1 -> x2, Pallas kernels: 5.99 us -> 6 us  [the longest x1 5.6 us: own_chunk(): pl.pallas_call(own_kernel, in_specs=[VMEM] * 5, out_specs=[VMEM] * 5, out...]
where the time goes in v3:
time: 182 us
  blocking collectives  71 us (39%)
  starting transfers between devices  62.2 us (34%)
  Pallas kernels  32.4 us (18%)
  waiting for transfers between devices  13.7 us (8%)
  between operations  2.17 us (1%)
    all_to_all x5, blocking collectives, exchange(): return lax.all_to_all(x, axes, 0, 0, tiled=True)  71 us
    ppermute x11, starting transfers between devices, shift(): lax.ppermute(value, axis, [(s, (s + steps) % count) for s in range(count)])  55.4 us
    pallas_call x4, Pallas kernels, more_chunk(): pl.pallas_call(functools.partial(more_kernel, tiles), in_specs=[VMEM] * 4...  17.4 us
    ppermute x11, waiting for transfers between devices, shift(): lax.ppermute(value, axis, [(s, (s + steps) % count) for s in range(count)])  9.6 us
    all_to_all x1, starting transfers between devices, exchange(): return lax.all_to_all(x, axes, 0, 0, tiled=True)  6.83 us
    pallas_call x2, Pallas kernels, second(): pl.pallas_call(functools.partial(second_kernel, tiles), in_specs=[VMEM] *...  5.95 us
    pallas_call x1, Pallas kernels, own_chunk(): pl.pallas_call(own_kernel, in_specs=[VMEM] * 5, out_specs=[VMEM] * 5, out...  5.6 us
    all_to_all x1, waiting for transfers between devices, exchange(): return lax.all_to_all(x, axes, 0, 0, tiled=True)  4.06 us
  transfers between devices with their start and end apart: 12, of which 4 were waited for; matrix products, arithmetic and copies ran while one was open for 0% of the time, Pallas kernels for 13%

profile of v3, /device:TPU:1, one launch (start us, length us, event | category | flops | bytes accessed | tf_op | source)
XLA Modules:
  0.0 181.6 jit_solution(3807570555171635087)
XLA Ops:
  1.9 1.9 %spread.1 = (f32[8,160,128]{2,1,0:T(8,128)}, f32[128,128]{1,0:T(8,128)S(1)}, f32[8,128]{1,0:T(8,128)S(1)}) custom-call(f32[128,128]{1,0:T(8,128)} %points_in.1, f32[1,128]{1,0:T(1,128)} %bitcast.16, f32[32,128]{1,0:T(8,128)} %targets.5, f32[1]{0:T(128)S(6)} %copy.13.scale, f32[1]{0:T(128)S(6)} %copy.14.noise), custom_call_target="tpu_custom_call" | custom-call | tf_op jit(solution)/shard_map/spread/pallas_call | solution.py:68
  3.8 11.5 %collective-permute-start.3 = (f32[128,128]{1,0:T(8,128)S(1)}, f32[128,128]{1,0:T(8,128)S(1)}, u32[]{:S(2)}, u32[]{:S(2)}) collective-permute-start(f32[128,128]{1,0:T(8,128)S(1)} %get-tuple-element.31), channel_id=1, source_target_pairs={{0,4},{1,5},{2,6},{3,7},{4,0},{5,1},{6,2},{7,3},{8,12},{9,13},{10,... | collective-permute-start | bytes 196616 | tf_op jit(solution)/shard_map/ppermute | solution.py:29
  15.2 2.0 %collective-permute-start.2 = (f32[128,128]{1,0:T(8,128)S(1)}, f32[128,128]{1,0:T(8,128)S(1)}, u32[]{:S(2)}, u32[]{:S(2)}) collective-permute-start(f32[128,128]{1,0:T(8,128)S(1)} %get-tuple-element.31), channel_id=1, source_target_pairs={{0,7},{1,0},{2,1},{3,2},{4,3},{5,4},{6,5},{7,6},{8,15},{9,8},{10,9... | collective-permute-start | bytes 196616 | tf_op jit(solution)/shard_map/ppermute | solution.py:29
  17.2 3.3 %collective-permute-start.1 = (f32[128,128]{1,0:T(8,128)S(1)}, f32[128,128]{1,0:T(8,128)S(1)}, u32[]{:S(2)}, u32[]{:S(2)}) collective-permute-start(f32[128,128]{1,0:T(8,128)S(1)} %get-tuple-element.31), channel_id=1, source_target_pairs={{0,1},{1,2},{2,3},{3,4},{4,5},{5,6},{6,7},{7,0},{8,9},{9,10},{10,1... | collective-permute-start | bytes 196616 | tf_op jit(solution)/shard_map/ppermute | solution.py:29
  20.5 6.8 %all-to-all-start = ((f32[8,160,128]{2,1,0:T(8,128)}), f32[8,160,128]{2,1,0:T(8,128)S(1)}, u32[]{:S(2)}, u32[]{:S(2)}) async-start(f32[8,160,128]{2,1,0:T(8,128)} %get-tuple-element.30), calls=%async_computation | async-start | bytes 1310720 | tf_op jit(solution)/shard_map/all_to_all | solution.py:33
  27.4 0.0 collective-permute-done.2
  27.4 0.0 collective-permute-done.1
  27.4 1.9 %collective-permute-start.5 = (f32[2,128,128]{2,1,0:T(8,128)S(1)}, f32[2,128,128]{2,1,0:T(8,128)S(1)}, u32[]{:S(2)}, u32[]{:S(2)}) collective-permute-start(f32[2,128,128]{2,1,0:T(8,128)S(1)} %get-tuple-element.56), channel_id=1, source_target_pairs={{0,6},{1,7},{2,0},{3,1},{4,2},{5,3},{6,4},{7,5},{8,14},{9,15},{10,... | collective-permute-start | bytes 393224 | tf_op jit(solution)/shard_map/ppermute | solution.py:29
  29.4 4.2 %collective-permute-start.4 = (f32[2,128,128]{2,1,0:T(8,128)S(1)}, f32[2,128,128]{2,1,0:T(8,128)S(1)}, u32[]{:S(2)}, u32[]{:S(2)}) collective-permute-start(f32[2,128,128]{2,1,0:T(8,128)S(1)} %get-tuple-element.57), channel_id=1, source_target_pairs={{0,2},{1,3},{2,4},{3,5},{4,6},{5,7},{6,0},{7,1},{8,10},{9,11},{10,... | collective-permute-start | bytes 393224 | tf_op jit(solution)/shard_map/ppermute | solution.py:29
  33.7 0.0 collective-permute-done.3
  33.7 4.5 %collective-permute-done.4 = f32[2,128,128]{2,1,0:T(8,128)S(1)} collective-permute-done((f32[2,128,128]{2,1,0:T(8,128)S(1)}, f32[2,128,128]{2,1,0:T(8,128)S(1)}, u32[]{:S(2)}, u32[]{:S(2)}) %collective-permute-start.4) | collective-permute-done | bytes 131104 | tf_op jit(solution)/shard_map/ppermute | solution.py:29
  38.2 0.0 collective-permute-done.5
  38.2 4.4 %collective-permute-start.6 = (f32[8,128,128]{2,1,0:T(8,128)S(1)}, f32[8,128,128]{2,1,0:T(8,128)S(1)}, u32[]{:S(2)}, u32[]{:S(2)}) collective-permute-start(f32[8,128,128]{2,1,0:T(8,128)S(1)} %constant_dynamic-update-slice_fusion.same), channel_id=1, source_target_pairs={{0,8},{8,0},{1,9},{9,1},{2,10},{10,2},{3,11},{11,3},{4,12},{12,4},... | collective-permute-start | bytes 1572872 | tf_op jit(solution)/shard_map/ppermute | solution.py:29
  42.6 4.1 %all-to-all-done.cols = f32[8,160,128]{2,1,0:T(8,128)S(1)} async-done(((f32[8,160,128]{2,1,0:T(8,128)}), f32[8,160,128]{2,1,0:T(8,128)S(1)}, u32[]{:S(2)}, u32[]{:S(2)}) %all-to-all-start) | async-done | bytes 655392 | tf_op jit(solution)/shard_map/all_to_all | solution.py:33
  46.6 3.1 %collective-permute-start.8 = (f32[8,160,128]{2,1,0:T(8,128)S(1)}, f32[8,160,128]{2,1,0:T(8,128)S(1)}, u32[]{:S(2)}, u32[]{:S(2)}) collective-permute-start(f32[8,160,128]{2,1,0:T(8,128)S(1)} %all-to-all-done.cols), channel_id=1, source_target_pairs={{0,128},{128,256},{256,384},{384,0},{1,129},{129,257},{257,385},{3... | collective-permute-start | bytes 1966088 | tf_op jit(solution)/shard_map/ppermute | solution.py:29
  49.7 3.4 %collective-permute-start.7 = (f32[8,160,128]{2,1,0:T(8,128)S(1)}, f32[8,160,128]{2,1,0:T(8,128)S(1)}, u32[]{:S(2)}, u32[]{:S(2)}) collective-permute-start(f32[8,160,128]{2,1,0:T(8,128)S(1)} %all-to-all-done.cols), channel_id=1, source_target_pairs={{0,384},{128,0},{256,128},{384,256},{1,385},{129,1},{257,129},{385... | collective-permute-start | bytes 1966088 | tf_op jit(solution)/shard_map/ppermute | solution.py:29
  53.1 3.4 %collective-permute-start = (f32[8,160,128]{2,1,0:T(8,128)S(1)}, f32[8,160,128]{2,1,0:T(8,128)S(1)}, u32[]{:S(2)}, u32[]{:S(2)}) collective-permute-start(f32[8,160,128]{2,1,0:T(8,128)S(1)} %all-to-all-done.cols), channel_id=1, source_target_pairs={{0,256},{128,384},{256,0},{384,128},{1,257},{129,385},{257,1},{385... | collective-permute-start | bytes 1966088 | tf_op jit(solution)/shard_map/ppermute | solution.py:29
  56.6 0.4 own_cols.1
  57.0 0.0 collective-permute-done.6.other
  57.0 5.6 %own_chunk.1 = (f32[16,32,128]{2,1,0:T(8,128)S(1)}, bf16[4,1024,512]{2,1,0:T(8,128)(2,1)S(1)}, bf16[4,1024,512]{2,1,0:T(8,128)(2,1)S(1)}, bf16[4,512,512]{2,1,0:T(8,128)(2,1)S(1)}, f32[4,1,512]{2,1,0:T(1,128)S(1)}) custom-call(f32[8,128,128]{2,1,0:T(8,128)S(1)} %constant_dynamic-update-slice_fusion.same, f32[8,128,128]{2,1,0:T(8,128)S(1)} %collective-permute-done.6.other, ...), custom_call_target="tpu_custom_call" | custom-call | flops 3221225472 | bytes 8388608 | tf_op jit(solution)/shard_map/own_chunk/pallas_call | solution.py:190
  62.6 1.4 collective-permute-done.8.cols
  64.0 5.6 %shard_map.68 = (f32[16,32,128]{2,1,0:T(8,128)S(1)}, bf16[4,1024,512]{2,1,0:T(8,128)(2,1)S(1)}, bf16[4,1024,512]{2,1,0:T(8,128)(2,1)S(1)}) custom-call(f32[8,160,128]{2,1,0:T(8,128)S(1)} %collective-permute-done.8.cols, bf16[4,512,512]{2,1,0:T(8,128)(2,1)S(1)} %get-tuple-element.35.left, f32[4,1,512]{2,1,0:T(1,128)S(1)} %get-tuple-element.36.left_sq, ...), custom_call_target="tpu_custom_call" | custom-call | flops 3221225472 | bytes 8388608 | tf_op jit(solution)/shard_map/pallas_call | solution.py:202
  69.7 0.0 collective-permute-done.7.cols
  69.7 5.7 %shard_map.69 = (f32[16,32,128]{2,1,0:T(8,128)S(1)}, bf16[4,1024,512]{2,1,0:T(8,128)(2,1)S(1)}, bf16[4,1024,512]{2,1,0:T(8,128)(2,1)S(1)}) custom-call(f32[8,160,128]{2,1,0:T(8,128)S(1)} %collective-permute-done.7.cols, bf16[4,512,512]{2,1,0:T(8,128)(2,1)S(1)} %get-tuple-element.35.left, f32[4,1,512]{2,1,0:T(1,128)S(1)} %get-tuple-element.36.left_sq, ...), custom_call_target="tpu_custom_call" | custom-call | flops 3221225472 | bytes 8388608 | tf_op jit(solution)/shard_map/pallas_call | solution.py:202
  75.3 3.7 %collective-permute-done.cols = f32[8,160,128]{2,1,0:T(8,128)S(1)} collective-permute-done((f32[8,160,128]{2,1,0:T(8,128)S(1)}, f32[8,160,128]{2,1,0:T(8,128)S(1)}, u32[]{:S(2)}, u32[]{:S(2)}) %collective-permute-start) | collective-permute-done | bytes 655392 | tf_op jit(solution)/shard_map/ppermute | solution.py:29
  79.0 3.0 %shard_map.71 = (f32[8,32,128]{2,1,0:T(8,128)S(1)}, bf16[2,1024,512]{2,1,0:T(8,128)(2,1)S(1)}, bf16[2,1024,512]{2,1,0:T(8,128)(2,1)S(1)}) custom-call(f32[8,160,128]{2,1,0:T(8,128)S(1)} %collective-permute-done.cols, bf16[4,512,512]{2,1,0:T(8,128)(2,1)S(1)} %get-tuple-element.35.left, f32[4,1,512]{2,1,0:T(1,128)S(1)} %get-tuple-element.36.left_sq, ...), custom_call_target="tpu_custom_call" | custom-call | flops 1610612736 | bytes 4194304 | tf_op jit(solution)/shard_map/pallas_call | solution.py:202
  82.1 0.0 copy-start
  82.1 10.7 %collective-permute-start.9 = (f32[8,32,128]{2,1,0:T(8,128)S(1)}, f32[8,32,128]{2,1,0:T(8,128)S(1)}, u32[]{:S(2)}, u32[]{:S(2)}) collective-permute-start(f32[8,32,128]{2,1,0:T(8,128)S(1)} %get-tuple-element.41), channel_id=1, source_target_pairs={{0,8},{8,0},{1,9},{9,1},{2,10},{10,2},{3,11},{11,3},{4,12},{12,4},... | collective-permute-start | bytes 393224 | tf_op jit(solution)/shard_map/ppermute | solution.py:29
  92.8 3.0 %shard_map.70 = (f32[8,32,128]{2,1,0:T(8,128)S(1)}, bf16[2,1024,512]{2,1,0:T(8,128)(2,1)S(1)}, bf16[2,1024,512]{2,1,0:T(8,128)(2,1)S(1)}) custom-call(f32[8,160,128]{2,1,0:T(8,128)S(1)} %collective-permute-done.cols, bf16[4,512,512]{2,1,0:T(8,128)(2,1)S(1)} %get-tuple-element.35.left, f32[4,1,512]{2,1,0:T(1,128)S(1)} %get-tuple-element.36.left_sq, ...), custom_call_target="tpu_custom_call" | custom-call | flops 1610612736 | bytes 4194304 | tf_op jit(solution)/shard_map/pallas_call | solution.py:202
  95.8 0.0 collective-permute-done.9
  95.8 13.9 %all_to_all.30.arrived = f32[8,32,128]{2,1,0:T(8,128)S(1)} all-to-all(f32[8,32,128]{2,1,0:T(8,128)S(1)} %add.6), channel_id=1, replica_groups=mesh['x'=4,'y'=8,'c'=2,'z'=8] {'z'}, dimensions={0} | all-to-all | bytes 262144 | tf_op jit(solution)/shard_map/all_to_all | solution.py:33
  109.8 0.0 copy-done
  109.8 0.1 between.1
  109.9 22.2 %all_to_all.31.gathered = f32[32,32,128]{2,1,0:T(8,128)S(1)} all-to-all(f32[32,32,128]{2,1,0:T(8,128)S(1)} %get-tuple-element.42), channel_id=1, replica_groups=mesh['x'=4,'y'=8,'c'=2,'z'=8] {'x','y'}, dimensions={0} | all-to-all | bytes 1048576 | tf_op jit(solution)/shard_map/all_to_all | solution.py:33
  132.0 3.0 %shard_map.73 = f32[8,32,128]{2,1,0:T(8,128)S(1)} custom-call(f32[32,32,128]{2,1,0:T(8,128)S(1)} %all_to_all.31.gathered, bf16[4,1024,512]{2,1,0:T(8,128)(2,1)S(1)} %get-tuple-element.43.refs_0_, bf16[4,1024,512]{2,1,0:T(8,128)(2,1)S(1)} %get-tuple-element.44.refs_1_, bf16[4,1024,512]{2,1,0:T(8,128)(2,1)S(1)} %get-tuple-element.45.refs_2_, ...), custom_call_target="tpu_custom_call" | custom-call | flops 1073741824 | bytes 16777216 | tf_op jit(solution)/shard_map/pallas_call | solution.py:258
  135.0 7.5 %collective-permute-start.10 = (f32[8,32,128]{2,1,0:T(8,128)S(1)}, f32[8,32,128]{2,1,0:T(8,128)S(1)}, u32[]{:S(2)}, u32[]{:S(2)}) collective-permute-start(f32[8,32,128]{2,1,0:T(8,128)S(1)} %shard_map.73), channel_id=1, source_target_pairs={{0,8},{8,0},{1,9},{9,1},{2,10},{10,2},{3,11},{11,3},{4,12},{12,4},... | collective-permute-start | bytes 393224 | tf_op jit(solution)/shard_map/ppermute | solution.py:29
  142.5 3.0 %shard_map.72 = f32[8,32,128]{2,1,0:T(8,128)S(1)} custom-call(f32[32,32,128]{2,1,0:T(8,128)S(1)} %all_to_all.31.gathered, bf16[4,1024,512]{2,1,0:T(8,128)(2,1)S(1)} %get-tuple-element.43.refs_0_, bf16[4,1024,512]{2,1,0:T(8,128)(2,1)S(1)} %get-tuple-element.44.refs_1_, bf16[4,1024,512]{2,1,0:T(8,128)(2,1)S(1)} %get-tuple-element.45.refs_2_, ...), custom_call_target="tpu_custom_call" | custom-call | flops 1073741824 | bytes 16777216 | tf_op jit(solution)/shard_map/pallas_call | solution.py:258
  145.5 0.0 collective-permute-done.10
  145.5 11.9 %all_to_all.32.arrived = f32[8,32,128]{2,1,0:T(8,128)S(1)} all-to-all(f32[8,32,128]{2,1,0:T(8,128)S(1)} %add.7), channel_id=1, replica_groups=mesh['x'=4,'y'=8,'c'=2,'z'=8] {'z'}, dimensions={0} | all-to-all | bytes 262144 | tf_op jit(solution)/shard_map/all_to_all | solution.py:33
  157.4 0.2 settle.1
  157.6 11.3 %all_to_all.33 = f32[16,1,128]{2,1,0:T(1,128)S(1)} all-to-all(f32[16,1,128]{2,1,0:T(1,128)S(1)} %broadcast_in_dim.19), channel_id=1, replica_groups=mesh['x'=4,'y'=8,'c'=2,'z'=8] {'y','c'}, dimensions={0} | all-to-all | bytes 16384 | tf_op jit(solution)/shard_map/all_to_all | solution.py:33
  169.0 11.6 %all_to_all.34.sums = f32[32,1,128]{2,1,0:T(1,128)S(1)} all-to-all(f32[32,1,128]{2,1,0:T(1,128)S(1)} %broadcast_in_dim.20), channel_id=1, replica_groups=mesh['x'=4,'y'=8,'c'=2,'z'=8] {'x','z'}, dimensions={0} | all-to-all | bytes 32768 | tf_op jit(solution)/shard_map/all_to_all | solution.py:33
  180.6 1.0 finish.1
  (13 shorter events, 0.2 us)
Async XLA Ops:
  3.8 29.9 %collective-permute-start.3 = (f32[128,128]{1,0:T(8,128)S(1)}, f32[128,128]{1,0:T(8,128)S(1)}, u32[]{:S(2)}, u32[]{:S(2)}) collective-permute-start(f32[128,128]{1,0:T(8,128)S(1)} %get-tuple-element.31), channel_id=1, source_target_pairs={{0,4},{1,5},{2,6},{3,7},{4,0},{5,1},{6,2},{7,3},{8,12},{9,13},{10,... | collective-permute-start | bytes 196616 | tf_op jit(solution)/shard_map/ppermute | solution.py:29
  15.2 12.1 %collective-permute-start.2 = (f32[128,128]{1,0:T(8,128)S(1)}, f32[128,128]{1,0:T(8,128)S(1)}, u32[]{:S(2)}, u32[]{:S(2)}) collective-permute-start(f32[128,128]{1,0:T(8,128)S(1)} %get-tuple-element.31), channel_id=1, source_target_pairs={{0,7},{1,0},{2,1},{3,2},{4,3},{5,4},{6,5},{7,6},{8,15},{9,8},{10,9... | collective-permute-start | bytes 196616 | tf_op jit(solution)/shard_map/ppermute | solution.py:29
  17.2 10.2 %collective-permute-start.1 = (f32[128,128]{1,0:T(8,128)S(1)}, f32[128,128]{1,0:T(8,128)S(1)}, u32[]{:S(2)}, u32[]{:S(2)}) collective-permute-start(f32[128,128]{1,0:T(8,128)S(1)} %get-tuple-element.31), channel_id=1, source_target_pairs={{0,1},{1,2},{2,3},{3,4},{4,5},{5,6},{6,7},{7,0},{8,9},{9,10},{10,1... | collective-permute-start | bytes 196616 | tf_op jit(solution)/shard_map/ppermute | solution.py:29
  20.5 26.1 %all-to-all-start = ((f32[8,160,128]{2,1,0:T(8,128)}), f32[8,160,128]{2,1,0:T(8,128)S(1)}, u32[]{:S(2)}, u32[]{:S(2)}) async-start(f32[8,160,128]{2,1,0:T(8,128)} %get-tuple-element.30), calls=%async_computation | async-start | bytes 1310720 | tf_op jit(solution)/shard_map/all_to_all | solution.py:33
  27.4 10.7 %collective-permute-start.5 = (f32[2,128,128]{2,1,0:T(8,128)S(1)}, f32[2,128,128]{2,1,0:T(8,128)S(1)}, u32[]{:S(2)}, u32[]{:S(2)}) collective-permute-start(f32[2,128,128]{2,1,0:T(8,128)S(1)} %get-tuple-element.56), channel_id=1, source_target_pairs={{0,6},{1,7},{2,0},{3,1},{4,2},{5,3},{6,4},{7,5},{8,14},{9,15},{10,... | collective-permute-start | bytes 393224 | tf_op jit(solution)/shard_map/ppermute | solution.py:29
  29.4 8.8 %collective-permute-start.4 = (f32[2,128,128]{2,1,0:T(8,128)S(1)}, f32[2,128,128]{2,1,0:T(8,128)S(1)}, u32[]{:S(2)}, u32[]{:S(2)}) collective-permute-start(f32[2,128,128]{2,1,0:T(8,128)S(1)} %get-tuple-element.57), channel_id=1, source_target_pairs={{0,2},{1,3},{2,4},{3,5},{4,6},{5,7},{6,0},{7,1},{8,10},{9,11},{10,... | collective-permute-start | bytes 393224 | tf_op jit(solution)/shard_map/ppermute | solution.py:29
  38.2 18.8 %collective-permute-start.6 = (f32[8,128,128]{2,1,0:T(8,128)S(1)}, f32[8,128,128]{2,1,0:T(8,128)S(1)}, u32[]{:S(2)}, u32[]{:S(2)}) collective-permute-start(f32[8,128,128]{2,1,0:T(8,128)S(1)} %constant_dynamic-update-slice_fusion.same), channel_id=1, source_target_pairs={{0,8},{8,0},{1,9},{9,1},{2,10},{10,2},{3,11},{11,3},{4,12},{12,4},... | collective-permute-start | bytes 1572872 | tf_op jit(solution)/shard_map/ppermute | solution.py:29
  46.6 17.4 %collective-permute-start.8 = (f32[8,160,128]{2,1,0:T(8,128)S(1)}, f32[8,160,128]{2,1,0:T(8,128)S(1)}, u32[]{:S(2)}, u32[]{:S(2)}) collective-permute-start(f32[8,160,128]{2,1,0:T(8,128)S(1)} %all-to-all-done.cols), channel_id=1, source_target_pairs={{0,128},{128,256},{256,384},{384,0},{1,129},{129,257},{257,385},{3... | collective-permute-start | bytes 1966088 | tf_op jit(solution)/shard_map/ppermute | solution.py:29
  49.7 19.9 %collective-permute-start.7 = (f32[8,160,128]{2,1,0:T(8,128)S(1)}, f32[8,160,128]{2,1,0:T(8,128)S(1)}, u32[]{:S(2)}, u32[]{:S(2)}) collective-permute-start(f32[8,160,128]{2,1,0:T(8,128)S(1)} %all-to-all-done.cols), channel_id=1, source_target_pairs={{0,384},{128,0},{256,128},{384,256},{1,385},{129,1},{257,129},{385... | collective-permute-start | bytes 1966088 | tf_op jit(solution)/shard_map/ppermute | solution.py:29
  53.1 25.9 %collective-permute-start = (f32[8,160,128]{2,1,0:T(8,128)S(1)}, f32[8,160,128]{2,1,0:T(8,128)S(1)}, u32[]{:S(2)}, u32[]{:S(2)}) collective-permute-start(f32[8,160,128]{2,1,0:T(8,128)S(1)} %all-to-all-done.cols), channel_id=1, source_target_pairs={{0,256},{128,384},{256,0},{384,128},{1,257},{129,385},{257,1},{385... | collective-permute-start | bytes 1966088 | tf_op jit(solution)/shard_map/ppermute | solution.py:29
  82.1 27.7 %copy-start = (f32[32,128]{1,0:T(8,128)S(1)}, f32[32,128]{1,0:T(8,128)}, u32[]{:S(2)}) copy-start(f32[32,128]{1,0:T(8,128)} %targets.5) | copy-start | bytes 49156
  82.1 13.7 %collective-permute-start.9 = (f32[8,32,128]{2,1,0:T(8,128)S(1)}, f32[8,32,128]{2,1,0:T(8,128)S(1)}, u32[]{:S(2)}, u32[]{:S(2)}) collective-permute-start(f32[8,32,128]{2,1,0:T(8,128)S(1)} %get-tuple-element.41), channel_id=1, source_target_pairs={{0,8},{8,0},{1,9},{9,1},{2,10},{10,2},{3,11},{11,3},{4,12},{12,4},... | collective-permute-start | bytes 393224 | tf_op jit(solution)/shard_map/ppermute | solution.py:29
  135.0 10.5 %collective-permute-start.10 = (f32[8,32,128]{2,1,0:T(8,128)S(1)}, f32[8,32,128]{2,1,0:T(8,128)S(1)}, u32[]{:S(2)}, u32[]{:S(2)}) collective-permute-start(f32[8,32,128]{2,1,0:T(8,128)S(1)} %shard_map.73), channel_id=1, source_target_pairs={{0,8},{8,0},{1,9},{9,1},{2,10},{10,2},{3,11},{11,3},{4,12},{12,4},... | collective-permute-start | bytes 393224 | tf_op jit(solution)/shard_map/ppermute | solution.py:29

commit v4 on v3

--- a/solution.py
+++ b/solution.py
@@ -17,7 +17,7 @@
 BLK = 128
 RHS = 32
 TILE = 512
-SUB = 512
+SUB = 256
 WIDE = 1024
 VMEM = pl.BlockSpec(memory_space=pltpu.VMEM)
 SMEM = pl.BlockSpec(memory_space=pltpu.SMEM)
@@ -85,7 +85,7 @@
     )(*[pltpu.with_memory_space_constraint(v, pltpu.HBM) for v in (points, lengths, targets)], scale, noise)
 
 
-ORDER = (0, -1, 1, 4, -3, -2, 2, 3)
+ORDER = (0, 3, -3, 4, 2, -2, 1, -1)
 
 
 def prepare_rows(row_refs, left, left_sq):
@@ -123,16 +123,15 @@
 def make_values(tiles, left, left_sq, right, right_sq, vecs, high_ref, low_ref, out, before):
     def one(to, carry):
         tile = tiles[0] + to
-        total = jnp.zeros((RHS, TILE), F32)
         for step in range(WIDE // SUB):
             rows = pl.ds(step * SUB, SUB)
             power = jnp.dot(right[rows, :], left[tile], preferred_element_type=F32)
             high, low = halves(jnp.exp2(power + right_sq[rows, :] + left_sq[tile]))
             high_ref[to, rows, :] = high
             low_ref[to, rows, :] = low
-            both = jnp.dot(vecs[:, rows], high, preferred_element_type=F32)
-            rest = jnp.dot(vecs[pl.ds(0, RHS), rows], low, preferred_element_type=F32)
-            total = total + both[:RHS] + both[RHS:] + rest
+        both = jnp.dot(vecs[...], high_ref[to], preferred_element_type=F32)
+        rest = jnp.dot(vecs[pl.ds(0, RHS), :], low_ref[to], preferred_element_type=F32)
+        total = both[:RHS] + both[RHS:] + rest
         for local in range(TILE // BLK):
             piece = total[:, local * BLK : (local + 1) * BLK]
             if before is not None:
@@ -337,11 +336,10 @@
     near = exchange(near, "y")
     behind, ahead = shift(near, "x", 1), shift(near, "x", -1)
     across = shift(near, "x", 2)
+    others = [shift(own, "z", -steps) for steps in ORDER[1:]]
+    same = jnp.stack([own, *others])
+    other = shift(same, "c", 1)
     prepared = own_cols(near)
-    below, above, far = shift(own, "z", 1), shift(own, "z", -1), shift(own, "z", 4)
-    pairs = [shift(jnp.stack([below, own]), "z", 2), shift(jnp.stack([own, above]), "z", -2)]
-    same = jnp.concatenate([jnp.stack([own, below, above, far]), *pairs])
-    other = shift(same, "c", 1)
     pieces, high, low, left, left_sq = own_chunk(same, other, prepared)
     highs, lows = [high], [low]
     for cols in (behind, ahead):

time: 182 us -> 191 us (1.049)
  waiting for transfers between devices: 13.7 us -> 21.1 us
  starting transfers between devices: 62.2 us -> 68.4 us
  Pallas kernels: 32.4 us -> 29.1 us
    ppermute x11 -> x13, waiting for transfers between devices: 9.6 us -> 21.1 us  [shift(): lax.ppermute(value, axis, [(s, (s + steps) % count) for s in range(count)])]
    ppermute x11 -> x13, starting transfers between devices: 55.4 us -> 61.6 us  [shift(): lax.ppermute(value, axis, [(s, (s + steps) % count) for s in range(count)])]
    all_to_all x1, waiting for transfers between devices: 4.06 us -> 0.01 us  [exchange(): return lax.all_to_all(x, axes, 0, 0, tiled=True)]
    pallas_call x4, Pallas kernels: 17.4 us -> 14.8 us  [more_chunk(): pl.pallas_call(functools.partial(more_kernel, tiles), in_specs=[VMEM] * 4...]
  transfers between devices with their start and end apart: 12 -> 14, of which waited for: 4 -> 4; matrix products, arithmetic and copies ran while one was open for 0% -> 0% of each run, Pallas kernels for 13% -> 11%
where the time goes in v4:
time: 191 us; the launch traced here: 190 us
  blocking collectives  69.5 us (36%)
  starting transfers between devices  68.4 us (36%)
  Pallas kernels  29.1 us (15%)
  waiting for transfers between devices  21.1 us (11%)
  between operations  2.2 us (1%)
    all_to_all x5, blocking collectives, exchange(): return lax.all_to_all(x, axes, 0, 0, tiled=True)  69.5 us
    ppermute x13, starting transfers between devices, shift(): lax.ppermute(value, axis, [(s, (s + steps) % count) for s in range(count)])  61.6 us
    ppermute x13, waiting for transfers between devices, shift(): lax.ppermute(value, axis, [(s, (s + steps) % count) for s in range(count)])  21.1 us
    pallas_call x4, Pallas kernels, more_chunk(): pl.pallas_call(functools.partial(more_kernel, tiles), in_specs=[VMEM] * 4...  14.8 us
    all_to_all x1, starting transfers between devices, exchange(): return lax.all_to_all(x, axes, 0, 0, tiled=True)  6.83 us
    pallas_call x2, Pallas kernels, second(): pl.pallas_call(functools.partial(second_kernel, tiles), in_specs=[VMEM] *...  5.94 us
    pallas_call x1, Pallas kernels, own_chunk(): pl.pallas_call(own_kernel, in_specs=[VMEM] * 5, out_specs=[VMEM] * 5, out...  4.77 us
  transfers between devices with their start and end apart: 14, of which 4 were waited for; matrix products, arithmetic and copies ran while one was open for 0% of the time, Pallas kernels for 11%

profile of v4, /device:TPU:1, one launch (start us, length us, event | category | flops | bytes accessed | tf_op | source)
XLA Modules:
  0.0 190.5 jit_solution(9433920332227038684)
XLA Ops:
  1.9 1.9 spread.1
  3.8 4.8 %collective-permute-start.7 = (f32[128,128]{1,0:T(8,128)S(1)}, f32[128,128]{1,0:T(8,128)S(1)}, u32[]{:S(2)}, u32[]{:S(2)}) collective-permute-start(f32[128,128]{1,0:T(8,128)S(1)} %get-tuple-element.31), channel_id=1, source_target_pairs={{0,1},{1,2},{2,3},{3,4},{4,5},{5,6},{6,7},{7,0},{8,9},{9,10},{10,1... | collective-permute-start | bytes 196616 | tf_op jit(solution)/shard_map/ppermute | solution.py:29
  8.6 8.6 %collective-permute-start.6 = (f32[128,128]{1,0:T(8,128)S(1)}, f32[128,128]{1,0:T(8,128)S(1)}, u32[]{:S(2)}, u32[]{:S(2)}) collective-permute-start(f32[128,128]{1,0:T(8,128)S(1)} %get-tuple-element.31), channel_id=1, source_target_pairs={{0,7},{1,0},{2,1},{3,2},{4,3},{5,4},{6,5},{7,6},{8,15},{9,8},{10,9... | collective-permute-start | bytes 196616 | tf_op jit(solution)/shard_map/ppermute | solution.py:29
  17.2 1.9 %collective-permute-start.5 = (f32[128,128]{1,0:T(8,128)S(1)}, f32[128,128]{1,0:T(8,128)S(1)}, u32[]{:S(2)}, u32[]{:S(2)}) collective-permute-start(f32[128,128]{1,0:T(8,128)S(1)} %get-tuple-element.31), channel_id=1, source_target_pairs={{0,2},{1,3},{2,4},{3,5},{4,6},{5,7},{6,0},{7,1},{8,10},{9,11},{10,... | collective-permute-start | bytes 196616 | tf_op jit(solution)/shard_map/ppermute | solution.py:29
  19.1 5.5 %collective-permute-start.4 = (f32[128,128]{1,0:T(8,128)S(1)}, f32[128,128]{1,0:T(8,128)S(1)}, u32[]{:S(2)}, u32[]{:S(2)}) collective-permute-start(f32[128,128]{1,0:T(8,128)S(1)} %get-tuple-element.31), channel_id=1, source_target_pairs={{0,6},{1,7},{2,0},{3,1},{4,2},{5,3},{6,4},{7,5},{8,14},{9,15},{10,... | collective-permute-start | bytes 196616 | tf_op jit(solution)/shard_map/ppermute | solution.py:29
  24.6 3.3 %collective-permute-start.1 = (f32[128,128]{1,0:T(8,128)S(1)}, f32[128,128]{1,0:T(8,128)S(1)}, u32[]{:S(2)}, u32[]{:S(2)}) collective-permute-start(f32[128,128]{1,0:T(8,128)S(1)} %get-tuple-element.31), channel_id=1, source_target_pairs={{0,5},{1,6},{2,7},{3,0},{4,1},{5,2},{6,3},{7,4},{8,13},{9,14},{10,... | collective-permute-start | bytes 196616 | tf_op jit(solution)/shard_map/ppermute | solution.py:29
  28.0 6.8 %all-to-all-start = ((f32[8,160,128]{2,1,0:T(8,128)}), f32[8,160,128]{2,1,0:T(8,128)S(1)}, u32[]{:S(2)}, u32[]{:S(2)}) async-start(f32[8,160,128]{2,1,0:T(8,128)} %get-tuple-element.30), calls=%async_computation | async-start | bytes 1310720 | tf_op jit(solution)/shard_map/all_to_all | solution.py:33
  34.8 0.0 collective-permute-done.1
  34.8 3.7 %collective-permute-start.2 = (f32[128,128]{1,0:T(8,128)S(1)}, f32[128,128]{1,0:T(8,128)S(1)}, u32[]{:S(2)}, u32[]{:S(2)}) collective-permute-start(f32[128,128]{1,0:T(8,128)S(1)} %get-tuple-element.31), channel_id=1, source_target_pairs={{0,3},{1,4},{2,5},{3,6},{4,7},{5,0},{6,1},{7,2},{8,11},{9,12},{10,... | collective-permute-start | bytes 196616 | tf_op jit(solution)/shard_map/ppermute | solution.py:29
  38.6 5.3 %collective-permute-done.2 = f32[128,128]{1,0:T(8,128)S(1)} collective-permute-done((f32[128,128]{1,0:T(8,128)S(1)}, f32[128,128]{1,0:T(8,128)S(1)}, u32[]{:S(2)}, u32[]{:S(2)}) %collective-permute-start.2) | collective-permute-done | bytes 65568 | tf_op jit(solution)/shard_map/ppermute | solution.py:29
  43.9 2.8 %collective-permute-start.3 = (f32[128,128]{1,0:T(8,128)S(1)}, f32[128,128]{1,0:T(8,128)S(1)}, u32[]{:S(2)}, u32[]{:S(2)}) collective-permute-start(f32[128,128]{1,0:T(8,128)S(1)} %get-tuple-element.31), channel_id=1, source_target_pairs={{0,4},{1,5},{2,6},{3,7},{4,0},{5,1},{6,2},{7,3},{8,12},{9,13},{10,... | collective-permute-start | bytes 196616 | tf_op jit(solution)/shard_map/ppermute | solution.py:29
  46.7 6.1 %collective-permute-done.3 = f32[128,128]{1,0:T(8,128)S(1)} collective-permute-done((f32[128,128]{1,0:T(8,128)S(1)}, f32[128,128]{1,0:T(8,128)S(1)}, u32[]{:S(2)}, u32[]{:S(2)}) %collective-permute-start.3) | collective-permute-done | bytes 65568 | tf_op jit(solution)/shard_map/ppermute | solution.py:29
  52.8 0.0 collective-permute-done.4
  52.8 0.0 collective-permute-done.5
  52.9 0.0 collective-permute-done.6
  52.9 0.0 collective-permute-done.7
  52.9 6.4 %collective-permute-start.8 = (f32[8,128,128]{2,1,0:T(8,128)S(1)}, f32[8,128,128]{2,1,0:T(8,128)S(1)}, u32[]{:S(2)}, u32[]{:S(2)}) collective-permute-start(f32[8,128,128]{2,1,0:T(8,128)S(1)} %bitcast_dynamic-update-slice_fusion.same), channel_id=1, source_target_pairs={{0,8},{8,0},{1,9},{9,1},{2,10},{10,2},{3,11},{11,3},{4,12},{12,4},... | collective-permute-start | bytes 1572872 | tf_op jit(solution)/shard_map/ppermute | solution.py:29
  59.4 0.0 all-to-all-done.cols
  59.4 3.1 %collective-permute-start.10 = (f32[8,160,128]{2,1,0:T(8,128)S(1)}, f32[8,160,128]{2,1,0:T(8,128)S(1)}, u32[]{:S(2)}, u32[]{:S(2)}) collective-permute-start(f32[8,160,128]{2,1,0:T(8,128)S(1)} %all-to-all-done.cols), channel_id=1, source_target_pairs={{0,128},{128,256},{256,384},{384,0},{1,129},{129,257},{257,385},{3... | collective-permute-start | bytes 1966088 | tf_op jit(solution)/shard_map/ppermute | solution.py:29
  62.5 3.4 %collective-permute-start.9 = (f32[8,160,128]{2,1,0:T(8,128)S(1)}, f32[8,160,128]{2,1,0:T(8,128)S(1)}, u32[]{:S(2)}, u32[]{:S(2)}) collective-permute-start(f32[8,160,128]{2,1,0:T(8,128)S(1)} %all-to-all-done.cols), channel_id=1, source_target_pairs={{0,384},{128,0},{256,128},{384,256},{1,385},{129,1},{257,129},{385... | collective-permute-start | bytes 1966088 | tf_op jit(solution)/shard_map/ppermute | solution.py:29
  65.9 3.4 %collective-permute-start = (f32[8,160,128]{2,1,0:T(8,128)S(1)}, f32[8,160,128]{2,1,0:T(8,128)S(1)}, u32[]{:S(2)}, u32[]{:S(2)}) collective-permute-start(f32[8,160,128]{2,1,0:T(8,128)S(1)} %all-to-all-done.cols), channel_id=1, source_target_pairs={{0,256},{128,384},{256,0},{384,128},{1,257},{129,385},{257,1},{385... | collective-permute-start | bytes 1966088 | tf_op jit(solution)/shard_map/ppermute | solution.py:29
  69.3 0.4 own_cols.1
  69.7 0.0 collective-permute-done.8.other
  69.7 4.8 %own_chunk.1 = (f32[16,32,128]{2,1,0:T(8,128)S(1)}, bf16[4,1024,512]{2,1,0:T(8,128)(2,1)S(1)}, bf16[4,1024,512]{2,1,0:T(8,128)(2,1)S(1)}, bf16[4,512,512]{2,1,0:T(8,128)(2,1)S(1)}, f32[4,1,512]{2,1,0:T(1,128)S(1)}) custom-call(f32[8,128,128]{2,1,0:T(8,128)S(1)} %bitcast_dynamic-update-slice_fusion.same, f32[8,128,128]{2,1,0:T(8,128)S(1)} %collective-permute-done.8.other, ...), custom_call_target="tpu_custom_call" | custom-call | flops 3221225472 | bytes 8388608 | tf_op jit(solution)/shard_map/own_chunk/pallas_call | solution.py:189
  74.5 4.2 %collective-permute-done.10.cols = f32[8,160,128]{2,1,0:T(8,128)S(1)} collective-permute-done((f32[8,160,128]{2,1,0:T(8,128)S(1)}, f32[8,160,128]{2,1,0:T(8,128)S(1)}, u32[]{:S(2)}, u32[]{:S(2)}) %collective-permute-start.10) | collective-permute-done | bytes 655392 | tf_op jit(solution)/shard_map/ppermute | solution.py:29
  78.7 4.8 %shard_map.68 = (f32[16,32,128]{2,1,0:T(8,128)S(1)}, bf16[4,1024,512]{2,1,0:T(8,128)(2,1)S(1)}, bf16[4,1024,512]{2,1,0:T(8,128)(2,1)S(1)}) custom-call(f32[8,160,128]{2,1,0:T(8,128)S(1)} %collective-permute-done.10.cols, bf16[4,512,512]{2,1,0:T(8,128)(2,1)S(1)} %get-tuple-element.35.left, f32[4,1,512]{2,1,0:T(1,128)S(1)} %get-tuple-element.36.left_sq, ...), custom_call_target="tpu_custom_call" | custom-call | flops 3221225472 | bytes 8388608 | tf_op jit(solution)/shard_map/pallas_call | solution.py:201
  83.6 0.0 collective-permute-done.9.cols
  83.6 4.8 %shard_map.69 = (f32[16,32,128]{2,1,0:T(8,128)S(1)}, bf16[4,1024,512]{2,1,0:T(8,128)(2,1)S(1)}, bf16[4,1024,512]{2,1,0:T(8,128)(2,1)S(1)}) custom-call(f32[8,160,128]{2,1,0:T(8,128)S(1)} %collective-permute-done.9.cols, bf16[4,512,512]{2,1,0:T(8,128)(2,1)S(1)} %get-tuple-element.35.left, f32[4,1,512]{2,1,0:T(1,128)S(1)} %get-tuple-element.36.left_sq, ...), custom_call_target="tpu_custom_call" | custom-call | flops 3221225472 | bytes 8388608 | tf_op jit(solution)/shard_map/pallas_call | solution.py:201
  88.4 5.4 %collective-permute-done.cols = f32[8,160,128]{2,1,0:T(8,128)S(1)} collective-permute-done((f32[8,160,128]{2,1,0:T(8,128)S(1)}, f32[8,160,128]{2,1,0:T(8,128)S(1)}, u32[]{:S(2)}, u32[]{:S(2)}) %collective-permute-start) | collective-permute-done | bytes 655392 | tf_op jit(solution)/shard_map/ppermute | solution.py:29
  93.8 2.6 %shard_map.71 = (f32[8,32,128]{2,1,0:T(8,128)S(1)}, bf16[2,1024,512]{2,1,0:T(8,128)(2,1)S(1)}, bf16[2,1024,512]{2,1,0:T(8,128)(2,1)S(1)}) custom-call(f32[8,160,128]{2,1,0:T(8,128)S(1)} %collective-permute-done.cols, bf16[4,512,512]{2,1,0:T(8,128)(2,1)S(1)} %get-tuple-element.35.left, f32[4,1,512]{2,1,0:T(1,128)S(1)} %get-tuple-element.36.left_sq, ...), custom_call_target="tpu_custom_call" | custom-call | flops 1610612736 | bytes 4194304 | tf_op jit(solution)/shard_map/pallas_call | solution.py:201
  96.4 0.0 copy-start
  96.4 8.0 %collective-permute-start.11 = (f32[8,32,128]{2,1,0:T(8,128)S(1)}, f32[8,32,128]{2,1,0:T(8,128)S(1)}, u32[]{:S(2)}, u32[]{:S(2)}) collective-permute-start(f32[8,32,128]{2,1,0:T(8,128)S(1)} %get-tuple-element.41), channel_id=1, source_target_pairs={{0,8},{8,0},{1,9},{9,1},{2,10},{10,2},{3,11},{11,3},{4,12},{12,4},... | collective-permute-start | bytes 393224 | tf_op jit(solution)/shard_map/ppermute | solution.py:29
  104.4 2.6 %shard_map.70 = (f32[8,32,128]{2,1,0:T(8,128)S(1)}, bf16[2,1024,512]{2,1,0:T(8,128)(2,1)S(1)}, bf16[2,1024,512]{2,1,0:T(8,128)(2,1)S(1)}) custom-call(f32[8,160,128]{2,1,0:T(8,128)S(1)} %collective-permute-done.cols, bf16[4,512,512]{2,1,0:T(8,128)(2,1)S(1)} %get-tuple-element.35.left, f32[4,1,512]{2,1,0:T(1,128)S(1)} %get-tuple-element.36.left_sq, ...), custom_call_target="tpu_custom_call" | custom-call | flops 1610612736 | bytes 4194304 | tf_op jit(solution)/shard_map/pallas_call | solution.py:201
  107.0 0.0 collective-permute-done.11
  107.0 11.9 %all_to_all.30.arrived = f32[8,32,128]{2,1,0:T(8,128)S(1)} all-to-all(f32[8,32,128]{2,1,0:T(8,128)S(1)} %add.6), channel_id=1, replica_groups=mesh['x'=4,'y'=8,'c'=2,'z'=8] {'z'}, dimensions={0} | all-to-all | bytes 262144 | tf_op jit(solution)/shard_map/all_to_all | solution.py:33
  118.9 0.0 copy-done
  118.9 0.1 between.1
  119.0 22.7 %all_to_all.31.gathered = f32[32,32,128]{2,1,0:T(8,128)S(1)} all-to-all(f32[32,32,128]{2,1,0:T(8,128)S(1)} %get-tuple-element.42), channel_id=1, replica_groups=mesh['x'=4,'y'=8,'c'=2,'z'=8] {'x','y'}, dimensions={0} | all-to-all | bytes 1048576 | tf_op jit(solution)/shard_map/all_to_all | solution.py:33
  141.7 3.0 %shard_map.73 = f32[8,32,128]{2,1,0:T(8,128)S(1)} custom-call(f32[32,32,128]{2,1,0:T(8,128)S(1)} %all_to_all.31.gathered, bf16[4,1024,512]{2,1,0:T(8,128)(2,1)S(1)} %get-tuple-element.43.refs_0_, bf16[4,1024,512]{2,1,0:T(8,128)(2,1)S(1)} %get-tuple-element.44.refs_1_, bf16[4,1024,512]{2,1,0:T(8,128)(2,1)S(1)} %get-tuple-element.45.refs_2_, ...), custom_call_target="tpu_custom_call" | custom-call | flops 1073741824 | bytes 16777216 | tf_op jit(solution)/shard_map/pallas_call | solution.py:257
  144.7 6.6 %collective-permute-start.12 = (f32[8,32,128]{2,1,0:T(8,128)S(1)}, f32[8,32,128]{2,1,0:T(8,128)S(1)}, u32[]{:S(2)}, u32[]{:S(2)}) collective-permute-start(f32[8,32,128]{2,1,0:T(8,128)S(1)} %shard_map.73), channel_id=1, source_target_pairs={{0,8},{8,0},{1,9},{9,1},{2,10},{10,2},{3,11},{11,3},{4,12},{12,4},... | collective-permute-start | bytes 393224 | tf_op jit(solution)/shard_map/ppermute | solution.py:29
  151.3 3.0 %shard_map.72 = f32[8,32,128]{2,1,0:T(8,128)S(1)} custom-call(f32[32,32,128]{2,1,0:T(8,128)S(1)} %all_to_all.31.gathered, bf16[4,1024,512]{2,1,0:T(8,128)(2,1)S(1)} %get-tuple-element.43.refs_0_, bf16[4,1024,512]{2,1,0:T(8,128)(2,1)S(1)} %get-tuple-element.44.refs_1_, bf16[4,1024,512]{2,1,0:T(8,128)(2,1)S(1)} %get-tuple-element.45.refs_2_, ...), custom_call_target="tpu_custom_call" | custom-call | flops 1073741824 | bytes 16777216 | tf_op jit(solution)/shard_map/pallas_call | solution.py:257
  154.3 0.0 collective-permute-done.12
  154.3 11.9 %all_to_all.32.arrived = f32[8,32,128]{2,1,0:T(8,128)S(1)} all-to-all(f32[8,32,128]{2,1,0:T(8,128)S(1)} %add.7), channel_id=1, replica_groups=mesh['x'=4,'y'=8,'c'=2,'z'=8] {'z'}, dimensions={0} | all-to-all | bytes 262144 | tf_op jit(solution)/shard_map/all_to_all | solution.py:33
  166.2 0.2 settle.1
  166.4 11.4 %all_to_all.33 = f32[16,1,128]{2,1,0:T(1,128)S(1)} all-to-all(f32[16,1,128]{2,1,0:T(1,128)S(1)} %broadcast_in_dim.19), channel_id=1, replica_groups=mesh['x'=4,'y'=8,'c'=2,'z'=8] {'y','c'}, dimensions={0} | all-to-all | bytes 16384 | tf_op jit(solution)/shard_map/all_to_all | solution.py:33
  177.9 11.6 %all_to_all.34.sums = f32[32,1,128]{2,1,0:T(1,128)S(1)} all-to-all(f32[32,1,128]{2,1,0:T(1,128)S(1)} %broadcast_in_dim.20), channel_id=1, replica_groups=mesh['x'=4,'y'=8,'c'=2,'z'=8] {'x','z'}, dimensions={0} | all-to-all | bytes 32768 | tf_op jit(solution)/shard_map/all_to_all | solution.py:33
  189.5 1.0 finish.1
  (14 shorter events, 0.2 us)
Async XLA Ops:
  3.8 49.1 %collective-permute-start.7 = (f32[128,128]{1,0:T(8,128)S(1)}, f32[128,128]{1,0:T(8,128)S(1)}, u32[]{:S(2)}, u32[]{:S(2)}) collective-permute-start(f32[128,128]{1,0:T(8,128)S(1)} %get-tuple-element.31), channel_id=1, source_target_pairs={{0,1},{1,2},{2,3},{3,4},{4,5},{5,6},{6,7},{7,0},{8,9},{9,10},{10,1... | collective-permute-start | bytes 196616 | tf_op jit(solution)/shard_map/ppermute | solution.py:29
  8.6 44.2 %collective-permute-start.6 = (f32[128,128]{1,0:T(8,128)S(1)}, f32[128,128]{1,0:T(8,128)S(1)}, u32[]{:S(2)}, u32[]{:S(2)}) collective-permute-start(f32[128,128]{1,0:T(8,128)S(1)} %get-tuple-element.31), channel_id=1, source_target_pairs={{0,7},{1,0},{2,1},{3,2},{4,3},{5,4},{6,5},{7,6},{8,15},{9,8},{10,9... | collective-permute-start | bytes 196616 | tf_op jit(solution)/shard_map/ppermute | solution.py:29
  17.2 35.6 %collective-permute-start.5 = (f32[128,128]{1,0:T(8,128)S(1)}, f32[128,128]{1,0:T(8,128)S(1)}, u32[]{:S(2)}, u32[]{:S(2)}) collective-permute-start(f32[128,128]{1,0:T(8,128)S(1)} %get-tuple-element.31), channel_id=1, source_target_pairs={{0,2},{1,3},{2,4},{3,5},{4,6},{5,7},{6,0},{7,1},{8,10},{9,11},{10,... | collective-permute-start | bytes 196616 | tf_op jit(solution)/shard_map/ppermute | solution.py:29
  19.1 33.7 %collective-permute-start.4 = (f32[128,128]{1,0:T(8,128)S(1)}, f32[128,128]{1,0:T(8,128)S(1)}, u32[]{:S(2)}, u32[]{:S(2)}) collective-permute-start(f32[128,128]{1,0:T(8,128)S(1)} %get-tuple-element.31), channel_id=1, source_target_pairs={{0,6},{1,7},{2,0},{3,1},{4,2},{5,3},{6,4},{7,5},{8,14},{9,15},{10,... | collective-permute-start | bytes 196616 | tf_op jit(solution)/shard_map/ppermute | solution.py:29
  24.6 10.2 %collective-permute-start.1 = (f32[128,128]{1,0:T(8,128)S(1)}, f32[128,128]{1,0:T(8,128)S(1)}, u32[]{:S(2)}, u32[]{:S(2)}) collective-permute-start(f32[128,128]{1,0:T(8,128)S(1)} %get-tuple-element.31), channel_id=1, source_target_pairs={{0,5},{1,6},{2,7},{3,0},{4,1},{5,2},{6,3},{7,4},{8,13},{9,14},{10,... | collective-permute-start | bytes 196616 | tf_op jit(solution)/shard_map/ppermute | solution.py:29
  28.0 31.4 %all-to-all-start = ((f32[8,160,128]{2,1,0:T(8,128)}), f32[8,160,128]{2,1,0:T(8,128)S(1)}, u32[]{:S(2)}, u32[]{:S(2)}) async-start(f32[8,160,128]{2,1,0:T(8,128)} %get-tuple-element.30), calls=%async_computation | async-start | bytes 1310720 | tf_op jit(solution)/shard_map/all_to_all | solution.py:33
  34.8 9.1 %collective-permute-start.2 = (f32[128,128]{1,0:T(8,128)S(1)}, f32[128,128]{1,0:T(8,128)S(1)}, u32[]{:S(2)}, u32[]{:S(2)}) collective-permute-start(f32[128,128]{1,0:T(8,128)S(1)} %get-tuple-element.31), channel_id=1, source_target_pairs={{0,3},{1,4},{2,5},{3,6},{4,7},{5,0},{6,1},{7,2},{8,11},{9,12},{10,... | collective-permute-start | bytes 196616 | tf_op jit(solution)/shard_map/ppermute | solution.py:29
  43.9 8.9 %collective-permute-start.3 = (f32[128,128]{1,0:T(8,128)S(1)}, f32[128,128]{1,0:T(8,128)S(1)}, u32[]{:S(2)}, u32[]{:S(2)}) collective-permute-start(f32[128,128]{1,0:T(8,128)S(1)} %get-tuple-element.31), channel_id=1, source_target_pairs={{0,4},{1,5},{2,6},{3,7},{4,0},{5,1},{6,2},{7,3},{8,12},{9,13},{10,... | collective-permute-start | bytes 196616 | tf_op jit(solution)/shard_map/ppermute | solution.py:29
  52.9 16.8 %collective-permute-start.8 = (f32[8,128,128]{2,1,0:T(8,128)S(1)}, f32[8,128,128]{2,1,0:T(8,128)S(1)}, u32[]{:S(2)}, u32[]{:S(2)}) collective-permute-start(f32[8,128,128]{2,1,0:T(8,128)S(1)} %bitcast_dynamic-update-slice_fusion.same), channel_id=1, source_target_pairs={{0,8},{8,0},{1,9},{9,1},{2,10},{10,2},{3,11},{11,3},{4,12},{12,4},... | collective-permute-start | bytes 1572872 | tf_op jit(solution)/shard_map/ppermute | solution.py:29
  59.4 19.4 %collective-permute-start.10 = (f32[8,160,128]{2,1,0:T(8,128)S(1)}, f32[8,160,128]{2,1,0:T(8,128)S(1)}, u32[]{:S(2)}, u32[]{:S(2)}) collective-permute-start(f32[8,160,128]{2,1,0:T(8,128)S(1)} %all-to-all-done.cols), channel_id=1, source_target_pairs={{0,128},{128,256},{256,384},{384,0},{1,129},{129,257},{257,385},{3... | collective-permute-start | bytes 1966088 | tf_op jit(solution)/shard_map/ppermute | solution.py:29
  62.5 21.1 %collective-permute-start.9 = (f32[8,160,128]{2,1,0:T(8,128)S(1)}, f32[8,160,128]{2,1,0:T(8,128)S(1)}, u32[]{:S(2)}, u32[]{:S(2)}) collective-permute-start(f32[8,160,128]{2,1,0:T(8,128)S(1)} %all-to-all-done.cols), channel_id=1, source_target_pairs={{0,384},{128,0},{256,128},{384,256},{1,385},{129,1},{257,129},{385... | collective-permute-start | bytes 1966088 | tf_op jit(solution)/shard_map/ppermute | solution.py:29
  65.9 27.9 %collective-permute-start = (f32[8,160,128]{2,1,0:T(8,128)S(1)}, f32[8,160,128]{2,1,0:T(8,128)S(1)}, u32[]{:S(2)}, u32[]{:S(2)}) collective-permute-start(f32[8,160,128]{2,1,0:T(8,128)S(1)} %all-to-all-done.cols), channel_id=1, source_target_pairs={{0,256},{128,384},{256,0},{384,128},{1,257},{129,385},{257,1},{385... | collective-permute-start | bytes 1966088 | tf_op jit(solution)/shard_map/ppermute | solution.py:29
  96.4 22.5 %copy-start = (f32[32,128]{1,0:T(8,128)S(1)}, f32[32,128]{1,0:T(8,128)}, u32[]{:S(2)}) copy-start(f32[32,128]{1,0:T(8,128)} %targets.5) | copy-start | bytes 49156
  96.4 10.6 %collective-permute-start.11 = (f32[8,32,128]{2,1,0:T(8,128)S(1)}, f32[8,32,128]{2,1,0:T(8,128)S(1)}, u32[]{:S(2)}, u32[]{:S(2)}) collective-permute-start(f32[8,32,128]{2,1,0:T(8,128)S(1)} %get-tuple-element.41), channel_id=1, source_target_pairs={{0,8},{8,0},{1,9},{9,1},{2,10},{10,2},{3,11},{11,3},{4,12},{12,4},... | collective-permute-start | bytes 393224 | tf_op jit(solution)/shard_map/ppermute | solution.py:29
  144.7 9.6 %collective-permute-start.12 = (f32[8,32,128]{2,1,0:T(8,128)S(1)}, f32[8,32,128]{2,1,0:T(8,128)S(1)}, u32[]{:S(2)}, u32[]{:S(2)}) collective-permute-start(f32[8,32,128]{2,1,0:T(8,128)S(1)} %shard_map.73), channel_id=1, source_target_pairs={{0,8},{8,0},{1,9},{9,1},{2,10},{10,2},{3,11},{11,3},{4,12},{12,4},... | collective-permute-start | bytes 393224 | tf_op jit(solution)/shard_map/ppermute | solution.py:29

commit v5 on v4

--- a/solution.py
+++ b/solution.py
@@ -85,7 +85,7 @@
     )(*[pltpu.with_memory_space_constraint(v, pltpu.HBM) for v in (points, lengths, targets)], scale, noise)
 
 
-ORDER = (0, 3, -3, 4, 2, -2, 1, -1)
+ORDER = (0, -1, 1, 4, -3, -2, 2, 3)
 
 
 def prepare_rows(row_refs, left, left_sq):
@@ -336,8 +336,9 @@
     near = exchange(near, "y")
     behind, ahead = shift(near, "x", 1), shift(near, "x", -1)
     across = shift(near, "x", 2)
-    others = [shift(own, "z", -steps) for steps in ORDER[1:]]
-    same = jnp.stack([own, *others])
+    below, above, far = shift(own, "z", 1), shift(own, "z", -1), shift(own, "z", 4)
+    pairs = [shift(jnp.stack([below, own]), "z", 2), shift(jnp.stack([own, above]), "z", -2)]
+    same = jnp.concatenate([jnp.stack([own, below, above, far]), *pairs])
     other = shift(same, "c", 1)
     prepared = own_cols(near)
     pieces, high, low, left, left_sq = own_chunk(same, other, prepared)

time: 191 us -> 181 us (0.948)
  starting transfers between devices: 68.4 us -> 61.3 us
  waiting for transfers between devices: 21.1 us -> 16.2 us
    ppermute x13 -> x11, waiting for transfers between devices: 21.1 us -> 12.1 us  [shift(): lax.ppermute(value, axis, [(s, (s + steps) % count) for s in range(count)])]
    ppermute x13 -> x11, starting transfers between devices: 61.6 us -> 54.5 us  [shift(): lax.ppermute(value, axis, [(s, (s + steps) % count) for s in range(count)])]
    all_to_all x1, waiting for transfers between devices: 0.01 us -> 4.06 us  [exchange(): return lax.all_to_all(x, axes, 0, 0, tiled=True)]
  transfers between devices with their start and end apart: 14 -> 12, of which waited for: 4 -> 4; matrix products, arithmetic and copies ran while one was open for 0% -> 0% of each run, Pallas kernels for 11% -> 11%
where the time goes in v5:
time: 181 us; the launch traced here: 180 us
  blocking collectives  70.9 us (39%)
  starting transfers between devices  61.3 us (34%)
  Pallas kernels  29.1 us (16%)
  waiting for transfers between devices  16.2 us (9%)
  between operations  2.17 us (1%)
    all_to_all x5, blocking collectives, exchange(): return lax.all_to_all(x, axes, 0, 0, tiled=True)  70.9 us
    ppermute x11, starting transfers between devices, shift(): lax.ppermute(value, axis, [(s, (s + steps) % count) for s in range(count)])  54.5 us
    pallas_call x4, Pallas kernels, more_chunk(): pl.pallas_call(functools.partial(more_kernel, tiles), in_specs=[VMEM] * 4...  14.8 us
    ppermute x11, waiting for transfers between devices, shift(): lax.ppermute(value, axis, [(s, (s + steps) % count) for s in range(count)])  12.1 us
    all_to_all x1, starting transfers between devices, exchange(): return lax.all_to_all(x, axes, 0, 0, tiled=True)  6.83 us
    pallas_call x2, Pallas kernels, second(): pl.pallas_call(functools.partial(second_kernel, tiles), in_specs=[VMEM] *...  5.94 us
    pallas_call x1, Pallas kernels, own_chunk(): pl.pallas_call(own_kernel, in_specs=[VMEM] * 5, out_specs=[VMEM] * 5, out...  4.76 us
    all_to_all x1, waiting for transfers between devices, exchange(): return lax.all_to_all(x, axes, 0, 0, tiled=True)  4.06 us
  transfers between devices with their start and end apart: 12, of which 4 were waited for; matrix products, arithmetic and copies ran while one was open for 0% of the time, Pallas kernels for 11%

profile of v5, /device:TPU:1, one launch (start us, length us, event | category | flops | bytes accessed | tf_op | source)
XLA Modules:
  0.0 179.9 jit_solution(17855054599414109713)
XLA Ops:
  1.9 1.9 %spread.1 = (f32[8,160,128]{2,1,0:T(8,128)}, f32[128,128]{1,0:T(8,128)S(1)}, f32[8,128]{1,0:T(8,128)S(1)}) custom-call(f32[128,128]{1,0:T(8,128)} %points_in.1, f32[1,128]{1,0:T(1,128)} %bitcast.16, f32[32,128]{1,0:T(8,128)} %targets.5, f32[1]{0:T(128)S(6)} %copy.13.scale, f32[1]{0:T(128)S(6)} %copy.14.noise), custom_call_target="tpu_custom_call" | custom-call | tf_op jit(solution)/shard_map/spread/pallas_call | solution.py:68
  3.8 11.5 %collective-permute-start.3 = (f32[128,128]{1,0:T(8,128)S(1)}, f32[128,128]{1,0:T(8,128)S(1)}, u32[]{:S(2)}, u32[]{:S(2)}) collective-permute-start(f32[128,128]{1,0:T(8,128)S(1)} %get-tuple-element.31), channel_id=1, source_target_pairs={{0,4},{1,5},{2,6},{3,7},{4,0},{5,1},{6,2},{7,3},{8,12},{9,13},{10,... | collective-permute-start | bytes 196616 | tf_op jit(solution)/shard_map/ppermute | solution.py:29
  15.2 2.0 %collective-permute-start.2 = (f32[128,128]{1,0:T(8,128)S(1)}, f32[128,128]{1,0:T(8,128)S(1)}, u32[]{:S(2)}, u32[]{:S(2)}) collective-permute-start(f32[128,128]{1,0:T(8,128)S(1)} %get-tuple-element.31), channel_id=1, source_target_pairs={{0,7},{1,0},{2,1},{3,2},{4,3},{5,4},{6,5},{7,6},{8,15},{9,8},{10,9... | collective-permute-start | bytes 196616 | tf_op jit(solution)/shard_map/ppermute | solution.py:29
  17.2 3.3 %collective-permute-start.1 = (f32[128,128]{1,0:T(8,128)S(1)}, f32[128,128]{1,0:T(8,128)S(1)}, u32[]{:S(2)}, u32[]{:S(2)}) collective-permute-start(f32[128,128]{1,0:T(8,128)S(1)} %get-tuple-element.31), channel_id=1, source_target_pairs={{0,1},{1,2},{2,3},{3,4},{4,5},{5,6},{6,7},{7,0},{8,9},{9,10},{10,1... | collective-permute-start | bytes 196616 | tf_op jit(solution)/shard_map/ppermute | solution.py:29
  20.5 6.8 %all-to-all-start = ((f32[8,160,128]{2,1,0:T(8,128)}), f32[8,160,128]{2,1,0:T(8,128)S(1)}, u32[]{:S(2)}, u32[]{:S(2)}) async-start(f32[8,160,128]{2,1,0:T(8,128)} %get-tuple-element.30), calls=%async_computation | async-start | bytes 1310720 | tf_op jit(solution)/shard_map/all_to_all | solution.py:33
  27.4 0.0 collective-permute-done.2
  27.4 0.0 collective-permute-done.1
  27.4 1.9 %collective-permute-start.5 = (f32[2,128,128]{2,1,0:T(8,128)S(1)}, f32[2,128,128]{2,1,0:T(8,128)S(1)}, u32[]{:S(2)}, u32[]{:S(2)}) collective-permute-start(f32[2,128,128]{2,1,0:T(8,128)S(1)} %get-tuple-element.56), channel_id=1, source_target_pairs={{0,6},{1,7},{2,0},{3,1},{4,2},{5,3},{6,4},{7,5},{8,14},{9,15},{10,... | collective-permute-start | bytes 393224 | tf_op jit(solution)/shard_map/ppermute | solution.py:29
  29.4 4.2 %collective-permute-start.4 = (f32[2,128,128]{2,1,0:T(8,128)S(1)}, f32[2,128,128]{2,1,0:T(8,128)S(1)}, u32[]{:S(2)}, u32[]{:S(2)}) collective-permute-start(f32[2,128,128]{2,1,0:T(8,128)S(1)} %get-tuple-element.57), channel_id=1, source_target_pairs={{0,2},{1,3},{2,4},{3,5},{4,6},{5,7},{6,0},{7,1},{8,10},{9,11},{10,... | collective-permute-start | bytes 393224 | tf_op jit(solution)/shard_map/ppermute | solution.py:29
  33.7 0.0 collective-permute-done.3
  33.7 4.5 %collective-permute-done.4 = f32[2,128,128]{2,1,0:T(8,128)S(1)} collective-permute-done((f32[2,128,128]{2,1,0:T(8,128)S(1)}, f32[2,128,128]{2,1,0:T(8,128)S(1)}, u32[]{:S(2)}, u32[]{:S(2)}) %collective-permute-start.4) | collective-permute-done | bytes 131104 | tf_op jit(solution)/shard_map/ppermute | solution.py:29
  38.2 0.0 collective-permute-done.5
  38.2 4.4 %collective-permute-start.6 = (f32[8,128,128]{2,1,0:T(8,128)S(1)}, f32[8,128,128]{2,1,0:T(8,128)S(1)}, u32[]{:S(2)}, u32[]{:S(2)}) collective-permute-start(f32[8,128,128]{2,1,0:T(8,128)S(1)} %constant_dynamic-update-slice_fusion.same), channel_id=1, source_target_pairs={{0,8},{8,0},{1,9},{9,1},{2,10},{10,2},{3,11},{11,3},{4,12},{12,4},... | collective-permute-start | bytes 1572872 | tf_op jit(solution)/shard_map/ppermute | solution.py:29
  42.6 4.1 %all-to-all-done.cols = f32[8,160,128]{2,1,0:T(8,128)S(1)} async-done(((f32[8,160,128]{2,1,0:T(8,128)}), f32[8,160,128]{2,1,0:T(8,128)S(1)}, u32[]{:S(2)}, u32[]{:S(2)}) %all-to-all-start) | async-done | bytes 655392 | tf_op jit(solution)/shard_map/all_to_all | solution.py:33
  46.6 3.1 %collective-permute-start.8 = (f32[8,160,128]{2,1,0:T(8,128)S(1)}, f32[8,160,128]{2,1,0:T(8,128)S(1)}, u32[]{:S(2)}, u32[]{:S(2)}) collective-permute-start(f32[8,160,128]{2,1,0:T(8,128)S(1)} %all-to-all-done.cols), channel_id=1, source_target_pairs={{0,128},{128,256},{256,384},{384,0},{1,129},{129,257},{257,385},{3... | collective-permute-start | bytes 1966088 | tf_op jit(solution)/shard_map/ppermute | solution.py:29
  49.7 3.4 %collective-permute-start.7 = (f32[8,160,128]{2,1,0:T(8,128)S(1)}, f32[8,160,128]{2,1,0:T(8,128)S(1)}, u32[]{:S(2)}, u32[]{:S(2)}) collective-permute-start(f32[8,160,128]{2,1,0:T(8,128)S(1)} %all-to-all-done.cols), channel_id=1, source_target_pairs={{0,384},{128,0},{256,128},{384,256},{1,385},{129,1},{257,129},{385... | collective-permute-start | bytes 1966088 | tf_op jit(solution)/shard_map/ppermute | solution.py:29
  53.1 3.4 %collective-permute-start = (f32[8,160,128]{2,1,0:T(8,128)S(1)}, f32[8,160,128]{2,1,0:T(8,128)S(1)}, u32[]{:S(2)}, u32[]{:S(2)}) collective-permute-start(f32[8,160,128]{2,1,0:T(8,128)S(1)} %all-to-all-done.cols), channel_id=1, source_target_pairs={{0,256},{128,384},{256,0},{384,128},{1,257},{129,385},{257,1},{385... | collective-permute-start | bytes 1966088 | tf_op jit(solution)/shard_map/ppermute | solution.py:29
  56.6 0.4 own_cols.1
  57.0 0.0 collective-permute-done.6.other
  57.0 4.8 %own_chunk.1 = (f32[16,32,128]{2,1,0:T(8,128)S(1)}, bf16[4,1024,512]{2,1,0:T(8,128)(2,1)S(1)}, bf16[4,1024,512]{2,1,0:T(8,128)(2,1)S(1)}, bf16[4,512,512]{2,1,0:T(8,128)(2,1)S(1)}, f32[4,1,512]{2,1,0:T(1,128)S(1)}) custom-call(f32[8,128,128]{2,1,0:T(8,128)S(1)} %constant_dynamic-update-slice_fusion.same, f32[8,128,128]{2,1,0:T(8,128)S(1)} %collective-permute-done.6.other, ...), custom_call_target="tpu_custom_call" | custom-call | flops 3221225472 | bytes 8388608 | tf_op jit(solution)/shard_map/own_chunk/pallas_call | solution.py:189
  61.8 2.3 %collective-permute-done.8.cols = f32[8,160,128]{2,1,0:T(8,128)S(1)} collective-permute-done((f32[8,160,128]{2,1,0:T(8,128)S(1)}, f32[8,160,128]{2,1,0:T(8,128)S(1)}, u32[]{:S(2)}, u32[]{:S(2)}) %collective-permute-start.8) | collective-permute-done | bytes 655392 | tf_op jit(solution)/shard_map/ppermute | solution.py:29
  64.0 4.8 %shard_map.68 = (f32[16,32,128]{2,1,0:T(8,128)S(1)}, bf16[4,1024,512]{2,1,0:T(8,128)(2,1)S(1)}, bf16[4,1024,512]{2,1,0:T(8,128)(2,1)S(1)}) custom-call(f32[8,160,128]{2,1,0:T(8,128)S(1)} %collective-permute-done.8.cols, bf16[4,512,512]{2,1,0:T(8,128)(2,1)S(1)} %get-tuple-element.35.left, f32[4,1,512]{2,1,0:T(1,128)S(1)} %get-tuple-element.36.left_sq, ...), custom_call_target="tpu_custom_call" | custom-call | flops 3221225472 | bytes 8388608 | tf_op jit(solution)/shard_map/pallas_call | solution.py:201
  68.8 0.0 collective-permute-done.7.cols
  68.8 4.8 %shard_map.69 = (f32[16,32,128]{2,1,0:T(8,128)S(1)}, bf16[4,1024,512]{2,1,0:T(8,128)(2,1)S(1)}, bf16[4,1024,512]{2,1,0:T(8,128)(2,1)S(1)}) custom-call(f32[8,160,128]{2,1,0:T(8,128)S(1)} %collective-permute-done.7.cols, bf16[4,512,512]{2,1,0:T(8,128)(2,1)S(1)} %get-tuple-element.35.left, f32[4,1,512]{2,1,0:T(1,128)S(1)} %get-tuple-element.36.left_sq, ...), custom_call_target="tpu_custom_call" | custom-call | flops 3221225472 | bytes 8388608 | tf_op jit(solution)/shard_map/pallas_call | solution.py:201
  73.7 5.4 %collective-permute-done.cols = f32[8,160,128]{2,1,0:T(8,128)S(1)} collective-permute-done((f32[8,160,128]{2,1,0:T(8,128)S(1)}, f32[8,160,128]{2,1,0:T(8,128)S(1)}, u32[]{:S(2)}, u32[]{:S(2)}) %collective-permute-start) | collective-permute-done | bytes 655392 | tf_op jit(solution)/shard_map/ppermute | solution.py:29
  79.0 2.6 %shard_map.71 = (f32[8,32,128]{2,1,0:T(8,128)S(1)}, bf16[2,1024,512]{2,1,0:T(8,128)(2,1)S(1)}, bf16[2,1024,512]{2,1,0:T(8,128)(2,1)S(1)}) custom-call(f32[8,160,128]{2,1,0:T(8,128)S(1)} %collective-permute-done.cols, bf16[4,512,512]{2,1,0:T(8,128)(2,1)S(1)} %get-tuple-element.35.left, f32[4,1,512]{2,1,0:T(1,128)S(1)} %get-tuple-element.36.left_sq, ...), custom_call_target="tpu_custom_call" | custom-call | flops 1610612736 | bytes 4194304 | tf_op jit(solution)/shard_map/pallas_call | solution.py:201
  81.6 0.0 copy-start
  81.7 10.0 %collective-permute-start.9 = (f32[8,32,128]{2,1,0:T(8,128)S(1)}, f32[8,32,128]{2,1,0:T(8,128)S(1)}, u32[]{:S(2)}, u32[]{:S(2)}) collective-permute-start(f32[8,32,128]{2,1,0:T(8,128)S(1)} %get-tuple-element.41), channel_id=1, source_target_pairs={{0,8},{8,0},{1,9},{9,1},{2,10},{10,2},{3,11},{11,3},{4,12},{12,4},... | collective-permute-start | bytes 393224 | tf_op jit(solution)/shard_map/ppermute | solution.py:29
  91.6 2.6 %shard_map.70 = (f32[8,32,128]{2,1,0:T(8,128)S(1)}, bf16[2,1024,512]{2,1,0:T(8,128)(2,1)S(1)}, bf16[2,1024,512]{2,1,0:T(8,128)(2,1)S(1)}) custom-call(f32[8,160,128]{2,1,0:T(8,128)S(1)} %collective-permute-done.cols, bf16[4,512,512]{2,1,0:T(8,128)(2,1)S(1)} %get-tuple-element.35.left, f32[4,1,512]{2,1,0:T(1,128)S(1)} %get-tuple-element.36.left_sq, ...), custom_call_target="tpu_custom_call" | custom-call | flops 1610612736 | bytes 4194304 | tf_op jit(solution)/shard_map/pallas_call | solution.py:201
  94.2 0.0 collective-permute-done.9
  94.3 13.9 %all_to_all.30.arrived = f32[8,32,128]{2,1,0:T(8,128)S(1)} all-to-all(f32[8,32,128]{2,1,0:T(8,128)S(1)} %add.6), channel_id=1, replica_groups=mesh['x'=4,'y'=8,'c'=2,'z'=8] {'z'}, dimensions={0} | all-to-all | bytes 262144 | tf_op jit(solution)/shard_map/all_to_all | solution.py:33
  108.2 0.0 copy-done
  108.2 0.1 between.1
  108.3 22.2 %all_to_all.31.gathered = f32[32,32,128]{2,1,0:T(8,128)S(1)} all-to-all(f32[32,32,128]{2,1,0:T(8,128)S(1)} %get-tuple-element.42), channel_id=1, replica_groups=mesh['x'=4,'y'=8,'c'=2,'z'=8] {'x','y'}, dimensions={0} | all-to-all | bytes 1048576 | tf_op jit(solution)/shard_map/all_to_all | solution.py:33
  130.5 3.0 %shard_map.73 = f32[8,32,128]{2,1,0:T(8,128)S(1)} custom-call(f32[32,32,128]{2,1,0:T(8,128)S(1)} %all_to_all.31.gathered, bf16[4,1024,512]{2,1,0:T(8,128)(2,1)S(1)} %get-tuple-element.43.refs_0_, bf16[4,1024,512]{2,1,0:T(8,128)(2,1)S(1)} %get-tuple-element.44.refs_1_, bf16[4,1024,512]{2,1,0:T(8,128)(2,1)S(1)} %get-tuple-element.45.refs_2_, ...), custom_call_target="tpu_custom_call" | custom-call | flops 1073741824 | bytes 16777216 | tf_op jit(solution)/shard_map/pallas_call | solution.py:257
  133.5 7.3 %collective-permute-start.10 = (f32[8,32,128]{2,1,0:T(8,128)S(1)}, f32[8,32,128]{2,1,0:T(8,128)S(1)}, u32[]{:S(2)}, u32[]{:S(2)}) collective-permute-start(f32[8,32,128]{2,1,0:T(8,128)S(1)} %shard_map.73), channel_id=1, source_target_pairs={{0,8},{8,0},{1,9},{9,1},{2,10},{10,2},{3,11},{11,3},{4,12},{12,4},... | collective-permute-start | bytes 393224 | tf_op jit(solution)/shard_map/ppermute | solution.py:29
  140.8 3.0 %shard_map.72 = f32[8,32,128]{2,1,0:T(8,128)S(1)} custom-call(f32[32,32,128]{2,1,0:T(8,128)S(1)} %all_to_all.31.gathered, bf16[4,1024,512]{2,1,0:T(8,128)(2,1)S(1)} %get-tuple-element.43.refs_0_, bf16[4,1024,512]{2,1,0:T(8,128)(2,1)S(1)} %get-tuple-element.44.refs_1_, bf16[4,1024,512]{2,1,0:T(8,128)(2,1)S(1)} %get-tuple-element.45.refs_2_, ...), custom_call_target="tpu_custom_call" | custom-call | flops 1073741824 | bytes 16777216 | tf_op jit(solution)/shard_map/pallas_call | solution.py:257
  143.7 0.0 collective-permute-done.10
  143.8 11.9 %all_to_all.32.arrived = f32[8,32,128]{2,1,0:T(8,128)S(1)} all-to-all(f32[8,32,128]{2,1,0:T(8,128)S(1)} %add.7), channel_id=1, replica_groups=mesh['x'=4,'y'=8,'c'=2,'z'=8] {'z'}, dimensions={0} | all-to-all | bytes 262144 | tf_op jit(solution)/shard_map/all_to_all | solution.py:33
  155.6 0.2 settle.1
  155.9 11.3 %all_to_all.33 = f32[16,1,128]{2,1,0:T(1,128)S(1)} all-to-all(f32[16,1,128]{2,1,0:T(1,128)S(1)} %broadcast_in_dim.19), channel_id=1, replica_groups=mesh['x'=4,'y'=8,'c'=2,'z'=8] {'y','c'}, dimensions={0} | all-to-all | bytes 16384 | tf_op jit(solution)/shard_map/all_to_all | solution.py:33
  167.3 11.6 %all_to_all.34.sums = f32[32,1,128]{2,1,0:T(1,128)S(1)} all-to-all(f32[32,1,128]{2,1,0:T(1,128)S(1)} %broadcast_in_dim.20), channel_id=1, replica_groups=mesh['x'=4,'y'=8,'c'=2,'z'=8] {'x','z'}, dimensions={0} | all-to-all | bytes 32768 | tf_op jit(solution)/shard_map/all_to_all | solution.py:33
  178.9 1.0 finish.1
  (13 shorter events, 0.2 us)
Async XLA Ops:
  3.8 29.9 %collective-permute-start.3 = (f32[128,128]{1,0:T(8,128)S(1)}, f32[128,128]{1,0:T(8,128)S(1)}, u32[]{:S(2)}, u32[]{:S(2)}) collective-permute-start(f32[128,128]{1,0:T(8,128)S(1)} %get-tuple-element.31), channel_id=1, source_target_pairs={{0,4},{1,5},{2,6},{3,7},{4,0},{5,1},{6,2},{7,3},{8,12},{9,13},{10,... | collective-permute-start | bytes 196616 | tf_op jit(solution)/shard_map/ppermute | solution.py:29
  15.2 12.1 %collective-permute-start.2 = (f32[128,128]{1,0:T(8,128)S(1)}, f32[128,128]{1,0:T(8,128)S(1)}, u32[]{:S(2)}, u32[]{:S(2)}) collective-permute-start(f32[128,128]{1,0:T(8,128)S(1)} %get-tuple-element.31), channel_id=1, source_target_pairs={{0,7},{1,0},{2,1},{3,2},{4,3},{5,4},{6,5},{7,6},{8,15},{9,8},{10,9... | collective-permute-start | bytes 196616 | tf_op jit(solution)/shard_map/ppermute | solution.py:29
  17.2 10.2 %collective-permute-start.1 = (f32[128,128]{1,0:T(8,128)S(1)}, f32[128,128]{1,0:T(8,128)S(1)}, u32[]{:S(2)}, u32[]{:S(2)}) collective-permute-start(f32[128,128]{1,0:T(8,128)S(1)} %get-tuple-element.31), channel_id=1, source_target_pairs={{0,1},{1,2},{2,3},{3,4},{4,5},{5,6},{6,7},{7,0},{8,9},{9,10},{10,1... | collective-permute-start | bytes 196616 | tf_op jit(solution)/shard_map/ppermute | solution.py:29
  20.5 26.1 %all-to-all-start = ((f32[8,160,128]{2,1,0:T(8,128)}), f32[8,160,128]{2,1,0:T(8,128)S(1)}, u32[]{:S(2)}, u32[]{:S(2)}) async-start(f32[8,160,128]{2,1,0:T(8,128)} %get-tuple-element.30), calls=%async_computation | async-start | bytes 1310720 | tf_op jit(solution)/shard_map/all_to_all | solution.py:33
  27.4 10.7 %collective-permute-start.5 = (f32[2,128,128]{2,1,0:T(8,128)S(1)}, f32[2,128,128]{2,1,0:T(8,128)S(1)}, u32[]{:S(2)}, u32[]{:S(2)}) collective-permute-start(f32[2,128,128]{2,1,0:T(8,128)S(1)} %get-tuple-element.56), channel_id=1, source_target_pairs={{0,6},{1,7},{2,0},{3,1},{4,2},{5,3},{6,4},{7,5},{8,14},{9,15},{10,... | collective-permute-start | bytes 393224 | tf_op jit(solution)/shard_map/ppermute | solution.py:29
  29.4 8.8 %collective-permute-start.4 = (f32[2,128,128]{2,1,0:T(8,128)S(1)}, f32[2,128,128]{2,1,0:T(8,128)S(1)}, u32[]{:S(2)}, u32[]{:S(2)}) collective-permute-start(f32[2,128,128]{2,1,0:T(8,128)S(1)} %get-tuple-element.57), channel_id=1, source_target_pairs={{0,2},{1,3},{2,4},{3,5},{4,6},{5,7},{6,0},{7,1},{8,10},{9,11},{10,... | collective-permute-start | bytes 393224 | tf_op jit(solution)/shard_map/ppermute | solution.py:29
  38.2 18.8 %collective-permute-start.6 = (f32[8,128,128]{2,1,0:T(8,128)S(1)}, f32[8,128,128]{2,1,0:T(8,128)S(1)}, u32[]{:S(2)}, u32[]{:S(2)}) collective-permute-start(f32[8,128,128]{2,1,0:T(8,128)S(1)} %constant_dynamic-update-slice_fusion.same), channel_id=1, source_target_pairs={{0,8},{8,0},{1,9},{9,1},{2,10},{10,2},{3,11},{11,3},{4,12},{12,4},... | collective-permute-start | bytes 1572872 | tf_op jit(solution)/shard_map/ppermute | solution.py:29
  46.6 17.4 %collective-permute-start.8 = (f32[8,160,128]{2,1,0:T(8,128)S(1)}, f32[8,160,128]{2,1,0:T(8,128)S(1)}, u32[]{:S(2)}, u32[]{:S(2)}) collective-permute-start(f32[8,160,128]{2,1,0:T(8,128)S(1)} %all-to-all-done.cols), channel_id=1, source_target_pairs={{0,128},{128,256},{256,384},{384,0},{1,129},{129,257},{257,385},{3... | collective-permute-start | bytes 1966088 | tf_op jit(solution)/shard_map/ppermute | solution.py:29
  49.7 19.1 %collective-permute-start.7 = (f32[8,160,128]{2,1,0:T(8,128)S(1)}, f32[8,160,128]{2,1,0:T(8,128)S(1)}, u32[]{:S(2)}, u32[]{:S(2)}) collective-permute-start(f32[8,160,128]{2,1,0:T(8,128)S(1)} %all-to-all-done.cols), channel_id=1, source_target_pairs={{0,384},{128,0},{256,128},{384,256},{1,385},{129,1},{257,129},{385... | collective-permute-start | bytes 1966088 | tf_op jit(solution)/shard_map/ppermute | solution.py:29
  53.1 25.9 %collective-permute-start = (f32[8,160,128]{2,1,0:T(8,128)S(1)}, f32[8,160,128]{2,1,0:T(8,128)S(1)}, u32[]{:S(2)}, u32[]{:S(2)}) collective-permute-start(f32[8,160,128]{2,1,0:T(8,128)S(1)} %all-to-all-done.cols), channel_id=1, source_target_pairs={{0,256},{128,384},{256,0},{384,128},{1,257},{129,385},{257,1},{385... | collective-permute-start | bytes 1966088 | tf_op jit(solution)/shard_map/ppermute | solution.py:29
  81.6 26.6 %copy-start = (f32[32,128]{1,0:T(8,128)S(1)}, f32[32,128]{1,0:T(8,128)}, u32[]{:S(2)}) copy-start(f32[32,128]{1,0:T(8,128)} %targets.5) | copy-start | bytes 49156
  81.7 12.6 %collective-permute-start.9 = (f32[8,32,128]{2,1,0:T(8,128)S(1)}, f32[8,32,128]{2,1,0:T(8,128)S(1)}, u32[]{:S(2)}, u32[]{:S(2)}) collective-permute-start(f32[8,32,128]{2,1,0:T(8,128)S(1)} %get-tuple-element.41), channel_id=1, source_target_pairs={{0,8},{8,0},{1,9},{9,1},{2,10},{10,2},{3,11},{11,3},{4,12},{12,4},... | collective-permute-start | bytes 393224 | tf_op jit(solution)/shard_map/ppermute | solution.py:29
  133.5 10.3 %collective-permute-start.10 = (f32[8,32,128]{2,1,0:T(8,128)S(1)}, f32[8,32,128]{2,1,0:T(8,128)S(1)}, u32[]{:S(2)}, u32[]{:S(2)}) collective-permute-start(f32[8,32,128]{2,1,0:T(8,128)S(1)} %shard_map.73), channel_id=1, source_target_pairs={{0,8},{8,0},{1,9},{9,1},{2,10},{10,2},{3,11},{11,3},{4,12},{12,4},... | collective-permute-start | bytes 393224 | tf_op jit(solution)/shard_map/ppermute | solution.py:29
